TPU v7x, 32 devices: a whole 2x2x4 slice. The times are simulated.
32 devices in a mesh: wide: 8 (over z, x), narrow: 4 (over y, core).
Axes of the slice: x: 2, y: 2, z: 4, core: 2. Of those that a mesh axis runs over, the one named last changes fastest.
Arguments:
- layer_input: bfloat16 [8192, 1536], P('wide'), may hold values from -6 to 6
- grad_out: bfloat16 [8192, 1536], P('wide'), may hold values from -6 to 6
- segment_ids: int32 [8192], P('wide'), may hold values from 0 to 8191, as said below
- positions: int32 [8192], P('wide'), may hold values from 0 to 4095, as said below
- norm_gains: float32 [2, 1536], P(None, ('wide', 'narrow')), may hold values from 0.5 to 1.5
- norm_gains_first: float32 [2, 1536], P(None, ('wide', 'narrow')), may hold values from -3 to 3
- norm_gains_second: float32 [2, 1536], P(None, ('wide', 'narrow')), may hold values from 0.1 to 10
- query_weight: float32 [1536, 1536], P('wide', 'narrow'), may hold values from -0.15625 to 0.15625
- query_weight_first: float32 [1536, 1536], P('wide', 'narrow'), may hold values from -3 to 3
- query_weight_second: float32 [1536, 1536], P('wide', 'narrow'), may hold values from 0.1 to 10
- query_bias: float32 [12, 128], P('narrow', 'wide'), may hold values from -3 to 3
- query_bias_first: float32 [12, 128], P('narrow', 'wide'), may hold values from -3 to 3
- query_bias_second: float32 [12, 128], P('narrow', 'wide'), may hold values from 0.1 to 10
- keyvalue_weight: float32 [1536, 512], P(('wide', 'narrow')), may hold values from -0.15625 to 0.15625
- keyvalue_weight_first: float32 [1536, 512], P(('wide', 'narrow')), may hold values from -3 to 3
- keyvalue_weight_second: float32 [1536, 512], P(('wide', 'narrow')), may hold values from 0.1 to 10
- keyvalue_bias: float32 [512], P(('wide', 'narrow')), may hold values from -3 to 3
- keyvalue_bias_first: float32 [512], P(('wide', 'narrow')), may hold values from -3 to 3
- keyvalue_bias_second: float32 [512], P(('wide', 'narrow')), may hold values from 0.1 to 10
- output_weight: float32 [1536, 1536], P('narrow', 'wide'), may hold values from -1.25 to 1.25
- output_weight_first: float32 [1536, 1536], P('narrow', 'wide'), may hold values from -3 to 3
- output_weight_second: float32 [1536, 1536], P('narrow', 'wide'), may hold values from 0.1 to 10
- gateup_weight: float32 [1536, 2, 8960], P('wide', None, 'narrow'), may hold values from -0.15625 to 0.15625
- gateup_weight_first: float32 [1536, 2, 8960], P('wide', None, 'narrow'), may hold values from -3 to 3
- gateup_weight_second: float32 [1536, 2, 8960], P('wide', None, 'narrow'), may hold values from 0.1 to 10
- down_weight: float32 [8960, 1536], P('narrow', 'wide'), may hold values from -0.0625 to 0.0625
- down_weight_first: float32 [8960, 1536], P('narrow', 'wide'), may hold values from -3 to 3
- down_weight_second: float32 [8960, 1536], P('narrow', 'wide'), may hold values from 0.1 to 10
Outputs:
- layer_output: bfloat16 [8192, 1536], P('wide')
- input_grad: bfloat16 [8192, 1536], P('wide')
- grad_norm_gains: float32 [2, 1536], P(None, ('wide', 'narrow'))
- update_norm_gains: float32 [2, 1536], P(None, ('wide', 'narrow'))
- grad_query_weight: float32 [1536, 1536], P('wide', 'narrow')
- update_query_weight: float32 [1536, 1536], P('wide', 'narrow')
- grad_query_bias: float32 [12, 128], P('narrow', 'wide')
- update_query_bias: float32 [12, 128], P('narrow', 'wide')
- grad_keyvalue_weight: float32 [1536, 512], P(('wide', 'narrow'))
- update_keyvalue_weight: float32 [1536, 512], P(('wide', 'narrow'))
- grad_keyvalue_bias: float32 [512], P(('wide', 'narrow'))
- update_keyvalue_bias: float32 [512], P(('wide', 'narrow'))
- grad_output_weight: float32 [1536, 1536], P('narrow', 'wide')
- update_output_weight: float32 [1536, 1536], P('narrow', 'wide')
- grad_gateup_weight: float32 [1536, 2, 8960], P('wide', None, 'narrow')
- update_gateup_weight: float32 [1536, 2, 8960], P('wide', None, 'narrow')
- grad_down_weight: float32 [8960, 1536], P('narrow', 'wide')
- update_down_weight: float32 [8960, 1536], P('narrow', 'wide')
Inputs may be any that keep to these rules, and one draw needn't show every extreme that they name: `segment_ids`: each token's value is the index of the first token of its segment, so it never falls along the tokens; every segment lies inside one aligned row of 4096 tokens; the last token of all is a segment by itself; in every draw at least one row is a single segment. `positions`: each token's value counts the tokens before it in its segment.
All inputs are finite; a program needn't handle non-finite values.
Results may differ from a plain program's by a relative error of at most 0.024.
Values may be sent and summed in bfloat16 or wider, within the bound.
No kernel may reach another device: no remote copies, remote signals or barrier semaphores. Data moves between devices by JAX's collectives and lax.ppermute only.
A program may use at most 320 MiB of HBM per device.

v0:
```python
import jax
import jax.numpy as jnp
from jax import lax
from jax.sharding import PartitionSpec as P

D = 1536
H = 12
KV = 2
HD = 128
LENGTH = 4096


norm_eps = 1e-06
rope_base = 1000000.0
beta_first = 0.9
beta_second = 0.95
adam_eps = 1e-08
decay_rate = 0.1
first_fix = 1.0 - 0.9**10
second_fix = 1.0 - 0.95**10
masked_score = -1e30


def shifted(block, axis, distance):
    devices = range(lax.axis_size(axis))
    route = [(i - distance, i) for i in devices if i - distance in devices]
    return lax.ppermute(block, axis, route)


def rotate(values, positions, sign):
    half = values.shape[-1] // 2
    freqs = rope_base ** (-2.0 * jnp.arange(half, dtype=jnp.float32) / values.shape[-1])
    angles = positions.astype(jnp.float32)[:, None] * freqs[None, :]
    cosine = jnp.cos(angles)[:, None, :]
    sine = sign * jnp.sin(angles)[:, None, :]
    first = values[..., :half]
    second = values[..., half:]
    return jnp.concatenate(
        [first * cosine - second * sine, second * cosine + first * sine], axis=-1
    )


def rms_back(grad_unit, unit, inverse):
    return inverse * (grad_unit - unit * jnp.mean(grad_unit * unit, axis=-1, keepdims=True))


def adam_update(grad, master, first, second, decay, count):
    mean_grad = grad / count
    first_new = beta_first * first + (1.0 - beta_first) * mean_grad
    second_new = beta_second * second + (1.0 - beta_second) * mean_grad * mean_grad
    update = first_new / first_fix / (jnp.sqrt(second_new / second_fix) + adam_eps)
    if decay:
        update = update + decay_rate * master
    return (grad, update)


def fetch_keys(keys, values, segments, distance):
    stacked, remote_segments = shifted((jnp.stack([keys, values]), segments), "wide", distance)
    return (stacked[0], stacked[1], remote_segments)


def return_grads(grad_keys, grad_values, distance):
    stacked = shifted(
        jnp.stack([grad_keys, grad_values]).astype(jnp.bfloat16), "wide", -distance
    ).astype(jnp.float32)
    return (stacked[0], stacked[1])


def visible(query_segments, key_segments, query_index, distance_rows):
    key_index = query_index - distance_rows
    same = query_segments[:, None] == key_segments[None, :]
    causal = key_index[None, :] <= query_index[:, None]
    return same & causal & (key_index[None, :] >= 0)


def masked_scores(queries, keys, allowed):
    scores = jnp.einsum("thd,sd->hts", queries, keys, preferred_element_type=jnp.float32)
    return jnp.where(allowed[None], scores, masked_score)


def local(
    layer_input,
    grad_out,
    segment_ids,
    positions,
    norm_gains,
    norm_gains_first,
    norm_gains_second,
    query_weight,
    query_weight_first,
    query_weight_second,
    query_bias,
    query_bias_first,
    query_bias_second,
    keyvalue_weight,
    keyvalue_weight_first,
    keyvalue_weight_second,
    keyvalue_bias,
    keyvalue_bias_first,
    keyvalue_bias_second,
    output_weight,
    output_weight_first,
    output_weight_second,
    gateup_weight,
    gateup_weight_first,
    gateup_weight_second,
    down_weight,
    down_weight_first,
    down_weight_second,
):
    tokens = layer_input.shape[0]
    local_heads = query_bias.shape[0]
    group = H // KV
    head_scale = HD ** (-0.5)
    key_head = lax.axis_index("narrow") * local_heads // group
    query_index = lax.axis_index("wide") * tokens + jnp.arange(tokens, dtype=jnp.int32)
    shifts = LENGTH // tokens
    token_count = float(tokens * lax.axis_size("wide"))
    w_query, b_query, w_output, w_gateup, w_down = (
        lax.all_gather(query_weight.astype(jnp.bfloat16), "wide", axis=0, tiled=True),
        lax.all_gather(query_bias.astype(jnp.bfloat16), "wide", axis=1, tiled=True),
        lax.all_gather(output_weight.astype(jnp.bfloat16), "wide", axis=1, tiled=True),
        lax.all_gather(gateup_weight.astype(jnp.bfloat16), "wide", axis=0, tiled=True),
        lax.all_gather(down_weight.astype(jnp.bfloat16), "wide", axis=1, tiled=True),
    )
    w_gains, w_keyvalue, b_keyvalue = (
        lax.all_gather(norm_gains.astype(jnp.bfloat16), ("wide", "narrow"), axis=1, tiled=True),
        lax.all_gather(
            keyvalue_weight.astype(jnp.bfloat16), ("wide", "narrow"), axis=0, tiled=True
        ),
        lax.all_gather(keyvalue_bias.astype(jnp.bfloat16), ("wide", "narrow"), axis=0, tiled=True),
    )
    w_pair = lax.dynamic_index_in_dim(
        w_keyvalue.reshape(D, 2, KV, HD), key_head, axis=2, keepdims=False
    ).reshape(D, 2 * HD)
    b_pair = lax.dynamic_index_in_dim(
        b_keyvalue.reshape(2, KV, HD), key_head, axis=1, keepdims=False
    ).reshape(2 * HD)
    gain_one = w_gains[0].astype(jnp.float32)
    gain_two = w_gains[1].astype(jnp.float32)
    input_float = layer_input.astype(jnp.float32)
    inverse_one = lax.rsqrt(jnp.mean(input_float * input_float, axis=-1, keepdims=True) + norm_eps)
    unit_one = input_float * inverse_one
    normed_one = (unit_one * gain_one).astype(jnp.bfloat16)
    query_linear = jnp.dot(
        normed_one, w_query, preferred_element_type=jnp.float32
    ) + b_query.astype(jnp.float32).reshape(-1)
    pair_linear = jnp.dot(normed_one, w_pair, preferred_element_type=jnp.float32) + b_pair.astype(
        jnp.float32
    )
    queries = (
        rotate(query_linear.reshape(tokens, local_heads, HD), positions, 1.0) * head_scale
    ).astype(jnp.bfloat16)
    keys = rotate(pair_linear[:, None, :HD], positions, 1.0)[:, 0].astype(jnp.bfloat16)
    values = pair_linear[:, HD:].astype(jnp.bfloat16)
    pieces = [(keys, values, segment_ids)]
    for distance in range(1, shifts):
        pieces.append(fetch_keys(keys, values, segment_ids, distance))
    masks = [
        visible(segment_ids, piece[2], query_index, distance * tokens)
        for distance, piece in enumerate(pieces)
    ]
    running_top = jnp.full((local_heads, tokens), masked_score, jnp.float32)
    running_total = jnp.zeros((local_heads, tokens), jnp.float32)
    for piece, allowed in zip(pieces, masks):
        scores = masked_scores(queries, piece[0], allowed)
        new_top = jnp.maximum(running_top, jnp.max(scores, axis=-1))
        running_total = running_total * jnp.exp(running_top - new_top) + jnp.sum(
            jnp.exp(scores - new_top[..., None]), axis=-1
        )
        running_top = new_top
    log_total = running_top + jnp.log(running_total)
    attention = jnp.zeros((tokens, local_heads, HD), jnp.float32)
    for piece, allowed in zip(pieces, masks):
        probs = jnp.exp(masked_scores(queries, piece[0], allowed) - log_total[..., None])
        attention = attention + jnp.einsum(
            "hts,sd->thd", probs.astype(jnp.bfloat16), piece[1], preferred_element_type=jnp.float32
        )
    attention_low = attention.astype(jnp.bfloat16).reshape(tokens, local_heads * HD)
    attention_out = lax.psum(
        jnp.dot(attention_low, w_output, preferred_element_type=jnp.float32).astype(jnp.bfloat16),
        "narrow",
    ).astype(jnp.float32)
    residual = input_float + attention_out
    inverse_two = lax.rsqrt(jnp.mean(residual * residual, axis=-1, keepdims=True) + norm_eps)
    unit_two = residual * inverse_two
    normed_two = (unit_two * gain_two).astype(jnp.bfloat16)
    gate_up = jnp.einsum("td,dgf->tgf", normed_two, w_gateup, preferred_element_type=jnp.float32)
    gate = gate_up[:, 0]
    upward = gate_up[:, 1]
    logistic = jax.nn.sigmoid(gate)
    active = gate * logistic
    hidden = (active * upward).astype(jnp.bfloat16)
    mlp_out = lax.psum(
        jnp.dot(hidden, w_down, preferred_element_type=jnp.float32).astype(jnp.bfloat16), "narrow"
    ).astype(jnp.float32)
    layer_output = (residual + mlp_out).astype(jnp.bfloat16)
    grad_float = grad_out.astype(jnp.float32)
    grad_down = jnp.einsum("tf,td->fd", hidden, grad_out, preferred_element_type=jnp.float32)
    grad_hidden = jnp.einsum("td,fd->tf", grad_out, w_down, preferred_element_type=jnp.float32)
    grad_gate = grad_hidden * upward * logistic * (1.0 + gate * (1.0 - logistic))
    grad_upward = grad_hidden * active
    grad_pair = jnp.stack([grad_gate, grad_upward], axis=1).astype(jnp.bfloat16)
    grad_gateup = jnp.einsum(
        "td,tgf->dgf", normed_two, grad_pair, preferred_element_type=jnp.float32
    )
    normed_two_part = jnp.einsum(
        "tgf,dgf->td", grad_pair, w_gateup, preferred_element_type=jnp.float32
    )
    gain_two_part = jnp.sum(normed_two_part * unit_two, axis=0)
    grad_normed_two = lax.psum(normed_two_part.astype(jnp.bfloat16), "narrow").astype(jnp.float32)
    grad_residual = grad_float + rms_back(grad_normed_two * gain_two, unit_two, inverse_two)
    residual_low = grad_residual.astype(jnp.bfloat16)
    grad_output = jnp.einsum(
        "tk,td->kd", attention_low, residual_low, preferred_element_type=jnp.float32
    )
    grad_attention = (
        jnp.einsum("td,kd->tk", residual_low, w_output, preferred_element_type=jnp.float32)
        .astype(jnp.bfloat16)
        .reshape(tokens, local_heads, HD)
    )
    delta = jnp.transpose(jnp.sum(grad_attention.astype(jnp.float32) * attention, axis=-1))
    grad_queries = jnp.zeros((tokens, local_heads, HD), jnp.float32)
    own_keys = jnp.zeros((tokens, HD), jnp.float32)
    own_values = jnp.zeros((tokens, HD), jnp.float32)
    for distance, (piece, allowed) in enumerate(zip(pieces, masks)):
        probs = jnp.exp(masked_scores(queries, piece[0], allowed) - log_total[..., None])
        grad_probs = jnp.einsum(
            "thd,sd->hts", grad_attention, piece[1], preferred_element_type=jnp.float32
        )
        grad_scores = (probs * (grad_probs - delta[..., None])).astype(jnp.bfloat16)
        grad_queries = grad_queries + jnp.einsum(
            "hts,sd->thd", grad_scores, piece[0], preferred_element_type=jnp.float32
        )
        piece_keys = jnp.einsum(
            "hts,thd->sd", grad_scores, queries, preferred_element_type=jnp.float32
        )
        piece_values = jnp.einsum(
            "hts,thd->sd",
            probs.astype(jnp.bfloat16),
            grad_attention,
            preferred_element_type=jnp.float32,
        )
        if distance > 0:
            piece_keys, piece_values = return_grads(piece_keys, piece_values, distance)
        own_keys = own_keys + piece_keys
        own_values = own_values + piece_values
    grad_key_linear = rotate(own_keys[:, None, :], positions, -1.0)[:, 0]
    grad_pair_linear = jnp.concatenate([grad_key_linear, own_values], axis=1).astype(jnp.bfloat16)
    grad_query_linear = (
        rotate(grad_queries * head_scale, positions, -1.0)
        .reshape(tokens, local_heads * HD)
        .astype(jnp.bfloat16)
    )
    grad_query = jnp.einsum(
        "td,tk->dk", normed_one, grad_query_linear, preferred_element_type=jnp.float32
    )
    grad_query_bias = jnp.sum(grad_query_linear.astype(jnp.float32), axis=0).reshape(
        local_heads, HD
    )
    grad_head = jnp.einsum(
        "td,tk->dk", normed_one, grad_pair_linear, preferred_element_type=jnp.float32
    ).reshape(D, 2, 1, HD)
    grad_keyvalue = lax.dynamic_update_slice_in_dim(
        jnp.zeros((D, 2, KV, HD), jnp.float32), grad_head, key_head, axis=2
    ).reshape(D, 2 * KV * HD)
    grad_head_bias = jnp.sum(grad_pair_linear.astype(jnp.float32), axis=0).reshape(2, 1, HD)
    grad_keyvalue_bias = lax.dynamic_update_slice_in_dim(
        jnp.zeros((2, KV, HD), jnp.float32), grad_head_bias, key_head, axis=1
    ).reshape(2 * KV * HD)
    normed_one_part = jnp.einsum(
        "tk,dk->td", grad_query_linear, w_query, preferred_element_type=jnp.float32
    )
    normed_one_part = normed_one_part + jnp.einsum(
        "tk,dk->td", grad_pair_linear, w_pair, preferred_element_type=jnp.float32
    )
    gain_one_part = jnp.sum(normed_one_part * unit_one, axis=0)
    grad_normed_one = lax.psum(normed_one_part.astype(jnp.bfloat16), "narrow").astype(jnp.float32)
    input_grad = (
        grad_residual + rms_back(grad_normed_one * gain_one, unit_one, inverse_one)
    ).astype(jnp.bfloat16)
    summed_query, summed_query_bias, summed_output, summed_gateup, summed_down = (
        lax.psum_scatter(
            grad_query.astype(jnp.bfloat16), "wide", scatter_dimension=0, tiled=True
        ).astype(jnp.float32),
        lax.psum_scatter(
            grad_query_bias.astype(jnp.bfloat16), "wide", scatter_dimension=1, tiled=True
        ).astype(jnp.float32),
        lax.psum_scatter(
            grad_output.astype(jnp.bfloat16), "wide", scatter_dimension=1, tiled=True
        ).astype(jnp.float32),
        lax.psum_scatter(
            grad_gateup.astype(jnp.bfloat16), "wide", scatter_dimension=0, tiled=True
        ).astype(jnp.float32),
        lax.psum_scatter(
            grad_down.astype(jnp.bfloat16), "wide", scatter_dimension=1, tiled=True
        ).astype(jnp.float32),
    )
    summed_gains, summed_keyvalue, summed_keyvalue_bias = (
        lax.psum_scatter(
            jnp.stack([gain_one_part, gain_two_part]),
            ("wide", "narrow"),
            scatter_dimension=1,
            tiled=True,
        ),
        lax.psum_scatter(grad_keyvalue, ("wide", "narrow"), scatter_dimension=0, tiled=True),
        lax.psum_scatter(grad_keyvalue_bias, ("wide", "narrow"), scatter_dimension=0, tiled=True),
    )
    gains_update = adam_update(
        summed_gains, norm_gains, norm_gains_first, norm_gains_second, False, token_count
    )
    query_update = adam_update(
        summed_query, query_weight, query_weight_first, query_weight_second, True, token_count
    )
    qbias_update = adam_update(
        summed_query_bias, query_bias, query_bias_first, query_bias_second, False, token_count
    )
    keyvalue_update = adam_update(
        summed_keyvalue,
        keyvalue_weight,
        keyvalue_weight_first,
        keyvalue_weight_second,
        True,
        token_count,
    )
    kvbias_update = adam_update(
        summed_keyvalue_bias,
        keyvalue_bias,
        keyvalue_bias_first,
        keyvalue_bias_second,
        False,
        token_count,
    )
    output_update = adam_update(
        summed_output, output_weight, output_weight_first, output_weight_second, True, token_count
    )
    gateup_update = adam_update(
        summed_gateup, gateup_weight, gateup_weight_first, gateup_weight_second, True, token_count
    )
    down_update = adam_update(
        summed_down, down_weight, down_weight_first, down_weight_second, True, token_count
    )
    return (
        layer_output,
        input_grad,
        *gains_update,
        *query_update,
        *qbias_update,
        *keyvalue_update,
        *kvbias_update,
        *output_update,
        *gateup_update,
        *down_update,
    )


def solution(mesh):
    in_specs = (
        P("wide", None),
        P("wide", None),
        P("wide"),
        P("wide"),
        P(None, ("wide", "narrow")),
        P(None, ("wide", "narrow")),
        P(None, ("wide", "narrow")),
        P("wide", "narrow"),
        P("wide", "narrow"),
        P("wide", "narrow"),
        P("narrow", "wide"),
        P("narrow", "wide"),
        P("narrow", "wide"),
        P(("wide", "narrow"), None),
        P(("wide", "narrow"), None),
        P(("wide", "narrow"), None),
        P(("wide", "narrow")),
        P(("wide", "narrow")),
        P(("wide", "narrow")),
        P("narrow", "wide"),
        P("narrow", "wide"),
        P("narrow", "wide"),
        P("wide", None, "narrow"),
        P("wide", None, "narrow"),
        P("wide", None, "narrow"),
        P("narrow", "wide"),
        P("narrow", "wide"),
        P("narrow", "wide"),
    )
    out_specs = (
        P("wide", None),
        P("wide", None),
        P(None, ("wide", "narrow")),
        P(None, ("wide", "narrow")),
        P("wide", "narrow"),
        P("wide", "narrow"),
        P("narrow", "wide"),
        P("narrow", "wide"),
        P(("wide", "narrow"), None),
        P(("wide", "narrow"), None),
        P(("wide", "narrow")),
        P(("wide", "narrow")),
        P("narrow", "wide"),
        P("narrow", "wide"),
        P("wide", None, "narrow"),
        P("wide", None, "narrow"),
        P("narrow", "wide"),
        P("narrow", "wide"),
    )
    return jax.shard_map(local, mesh=mesh, in_specs=in_specs, out_specs=out_specs, check_vma=False)
```

profile of v0, /device:TPU:0, one launch (start us, length us, event | category | flops | bytes accessed | tf_op | source)
XLA Modules:
  0.0 1797.7 jit_solution(17370780319943554391)
XLA Ops:
  26.3 38.8 %all-reduce.1 = bf16[2,2,128]{2,1,0:T(2,128)(2,1)S(1)} all-reduce(bf16[2,2,128]{2,1,0:T(2,128)(2,1)S(1)} %bitcast.408), channel_id=1, replica_groups=mesh['wide'=8,'narrow'=4] {'wide','narrow'}, use_global_device_ids=true, to_apply=%add | all-reduce | flops 512 | bytes 2048
  65.7 39.7 %all-gather = bf16[32,48,2]{1,2,0:T(2,128)(2,1)S(1)} all-gather(bf16[1,48,2]{1,2,0:T(2,128)(2,1)S(1)} %convert_bitcast_fusion.1), channel_id=1, replica_groups=mesh['wide'=8,'narrow'=4] {'wide','narrow'}, dimensions={0}, use_global_device_ids=true | all-gather | bytes 6336 | tf_op jit(solution)/shard_map/all_gather | solution.py:127
  109.5 16.3 all-gather.1
  190.0 7.5 exponential_reduce_fusion.3
  197.5 7.3 exponential_reduce_fusion.2
  204.8 6.9 exponential_reduce_fusion.1
  211.8 7.1 exponential_reduce_fusion
  219.0 9.4 fusion.80
  256.8 76.7 %all-reduce.8.cloned.1.call-done = bf16[1024,1536]{1,0:T(8,128)(2,1)} async-done(((bf16[1024,1536]{1,0:T(8,128)(2,1)}), bf16[1024,1536]{1,0:T(8,128)(2,1)}) %all-reduce.8.cloned.1.call-update) | async-done | bytes 3145744 | tf_op jit(solution)/shard_map/psum | solution.py:180
  336.5 195.4 %all-gather.14.cloned.1.call-done = bf16[1536,2,2240]{2,0,1:T(8,128)(2,1)} async-done(((bf16[192,2,2240]{2,0,1:T(8,128)(2,1)}), bf16[1536,2,2240]{2,0,1:T(8,128)(2,1)}) %all-gather.14.cloned.1.call-update) | async-done | bytes 13762576 | tf_op jit(solution)/shard_map/all_gather | solution.py:123
  531.9 21.8 %fusion.137 = f32[1024,2,2240]{0,2,1:T(8,128)} fusion(bf16[1536,2,2240]{2,0,1:T(8,128)(2,1)} %all-gather.14.cloned.1.call-done, bf16[1024,1536]{1,0:T(8,128)(2,1)} %all-reduce.8.cloned.1.call-done, bf16[1024,1536]{1,0:T(8,128)(2,1)S(1)} %copy-done, f32[1536]{0:T(1024)S(1)} %get-tuple-element.112, f32[1024]{0:T(1024)S(1)} %add_rsqrt_fusion), kind=kOutput, calls=%fused_computation.244 | convolution fusion | flops 14102298624 | bytes 38414336 | tf_op jit(solution)/shard_map/td,dgf->tgf/dot_general | solution.py:188
  553.7 87.8 %all-gather.16.cloned.1.call-done = bf16[2240,1536]{0,1:T(8,128)(2,1)} async-done(((bf16[2240,192]{0,1:T(8,128)(2,1)}), bf16[2240,1536]{0,1:T(8,128)(2,1)}) %all-gather.16.cloned.1.call-update) | async-done | bytes 6881296 | tf_op jit(solution)/shard_map/all_gather | solution.py:124
  641.5 20.2 %fusion.33 = (bf16[1024,1,2240]{0,2,1:T(8,128)(2,1)}, bf16[1024,1,2240]{0,2,1:T(8,128)(2,1)}, bf16[1024,2240]{0,1:T(8,128)(2,1)}) fusion(f32[1024,2,2240]{0,2,1:T(8,128)} %fusion.137, bf16[1024,1536]{1,0:T(8,128)(2,1)} %param.29, bf16[2240,1536]{0,1:T(8,128)(2,1)} %all-gather.16.cloned.1.call-done), kind=kOutput, calls=%fused_computation.70 | convolution fusion | flops 7080837120 | bytes 42139648 | tf_op jit(solution)/shard_map/td,fd->tf/dot_general | solution.py:200
  661.7 22.5 %bitcast_convert_fusion = (bf16[1024,1536]{1,0:T(8,128)(2,1)}, f32[1024,1536,1]{1,0,2:T(8,128)}) fusion(bf16[1536,2,2240]{2,0,1:T(8,128)(2,1)} %all-gather.14.cloned.1.call-done, bf16[1024,1,2240]{0,2,1:T(8,128)(2,1)} %get-tuple-element.132, bf16[1024,1,2240]{0,2,1:T(8,128)(2,1)} %get-tuple-element.131), kind=kOutput, calls=%fused_computation.58 | convolution fusion | flops 14099021824 | bytes 32374784 | tf_op jit(solution)/shard_map/tgf,dgf->td/dot_general | solution.py:207
  684.3 12.4 convolution_convert_fusion.2
  696.7 54.4 %all-reduce.10.cloned.1.call-done = bf16[1024,1536]{1,0:T(8,128)(2,1)} async-done(((bf16[1024,1536]{1,0:T(8,128)(2,1)}), bf16[1024,1536]{1,0:T(8,128)(2,1)}) %all-reduce.10.cloned.1.call-update) | async-done | bytes 3145744 | tf_op jit(solution)/shard_map/psum | solution.py:211
  764.2 9.5 fusion.61
  783.8 8.7 fusion.7
  792.5 11.7 fusion.5
  811.6 11.5 fusion.3
  830.3 7.9 fusion.1
  901.7 114.0 %all-reduce.12.cloned.1.call-done = (bf16[1024,1536]{1,0:T(8,128)(2,1)}, bf16[1024,1536]{1,0:T(8,128)(2,1)}) async-done(((bf16[1024,1536]{1,0:T(8,128)(2,1)}, bf16[1024,1536]{1,0:T(8,128)(2,1)}), (bf16[1024,1536]{1,0:T(8,128)(2,1)}, bf16[1024,1536]{1,0:T(8,128)(2,1)})) %all-reduce.12.cloned.1.call-update) | async-done | bytes 6291472 | tf_op jit(solution)/shard_map/psum | solution.py:194
  1032.6 37.6 %dynamic_update_slice.6 = f32[1536,2,2,128]{3,2,1,0:T(2,128)} dynamic-update-slice(f32[1536,2,2,128]{3,2,1,0:T(2,128)} %broadcast_in_dim.83, f32[1536,2,1,128]{3,2,1,0:T(1,128)} %copy.284, s32[]{:T(128)} %constant.64.clone.1, s32[]{:T(128)} %constant.64.clone.1, s32[]{:T(128)S(6)} %select_n.35, s32[]{:T(128)} %constant.64.clone.1) | dynamic-update-slice | bytes 3145732 | tf_op jit(solution)/shard_map/dynamic_update_slice | solution.py:264
  1075.7 12.4 convolution_convert_fusion.1
  1088.2 21.5 %convolution_convert_fusion = bf16[1536,2,2240]{2,0,1:T(8,128)(2,1)} fusion(bf16[1024,1,2240]{0,2,1:T(8,128)(2,1)} %get-tuple-element.132, bf16[1024,1,2240]{0,2,1:T(8,128)(2,1)} %get-tuple-element.131, bf16[1024,1536]{1,0:T(8,128)(2,1)} %all-reduce.8.cloned.1.call-done, bf16[1024,1536]{1,0:T(8,128)(2,1)S(1)} %copy-done, f32[1536]{0:T(1024)S(1)} %get-tuple-element.112, ...), kind=kOutput, calls=%fused_computation | convolution fusion | flops 14127529984 | bytes 29239296 | tf_op jit(solution)/shard_map/td,tgf->dgf/dot_general | solution.py:204
  1112.3 40.0 %all-reduce.2 = f32[512]{0:T(512)S(1)} all-reduce(f32[512]{0:T(512)S(1)} %bitcast.403), channel_id=6, replica_groups=mesh['wide'=8,'narrow'=4] {'wide','narrow'}, use_global_device_ids=true, to_apply=%region_25.26.clone | all-reduce | flops 512 | bytes 4096
  1155.1 51.6 %reduce-scatter.12.cloned.1.call-done = bf16[192,384]{1,0:T(8,128)(2,1)} async-done(((bf16[1536,384]{1,0:T(8,128)(2,1)}), bf16[192,384]{1,0:T(8,128)(2,1)}) %reduce-scatter.12.cloned.1.call-update) | async-done | bytes 147472 | tf_op jit(solution)/shard_map/reduce_scatter | solution.py:283
  1208.9 8.7 fusion.26
  1217.6 88.5 %reduce-scatter.22.cloned.1.call-done = f32[48,2]{1,0:T(8,128)} async-done(((f32[1536,2]{1,0:T(8,128)}), f32[48,2]{1,0:T(8,128)}) %reduce-scatter.22.cloned.1.call-update) | async-done | bytes 400
  1307.5 105.2 %reduce-scatter.14.cloned.1.call-done = f32[48,512]{1,0:T(8,128)} async-done(((f32[1536,512]{1,0:T(8,128)}), f32[48,512]{1,0:T(8,128)}) %reduce-scatter.14.cloned.1.call-update) | async-done | bytes 98320 | tf_op jit(solution)/shard_map/reduce_scatter | solution.py:306
  1414.3 130.0 %reduce-scatter.20.cloned.1.call-done = bf16[2240,192]{0,1:T(8,128)(2,1)} async-done(((bf16[2240,1536]{0,1:T(8,128)(2,1)}), bf16[2240,192]{0,1:T(8,128)(2,1)}) %reduce-scatter.20.cloned.1.call-update) | async-done | bytes 860176 | tf_op jit(solution)/shard_map/reduce_scatter | solution.py:295
  1550.1 226.4 %reduce-scatter.18.cloned.1.call-done = bf16[192,2,2240]{2,0,1:T(8,128)(2,1)} async-done(((bf16[1536,2,2240]{2,0,1:T(8,128)(2,1)}), bf16[192,2,2240]{2,0,1:T(8,128)(2,1)}) %reduce-scatter.18.cloned.1.call-update) | async-done | bytes 1720336 | tf_op jit(solution)/shard_map/reduce_scatter | solution.py:292
  (347 shorter events, 272.6 us)
Async XLA Ops:
  7.2 121.8 %copy-start.60 = (s32[1024]{0:T(1024)S(1)}, s32[1024]{0:T(1024)}, u32[]{:S(2)}) copy-start(s32[1024]{0:T(1024)} %param.30) | copy-start | bytes 12292
  7.2 127.7 %copy-start = (bf16[1024,1536]{1,0:T(8,128)(2,1)S(1)}, bf16[1024,1536]{1,0:T(8,128)(2,1)}, u32[]{:S(2)}) copy-start(bf16[1024,1536]{1,0:T(8,128)(2,1)} %param.28) | copy-start | bytes 9437188
  7.2 127.7 %all-gather.10.cloned.1.call-start = ((), (), s32[]{:S(2)}) async-start(), calls=%async_computation.8 | async-start | bytes 1327104 | tf_op jit(solution)/shard_map/all_gather | solution.py:120
  9.1 139.4 %all-gather.8.cloned.1.call-start = ((), (), s32[]{:S(2)}) async-start(), calls=%async_computation.7 | async-start | bytes 1622016 | tf_op jit(solution)/shard_map/all_gather | solution.py:128
  10.7 235.0 %all-gather.12.cloned.1.call-start = ((), (), s32[]{:S(2)}) async-start(), calls=%async_computation.9 | async-start | bytes 1327104 | tf_op jit(solution)/shard_map/all_gather | solution.py:122
  10.7 118.3 %collective-permute-start = (s32[1024]{0:T(1024)}, s32[1024]{0:T(1024)S(1)}, u32[]{:S(2)}, u32[]{:S(2)}) collective-permute-start(s32[1024]{0:T(1024)} %param.30), channel_id=1, source_target_pairs={{0,4},{4,8},{8,12},{12,16},{16,20},{20,24},{24,28},{1,5},{5,9},{9,... | collective-permute-start | bytes 12296 | tf_op jit(solution)/shard_map/ppermute | solution.py:27
  15.6 113.4 %collective-permute-start.2 = (s32[1024]{0:T(1024)}, s32[1024]{0:T(1024)S(1)}, u32[]{:S(2)}, u32[]{:S(2)}) collective-permute-start(s32[1024]{0:T(1024)} %param.30), channel_id=1, source_target_pairs={{0,8},{4,12},{8,16},{12,20},{16,24},{20,28},{1,9},{5,13},{9,17},{1... | collective-permute-start | bytes 12296 | tf_op jit(solution)/shard_map/ppermute | solution.py:27
  19.1 109.9 %collective-permute-start.4 = (s32[1024]{0:T(1024)}, s32[1024]{0:T(1024)S(1)}, u32[]{:S(2)}, u32[]{:S(2)}) collective-permute-start(s32[1024]{0:T(1024)} %param.30), channel_id=1, source_target_pairs={{0,12},{4,16},{8,20},{12,24},{16,28},{1,13},{5,17},{9,21},{13,25},... | collective-permute-start | bytes 12296 | tf_op jit(solution)/shard_map/ppermute | solution.py:27
  25.2 308.3 %all-reduce.8.cloned.1.call-start = ((), (), s32[]{:S(2)}) async-start(), calls=%async_computation.10 | async-start | bytes 6291456 | tf_op jit(solution)/shard_map/psum | solution.py:180
  25.3 128.3 %copy-start.61 = (f32[64]{0:T(128)}, f32[64]{0:T(128)S(1)}, u32[]{:S(2)}) copy-start(f32[64]{0:T(128)S(1)} %multiply_power_fusion) | copy-start | bytes 772
  154.8 15.0 collective-permute-start.3
  156.2 20.4 %collective-permute-start.1 = (bf16[2,1024,128]{1,2,0:T(8,128)(2,1)S(1)}, bf16[2,1024,128]{1,2,0:T(8,128)(2,1)S(1)}, u32[]{:S(2)}, u32[]{:S(2)}) collective-permute-start(bf16[2,1024,128]{1,2,0:T(8,128)(2,1)S(1)} %pad_maximum_fusion.3), channel_id=1, source_target_pairs={{0,4},{4,8},{8,12},{12,16},{16,20},{20,24},{24,28},{1,5},{5,9},{9,... | collective-permute-start | bytes 1572872 | tf_op jit(solution)/shard_map/ppermute | solution.py:27
  160.1 23.1 %collective-permute-start.5 = (bf16[2,1024,128]{1,2,0:T(8,128)(2,1)S(1)}, bf16[2,1024,128]{1,2,0:T(8,128)(2,1)S(1)}, u32[]{:S(2)}, u32[]{:S(2)}) collective-permute-start(bf16[2,1024,128]{1,2,0:T(8,128)(2,1)S(1)} %pad_maximum_fusion.3), channel_id=1, source_target_pairs={{0,12},{4,16},{8,20},{12,24},{16,28},{1,13},{5,17},{9,21},{13,25},... | collective-permute-start | bytes 1572872 | tf_op jit(solution)/shard_map/ppermute | solution.py:27
  250.7 281.2 %all-gather.14.cloned.1.call-start = ((), (), s32[]{:S(2)}) async-start(), calls=%async_computation.11 | async-start | bytes 15925248 | tf_op jit(solution)/shard_map/all_gather | solution.py:123
  254.1 387.3 %all-gather.16.cloned.1.call-start = ((), (), s32[]{:S(2)}) async-start(), calls=%async_computation.12 | async-start | bytes 7962624 | tf_op jit(solution)/shard_map/all_gather | solution.py:124
  256.7 494.3 %all-reduce.10.cloned.1.call-start = ((), (), s32[]{:S(2)}) async-start(), calls=%async_computation.13 | async-start | bytes 6291456 | tf_op jit(solution)/shard_map/psum | solution.py:211
  684.2 331.5 %all-reduce.12.cloned.1.call-start = ((), (), s32[]{:S(2)}) async-start(), calls=%async_computation.21 | async-start | bytes 12582912 | tf_op jit(solution)/shard_map/psum | solution.py:194
  810.1 60.5 %collective-permute-start.6 = (bf16[2,1024,128]{1,2,0:T(8,128)(2,1)}, bf16[2,1024,128]{1,2,0:T(8,128)(2,1)}, u32[]{:S(2)}, u32[]{:S(2)}) collective-permute-start(bf16[2,1024,128]{1,2,0:T(8,128)(2,1)} %pad_maximum_fusion.4), channel_id=1, source_target_pairs={{4,0},{8,4},{12,8},{16,12},{20,16},{24,20},{28,24},{5,1},{9,5},{13... | collective-permute-start | bytes 1572872 | tf_op jit(solution)/shard_map/ppermute | solution.py:27
  829.0 42.7 %collective-permute-start.7 = (bf16[2,1024,128]{1,2,0:T(8,128)(2,1)}, bf16[2,1024,128]{1,2,0:T(8,128)(2,1)}, u32[]{:S(2)}, u32[]{:S(2)}) collective-permute-start(bf16[2,1024,128]{1,2,0:T(8,128)(2,1)} %pad_maximum_fusion.5), channel_id=1, source_target_pairs={{8,0},{12,4},{16,8},{20,12},{24,16},{28,20},{9,1},{13,5},{17,9},{2... | collective-permute-start | bytes 1572872 | tf_op jit(solution)/shard_map/ppermute | solution.py:27
  844.1 28.8 %collective-permute-start.8 = (bf16[2,1024,128]{1,2,0:T(8,128)(2,1)}, bf16[2,1024,128]{1,2,0:T(8,128)(2,1)}, u32[]{:S(2)}, u32[]{:S(2)}) collective-permute-start(bf16[2,1024,128]{1,2,0:T(8,128)(2,1)} %pad_maximum_fusion.6), channel_id=1, source_target_pairs={{12,0},{16,4},{20,8},{24,12},{28,16},{13,1},{17,5},{21,9},{25,13},... | collective-permute-start | bytes 1572872 | tf_op jit(solution)/shard_map/ppermute | solution.py:27
  890.5 219.3 %reduce-scatter.24.cloned.1.call-start = ((), (), s32[]{:S(2)}) async-start(), calls=%async_computation.20 | async-start | bytes 36864
  891.3 261.6 %reduce-scatter.16.cloned.1.call-start = ((), (), s32[]{:S(2)}) async-start(), calls=%async_computation.16 | async-start | bytes 1327104 | tf_op jit(solution)/shard_map/reduce_scatter | solution.py:289
  897.3 309.3 %reduce-scatter.12.cloned.1.call-start = ((), (), s32[]{:S(2)}) async-start(), calls=%async_computation.14 | async-start | bytes 1327104 | tf_op jit(solution)/shard_map/reduce_scatter | solution.py:283
  901.7 404.4 %reduce-scatter.22.cloned.1.call-start = ((), (), s32[]{:S(2)}) async-start(), calls=%async_computation.19 | async-start | bytes 811008
  1021.8 390.9 %reduce-scatter.14.cloned.1.call-start = ((), (), s32[]{:S(2)}) async-start(), calls=%async_computation.15 | async-start | bytes 3244032 | tf_op jit(solution)/shard_map/reduce_scatter | solution.py:306
  1075.7 468.6 %reduce-scatter.20.cloned.1.call-start = ((), (), s32[]{:S(2)}) async-start(), calls=%async_computation.18 | async-start | bytes 7962624 | tf_op jit(solution)/shard_map/reduce_scatter | solution.py:295
  1088.2 688.4 %reduce-scatter.18.cloned.1.call-start = ((), (), s32[]{:S(2)}) async-start(), calls=%async_computation.17 | async-start | bytes 15925248 | tf_op jit(solution)/shard_map/reduce_scatter | solution.py:292
  1208.9 98.1 %copy-start.67 = (f32[2,48]{1,0:T(2,128)S(1)}, f32[2,48]{1,0:T(2,128)}, u32[]{:S(2)}) copy-start(f32[2,48]{1,0:T(2,128)} %param.33) | copy-start | bytes 1156
  1208.9 203.9 %copy-start.43 = (f32[48,512]{1,0:T(8,128)S(1)}, f32[48,512]{1,0:T(8,128)}, u32[]{:S(2)}) copy-start(f32[48,512]{1,0:T(8,128)} %param.41) | copy-start | bytes 294916
  1208.9 203.8 %copy-start.49 = (f32[48,512]{1,0:T(8,128)S(1)}, f32[48,512]{1,0:T(8,128)}, u32[]{:S(2)}) copy-start(f32[48,512]{1,0:T(8,128)} %param.43) | copy-start | bytes 294916
  1208.9 203.8 %copy-start.50 = (f32[48,512]{1,0:T(8,128)S(1)}, f32[48,512]{1,0:T(8,128)}, u32[]{:S(2)}) copy-start(f32[48,512]{1,0:T(8,128)} %param.42) | copy-start | bytes 294916
  1306.9 475.6 %copy-start.63 = (f32[2,48]{1,0:T(2,128)}, f32[2,48]{1,0:T(2,128)S(1)}, u32[]{:S(2)}) copy-start(f32[2,48]{1,0:T(2,128)S(1)} %copy.344) | copy-start | bytes 1156
  (81 other events, 923.1 us)
Sparse Core Ops, SparseCore 0:
  10.8 43.9 all-gather.9
  58.2 53.5 all-gather.7
  114.6 39.9 all-gather.11
  250.8 82.6 all-reduce.7
  336.1 195.7 all-gather.13
  534.5 106.9 all-gather.15
  684.4 66.6 all-reduce.9
  890.6 125.0 all-reduce.11
  1019.4 53.6 reduce-scatter.23
  1076.3 63.2 reduce-scatter.15
  1143.5 63.0 reduce-scatter.11
  1211.6 94.4 reduce-scatter.21
  1312.1 100.5 reduce-scatter.13
  1416.2 128.0 reduce-scatter.19
  1548.2 228.2 reduce-scatter.17
where the time goes:
time: 1810 us; the launch traced here: 1800 us
  waiting for transfers between devices  1130 us (62%)
  matrix products  296 us (16%)
  blocking collectives  135 us (7%)
  other arithmetic  111 us (6%)
  local copies, waits for them, and re-layouts  82.8 us (5%)
  starting transfers between devices  26.6 us (1%)
    reduce_scatter x1, waiting for transfers between devices, local(): lax.psum_scatter(grad_gateup.astype(jnp.bfloat16), 'wide', scatter_dimens...  226 us
    all_gather x1, waiting for transfers between devices, local(): lax.all_gather(gateup_weight.astype(jnp.bfloat16), 'wide', axis=0, tiled=...  195 us
    reduce_scatter x1, waiting for transfers between devices, local(): lax.psum_scatter(grad_down.astype(jnp.bfloat16), 'wide', scatter_dimensio...  130 us
    psum x1, waiting for transfers between devices, local(): lax.psum(jnp.dot(hidden, w_down, preferred_element_type=jnp.float32).asty...  114 us
    reduce_scatter x1, waiting for transfers between devices, local(): lax.psum_scatter(grad_keyvalue, ('wide', 'narrow'), scatter_dimension=0,...  105 us
    unnamed x17, waiting for transfers between devices  88.8 us
    all_gather x1, waiting for transfers between devices, local(): lax.all_gather(down_weight.astype(jnp.bfloat16), 'wide', axis=1, tiled=True)  87.8 us
    unnamed x2, blocking collectives  78.7 us
  transfers between devices with their start and end apart: 24, of which 10 were waited for; matrix products, arithmetic and copies ran while one was open for 19% of the time, Pallas kernels for 0%

commit v1 on v0

v1 whole, which is shorter than its diff:
```python
import jax
import jax.numpy as jnp
from jax import lax
from jax.experimental import pallas as pl
from jax.experimental.pallas import tpu as pltpu
from jax.sharding import Mesh
from jax.sharding import PartitionSpec as P

D = 1536
H = 12
KV = 2
HD = 128
LENGTH = 4096
LANES = 128

norm_eps = 1e-06
rope_base = 1000000.0
beta_first = 0.9
beta_second = 0.95
adam_eps = 1e-08
decay_rate = 0.1
first_fix = 1.0 - 0.9**10
second_fix = 1.0 - 0.95**10
masked_score = -1e30

WIDE = ("hi", "lo", "x")
NARROW = ("y", "c")
BLOCK_Q = 256
BLOCK_K = 512


def low(a):
    return a.astype(jnp.bfloat16)


def wide_float(a):
    return a.astype(jnp.float32)


def matmul(left, right):
    return jnp.dot(left, right, preferred_element_type=jnp.float32)


def matmul_nt(left, right):
    return lax.dot_general(left, right, (((1,), (1,)), ((), ())), preferred_element_type=jnp.float32)


def matmul_tn(left, right):
    return lax.dot_general(left, right, (((0,), (0,)), ((), ())), preferred_element_type=jnp.float32)


def swap(block, axis, distance=1):
    size = 1
    for name in axis if isinstance(axis, tuple) else (axis,):
        size *= lax.axis_size(name)
    return lax.ppermute(block, axis, [(i, i ^ distance) for i in range(size)])


def pick(stacked, index):
    return lax.dynamic_index_in_dim(stacked, index, axis=0, keepdims=False)


def pair(mine, other, index):
    return jnp.where(index == 0, jnp.stack([mine, other]), jnp.stack([other, mine]))


def place_blocks(blocks):
    lead = tuple(blocks[0][2])
    tail = blocks[0][0].shape
    full = jnp.zeros(lead + tail, blocks[0][0].dtype)
    for block, index, _ in blocks:
        start = tuple(index) + (0,) * len(tail)
        full = lax.dynamic_update_slice(full, block.reshape((1,) * len(lead) + tail), start)
    return full


def gather_wide(block):
    hi, lo, x = (lax.axis_index(name) for name in WIDE)
    count = lax.axis_size("hi")
    both = pair(block, swap(block, "lo"), lo)
    lead = (count, 2)
    columns = [both] + [swap(both, "hi", d) for d in range(1, count)]
    placed = []
    for d, column in enumerate(columns):
        other = swap(column, "x")
        for at, part in ((x, column), (1 - x, other)):
            placed.append((part, hi ^ d, at))
    full = jnp.zeros((count, 2, 2) + block.shape, block.dtype)
    for part, at_hi, at_x in placed:
        full = lax.dynamic_update_slice(
            full, part[None, :, None], (at_hi, 0, at_x) + (0,) * block.ndim
        )
    return full.reshape((count * 4,) + block.shape)


def scatter_wide(parts):
    hi, lo, x = (lax.axis_index(name) for name in WIDE)
    count = lax.axis_size("hi")
    shape = parts.shape[1:]
    parts = parts.reshape((count, 2, 2) + shape)
    kept = lax.dynamic_index_in_dim(parts, x, axis=2, keepdims=False)
    sent = lax.dynamic_index_in_dim(parts, 1 - x, axis=2, keepdims=False)
    parts = low(wide_float(kept) + wide_float(swap(sent, "x")))
    total = wide_float(pick(parts, hi))
    for d in range(1, count):
        total = total + wide_float(swap(pick(parts, hi ^ d), "hi", d))
    kept, sent = pick(total, lo), low(pick(total, 1 - lo))
    return kept + wide_float(swap(sent, "lo"))


def gather_hidden(shard):
    hi, lo, x = (lax.axis_index(name) for name in WIDE)
    count = lax.axis_size("hi")
    rows, half = shard.shape[0], shard.shape[1] // 2
    mine = lax.dynamic_slice_in_dim(shard, lo * half, half, axis=1)
    sent = lax.dynamic_slice_in_dim(shard, (1 - lo) * half, half, axis=1)
    both = pair(mine, swap(sent, "lo"), lo)
    columns = [both] + [swap(both, "hi", d) for d in range(1, count)]
    full = jnp.zeros((count, 2, 2, rows, half), shard.dtype)
    for d, column in enumerate(columns):
        for at_x, part in ((x, column), (1 - x, swap(column, "x"))):
            full = lax.dynamic_update_slice(full, part[None, :, None], (hi ^ d, 0, at_x, 0, 0))
    return full.reshape(count * 4 * rows, half)


def scatter_hidden(grad):
    hi, lo, x = (lax.axis_index(name) for name in WIDE)
    count = lax.axis_size("hi")
    rows, half = grad.shape[0] // (count * 4), grad.shape[1]
    parts = grad.reshape(count, 2, 2, rows, half)
    kept = lax.dynamic_index_in_dim(parts, x, axis=2, keepdims=False)
    sent = lax.dynamic_index_in_dim(parts, 1 - x, axis=2, keepdims=False)
    parts = low(wide_float(kept) + wide_float(swap(sent, "x")))
    total = wide_float(pick(parts, hi))
    for d in range(1, count):
        total = total + wide_float(swap(pick(parts, hi ^ d), "hi", d))
    total = low(total)
    mine, other = pick(total, lo), swap(pick(total, 1 - lo), "lo")
    first = jnp.where(lo == 0, mine, other)
    second = jnp.where(lo == 0, other, mine)
    return wide_float(jnp.concatenate([first, second], axis=1))


def exchange_narrow(blocks):
    y, c = (lax.axis_index(name) for name in NARROW)
    shape = blocks.shape[2:]
    flat = blocks.reshape((4,) + shape)
    me = y * 2 + c
    got = [pick(flat, me)] + [swap(pick(flat, me ^ d), NARROW, d) for d in range(1, 4)]
    near, far = pair(got[0], got[1], c), pair(got[2], got[3], c)
    return pair(near, far, y)


def gather_tokens(block):
    y, c = (lax.axis_index(name) for name in NARROW)
    both = pair(block, swap(block, "y"), y)
    both = both.reshape((-1,) + block.shape[1:])
    every = pair(both, swap(both, "c"), c)
    return every.reshape((-1,) + block.shape[1:])


def rotation(positions):
    half = HD // 2
    freqs = rope_base ** (-2.0 * jnp.arange(half, dtype=jnp.float32) / HD)
    angles = positions.astype(jnp.float32)[:, None] * freqs[None, :]
    return jnp.cos(angles)[:, None, :], jnp.sin(angles)[:, None, :]


def rotate(values, cosine, sine):
    half = values.shape[-1] // 2
    first = values[..., :half]
    second = values[..., half:]
    return jnp.concatenate(
        [first * cosine - second * sine, second * cosine + first * sine], axis=-1
    )


def rms_back(grad_unit, unit, inverse):
    return inverse * (grad_unit - unit * jnp.mean(grad_unit * unit, axis=-1, keepdims=True))


def adam_update(grad, master, first, second, decay, count):
    mean_grad = grad / count
    first_new = beta_first * first + (1.0 - beta_first) * mean_grad
    second_new = beta_second * second + (1.0 - beta_second) * mean_grad * mean_grad
    update = first_new / first_fix / (jnp.sqrt(second_new / second_fix) + adam_eps)
    if decay:
        update = update + decay_rate * master
    return (grad, update)


def stacked_heads(ref, heads):
    return jnp.concatenate([ref[:, h * HD : (h + 1) * HD] for h in range(heads)], axis=0)


def attention_forward(queries, keys, values, begins, starts, place):
    tokens, columns = queries.shape
    heads = columns // HD
    length = keys.shape[0]
    rows = heads * BLOCK_Q

    def kernel(starts_ref, place_ref, q_ref, k_ref, v_ref, begin_ref, o_ref, lse_ref):
        step = pl.program_id(0)
        base = place_ref[0] * tokens + step * BLOCK_Q
        q = stacked_heads(q_ref, heads)
        row = base + lax.broadcasted_iota(jnp.int32, (BLOCK_Q, 1), 0)
        row = jnp.concatenate([row] * heads, axis=0)
        begin = jnp.concatenate([begin_ref[...]] * heads, axis=0)

        def body(j, carry):
            top, total, acc = carry
            at = pl.multiple_of(j * BLOCK_K, BLOCK_K)
            k = k_ref[pl.ds(at, BLOCK_K), :]
            v = v_ref[pl.ds(at, BLOCK_K), :]
            s = matmul_nt(q, k)
            col = at + lax.broadcasted_iota(jnp.int32, (1, BLOCK_K), 1)
            s = jnp.where((col <= row) & (col >= begin), s, masked_score)
            new_top = jnp.maximum(top, jnp.max(s, axis=1, keepdims=True))
            p = jnp.exp(s - new_top)
            scale = jnp.exp(top - new_top)
            total = scale * total + jnp.sum(p, axis=1, keepdims=True)
            acc = scale * acc + matmul(low(p), v)
            return new_top, total, acc

        first = starts_ref[step] // BLOCK_K
        last = (base + BLOCK_Q - 1) // BLOCK_K
        top, total, acc = lax.fori_loop(
            first,
            last + 1,
            body,
            (
                jnp.full((rows, 1), masked_score, jnp.float32),
                jnp.zeros((rows, 1), jnp.float32),
                jnp.zeros((rows, HD), jnp.float32),
            ),
        )
        out = acc / total
        for h in range(heads):
            o_ref[:, h * HD : (h + 1) * HD] = out[h * BLOCK_Q : (h + 1) * BLOCK_Q]
        lse_ref[...] = (top + jnp.log(total)).reshape(heads, BLOCK_Q, 1)

    block = pl.BlockSpec((BLOCK_Q, columns), lambda i, *_: (i, 0))
    whole = pl.BlockSpec((length, HD), lambda i, *_: (0, 0))
    return pl.pallas_call(
        kernel,
        grid_spec=pltpu.PrefetchScalarGridSpec(
            num_scalar_prefetch=2,
            grid=(tokens // BLOCK_Q,),
            in_specs=[block, whole, whole, pl.BlockSpec((BLOCK_Q, 1), lambda i, *_: (i, 0))],
            out_specs=[block, pl.BlockSpec((heads, BLOCK_Q, 1), lambda i, *_: (0, i, 0))],
        ),
        out_shape=[
            jax.ShapeDtypeStruct((tokens, columns), jnp.float32),
            jax.ShapeDtypeStruct((heads, tokens, 1), jnp.float32),
        ],
        compiler_params=pltpu.CompilerParams(dimension_semantics=("arbitrary",)),
        name="attention_forward",
    )(starts, place, queries, keys, values, begins)


def attention_backward(queries, keys, values, begins, starts, place, grads, lse, outputs):
    tokens, columns = queries.shape
    heads = columns // HD
    length = keys.shape[0]
    rows = heads * BLOCK_Q

    def kernel(
        starts_ref, place_ref, q_ref, k_ref, v_ref, begin_ref, g_ref, lse_ref, o_ref,
        dq_ref, dk_ref, dv_ref,
    ):
        step = pl.program_id(0)

        @pl.when(step == 0)
        def _():
            dk_ref[...] = jnp.zeros_like(dk_ref)
            dv_ref[...] = jnp.zeros_like(dv_ref)

        base = place_ref[0] * tokens + step * BLOCK_Q
        q = stacked_heads(q_ref, heads)
        g = stacked_heads(g_ref, heads)
        delta = jnp.sum(wide_float(g) * stacked_heads(o_ref, heads), axis=1, keepdims=True)
        lse = lse_ref[...].reshape(rows, 1)
        row = base + lax.broadcasted_iota(jnp.int32, (BLOCK_Q, 1), 0)
        row = jnp.concatenate([row] * heads, axis=0)
        begin = jnp.concatenate([begin_ref[...]] * heads, axis=0)

        def body(j, dq):
            at = pl.multiple_of(j * BLOCK_K, BLOCK_K)
            k = k_ref[pl.ds(at, BLOCK_K), :]
            v = v_ref[pl.ds(at, BLOCK_K), :]
            col = at + lax.broadcasted_iota(jnp.int32, (1, BLOCK_K), 1)
            s = jnp.where((col <= row) & (col >= begin), matmul_nt(q, k), masked_score)
            p = jnp.exp(s - lse)
            dp = matmul_nt(g, v)
            ds = low(p * (dp - delta))
            dk_ref[pl.ds(at, BLOCK_K), :] += matmul_tn(ds, q)
            dv_ref[pl.ds(at, BLOCK_K), :] += matmul_tn(low(p), g)
            return dq + matmul(ds, k)

        first = starts_ref[step] // BLOCK_K
        last = (base + BLOCK_Q - 1) // BLOCK_K
        dq = lax.fori_loop(first, last + 1, body, jnp.zeros((rows, HD), jnp.float32))
        for h in range(heads):
            dq_ref[:, h * HD : (h + 1) * HD] = dq[h * BLOCK_Q : (h + 1) * BLOCK_Q]

    block = pl.BlockSpec((BLOCK_Q, columns), lambda i, *_: (i, 0))
    whole = pl.BlockSpec((length, HD), lambda i, *_: (0, 0))
    return pl.pallas_call(
        kernel,
        grid_spec=pltpu.PrefetchScalarGridSpec(
            num_scalar_prefetch=2,
            grid=(tokens // BLOCK_Q,),
            in_specs=[
                block,
                whole,
                whole,
                pl.BlockSpec((BLOCK_Q, 1), lambda i, *_: (i, 0)),
                block,
                pl.BlockSpec((heads, BLOCK_Q, 1), lambda i, *_: (0, i, 0)),
                block,
            ],
            out_specs=[block, whole, whole],
        ),
        out_shape=[
            jax.ShapeDtypeStruct((tokens, columns), jnp.float32),
            jax.ShapeDtypeStruct((length, HD), jnp.float32),
            jax.ShapeDtypeStruct((length, HD), jnp.float32),
        ],
        compiler_params=pltpu.CompilerParams(dimension_semantics=("arbitrary",)),
        name="attention_backward",
    )(starts, place, queries, keys, values, begins, grads, lse, outputs)


def local(
    layer_input,
    grad_out,
    segment_ids,
    positions,
    norm_gains,
    norm_gains_first,
    norm_gains_second,
    query_weight,
    query_weight_first,
    query_weight_second,
    query_bias,
    query_bias_first,
    query_bias_second,
    keyvalue_weight,
    keyvalue_weight_first,
    keyvalue_weight_second,
    keyvalue_bias,
    keyvalue_bias_first,
    keyvalue_bias_second,
    output_weight,
    output_weight_first,
    output_weight_second,
    gateup_weight,
    gateup_weight_first,
    gateup_weight_second,
    down_weight,
    down_weight_first,
    down_weight_second,
):
    hi, lo, x, y, c = (lax.axis_index(name) for name in WIDE + NARROW)
    wide = lax.axis_size("hi") * 4
    tokens = layer_input.shape[0]
    quarter = tokens // 4
    heads = query_bias.shape[0]
    head_scale = HD ** (-0.5)
    token_count = float(tokens * wide)
    rows = D // wide
    narrow_rows = rows // 4
    bias_part = query_bias.shape[1]
    kv_part = keyvalue_bias.shape[0]
    column_block = c * KV + y
    hidden = gateup_weight.shape[2]
    half = -(-hidden // (2 * LANES)) * LANES
    padding = 2 * half - hidden
    own = c * 2 + y

    kv_columns = low(keyvalue_weight).reshape(narrow_rows, 2, KV, HD)
    kv_columns = jnp.transpose(kv_columns, (2, 1, 0, 3))
    small = jnp.concatenate([low(norm_gains).reshape(-1), low(keyvalue_bias)])
    small = jnp.pad(small, (0, HD - small.shape[0])).reshape(1, 1, 1, HD)
    small = jnp.pad(small, ((0, 0), (0, 0), (0, 15), (0, 0)))
    blocks = jnp.concatenate([kv_columns, jnp.broadcast_to(small, (2, 2, 16, HD))], axis=2)
    blocks = exchange_narrow(blocks).reshape(4, narrow_rows + 16, HD)
    kv_mine = blocks[:, :narrow_rows].reshape(rows, HD)
    small_row = blocks[:, narrow_rows].reshape(1, 4 * HD)
    bias_row = jnp.pad(low(query_bias).reshape(1, -1), ((0, 0), (0, 4 * HD - heads * bias_part)))
    extra = jnp.pad(jnp.concatenate([small_row, bias_row]), ((0, 14), (0, 0)))
    packed = jnp.concatenate(
        [jnp.concatenate([low(query_weight), kv_mine], axis=1), extra], axis=0
    )
    packed = gather_wide(packed)
    w_qkv = packed[:, :rows].reshape(D, 4 * HD)
    small_all = wide_float(packed[:, rows]).reshape(wide, 4, HD)
    gains = small_all[:, :, : 2 * narrow_rows].reshape(wide, 4, 2, narrow_rows)
    gains = jnp.transpose(gains, (2, 0, 1, 3)).reshape(2, D)
    b_kv = small_all[:, :, 2 * narrow_rows : 2 * narrow_rows + kv_part].reshape(2 * KV, HD)
    b_query = wide_float(packed[:, rows + 1, : heads * bias_part]).reshape(wide, heads, bias_part)
    b_query = jnp.transpose(b_query, (1, 0, 2)).reshape(heads * HD)
    b_qkv = jnp.concatenate([b_query, pick(b_kv, column_block)])
    gain_one, gain_two = gains[0], gains[1]

    w_output = gather_wide(low(output_weight).T)
    w_output = w_output.reshape(D, heads * HD)

    def padded(shard):
        return jnp.pad(low(shard), ((0, 0), (0, padding)))

    w_gate = gather_hidden(padded(gateup_weight[:, 0]))
    w_up = gather_hidden(padded(gateup_weight[:, 1]))
    w_down = gather_hidden(padded(down_weight.T))

    input_float = wide_float(layer_input)
    inverse_one = lax.rsqrt(jnp.mean(input_float * input_float, axis=-1, keepdims=True) + norm_eps)
    normed_one = low(input_float * inverse_one * gain_one)
    linear = (matmul(normed_one, w_qkv) + b_qkv).reshape(tokens, 4, HD)
    cosine, sine = rotation(positions)
    kv_cosine = jnp.where(c == 0, cosine, 1.0)
    kv_sine = jnp.where(c == 0, sine, 0.0)
    queries = low(rotate(linear[:, :heads], cosine, sine) * head_scale).reshape(tokens, heads * HD)
    kv_own = low(rotate(linear[:, heads:], kv_cosine, kv_sine)).reshape(tokens, HD)
    both = pair(kv_own, swap(kv_own, "x"), x)
    kv_row = pair(both, swap(both, "lo"), lo).reshape(4 * tokens, HD)
    kv_other = swap(kv_row, "c")
    keys = jnp.where(c == 0, kv_row, kv_other)
    values = jnp.where(c == 0, kv_other, kv_row)
    begins = segment_ids - hi * (4 * tokens)
    starts = begins[::BLOCK_Q]
    begins = begins[:, None]
    place = (lo * 2 + x).reshape(1).astype(jnp.int32)
    attention, log_total = attention_forward(queries, keys, values, begins, starts, place)
    attention_low = low(attention)

    def halves(block):
        split = block.reshape(2, -1, block.shape[-1])
        return pick(split, c), pick(split, 1 - c)

    def scatter_narrow(kept, sent):
        total = (kept + wide_float(swap(low(sent), "c"))).reshape(2, quarter, D)
        return pick(total, y) + wide_float(swap(low(pick(total, 1 - y)), "y"))

    attention_kept, attention_sent = halves(attention_low)
    sent = matmul_nt(attention_sent, w_output)
    attention_out = scatter_narrow(matmul_nt(attention_kept, w_output), sent)
    residual = wide_float(pick(layer_input.reshape(4, quarter, D), own)) + attention_out
    inverse_two = lax.rsqrt(jnp.mean(residual * residual, axis=-1, keepdims=True) + norm_eps)
    unit_two = residual * inverse_two
    normed_two = low(unit_two * gain_two)

    by_y = swap(normed_two, "y")
    by_lo = swap(normed_two, "lo")
    by_both = swap(by_y, "lo")
    core_tokens = jnp.concatenate([normed_two, by_y, by_lo, by_both])
    ff_input = jnp.concatenate([core_tokens, swap(core_tokens, "c")])
    grad_blocks = grad_out.reshape(4, quarter, D)
    grad_own = pick(grad_blocks, own)
    grad_near = jnp.concatenate([grad_own, pick(grad_blocks, c * 2 + 1 - y)])
    grad_far = swap(grad_near, "lo")
    grad_core = jnp.concatenate(
        [pick(grad_blocks, (1 - c) * 2 + y), pick(grad_blocks, (1 - c) * 2 + 1 - y)]
    )
    ff_grad = jnp.concatenate([grad_near, grad_far, grad_core, swap(grad_far, "c")])

    gate = matmul(ff_input, w_gate)
    upward = matmul(ff_input, w_up)
    grad_hidden = matmul(ff_grad, w_down)
    logistic = jax.nn.sigmoid(gate)
    active = gate * logistic
    hidden_low = low(active * upward)
    grad_gate = low(grad_hidden * upward * logistic * (1.0 + gate * (1.0 - logistic)))
    grad_upward = low(grad_hidden * active)

    def scatter_group(kept, sent):
        total = kept + wide_float(swap(low(sent), "c"))
        total = total.reshape(2, 2, quarter, D)
        total = total[:, 0] + wide_float(swap(low(total[:, 1]), "y"))
        return total[0] + wide_float(swap(low(total[1]), "lo"))

    count = 4 * quarter

    def feed_back(at):
        part = slice(at * count, (at + 1) * count)
        return matmul_nt(grad_gate[part], w_gate) + matmul_nt(grad_upward[part], w_up)

    grad_sent = feed_back(1)
    grad_normed_two = scatter_group(feed_back(0), grad_sent)
    grad_residual = wide_float(grad_own) + rms_back(
        grad_normed_two * gain_two, unit_two, inverse_two
    )
    residual_low = gather_tokens(low(grad_residual))

    mlp_sent = matmul_nt(hidden_low[count:], w_down)
    mlp_out = scatter_group(matmul_nt(hidden_low[:count], w_down), mlp_sent)
    layer_output = gather_tokens(low(residual + mlp_out))

    summed_down = scatter_hidden(low(matmul_tn(ff_grad, hidden_low)))
    summed_gate = scatter_hidden(low(matmul_tn(ff_input, grad_gate)))
    summed_up = scatter_hidden(low(matmul_tn(ff_input, grad_upward)))

    grad_attention = low(matmul(residual_low, w_output))
    summed_output = scatter_wide(
        low(matmul_tn(residual_low, attention_low)).reshape(wide, rows, heads * HD)
    )
    grad_queries, grad_keys, grad_values = attention_backward(
        queries, keys, values, begins, starts, place, grad_attention, log_total, attention
    )
    kv_sent = low(jnp.where(c == 0, grad_values, grad_keys))
    kv_grad = jnp.where(c == 0, grad_keys, grad_values) + wide_float(swap(kv_sent, "c"))
    kv_grad = kv_grad.reshape(2, 2 * tokens, HD)
    kv_grad = pick(kv_grad, lo) + wide_float(swap(low(pick(kv_grad, 1 - lo)), "lo"))
    kv_grad = kv_grad.reshape(2, tokens, HD)
    kv_grad = pick(kv_grad, x) + wide_float(swap(low(pick(kv_grad, 1 - x)), "x"))
    kv_grad = rotate(kv_grad[:, None], kv_cosine, -kv_sine)
    query_grad = rotate(
        grad_queries.reshape(tokens, heads, HD) * head_scale, cosine, -sine
    )
    grad_linear = low(jnp.concatenate([query_grad, kv_grad], axis=1)).reshape(tokens, 4 * HD)

    linear_kept, linear_sent = halves(grad_linear)
    part_sent = matmul_nt(linear_sent, w_qkv)
    grad_normed_one = scatter_narrow(matmul_nt(linear_kept, w_qkv), part_sent)
    own_input = wide_float(pick(layer_input.reshape(4, quarter, D), own))
    own_inverse = lax.rsqrt(jnp.mean(own_input * own_input, axis=-1, keepdims=True) + norm_eps)
    input_grad = gather_tokens(
        low(
            grad_residual
            + rms_back(grad_normed_one * gain_one, own_input * own_inverse, own_inverse)
        )
    )

    grad_qkv = low(matmul_tn(normed_one, grad_linear)).reshape(wide, rows, 4 * HD)
    bias_sums = jnp.sum(wide_float(grad_linear), axis=0).reshape(4, HD)
    bias_query = jnp.transpose(bias_sums[:heads].reshape(heads, wide, bias_part), (1, 0, 2))
    bias_query = bias_query.reshape(wide, heads * bias_part)
    bias_kv = lax.dynamic_update_slice(
        jnp.zeros((2 * KV, HD), jnp.float32), bias_sums[heads:], (column_block, 0)
    ).reshape(wide, 4 * kv_part)
    bias_all = jnp.concatenate([bias_query, bias_kv], axis=1)
    bias_all = jnp.pad(bias_all, ((0, 0), (0, 4 * HD - bias_all.shape[1])))
    extra = jnp.pad(low(bias_all)[:, None], ((0, 0), (0, 15), (0, 0)))
    summed = scatter_wide(jnp.concatenate([grad_qkv, extra], axis=1))
    summed_query = summed[:rows, : heads * HD]
    summed_kv = summed[:rows, heads * HD :]
    summed_query_bias = summed[rows, : heads * bias_part].reshape(heads, bias_part)
    kv_bias = summed[rows, heads * bias_part : heads * bias_part + 4 * kv_part]

    my_gains = lax.dynamic_slice_in_dim(gains, (hi * 4 + lo * 2 + x) * rows, rows, axis=1)
    my_w = wide_float(lax.dynamic_slice_in_dim(w_qkv, (hi * 4 + lo * 2 + x) * rows, rows, axis=0))
    grad_gain_one = jnp.sum(summed[:rows] * my_w, axis=1) / my_gains[0]
    summed_gateup = jnp.stack([summed_gate[:, :hidden], summed_up[:, :hidden]], axis=1)
    grad_gain_two = (
        jnp.sum(summed_gateup * wide_float(low(gateup_weight)), axis=(1, 2)) / my_gains[1]
    )
    gain_parts = jnp.stack([grad_gain_one, grad_gain_two]).reshape(2, 4, narrow_rows)
    gain_parts = jnp.transpose(gain_parts, (1, 0, 2)).reshape(4, 2 * narrow_rows)
    last = jnp.concatenate([gain_parts, kv_bias.reshape(4, kv_part)], axis=1)
    last = jnp.pad(last, ((0, 0), (0, HD - last.shape[1])))[:, None]
    last = jnp.pad(last, ((0, 0), (0, 7), (0, 0)))
    last = jnp.concatenate([summed_kv.reshape(4, narrow_rows, HD), last], axis=1)
    last = exchange_narrow(last.reshape((2, 2) + last.shape[1:]))
    summed_keyvalue = jnp.transpose(last[:, :, :narrow_rows], (2, 1, 0, 3))
    summed_keyvalue = summed_keyvalue.reshape(narrow_rows, 2 * KV * HD)
    small_sums = jnp.sum(last[:, :, narrow_rows], axis=(0, 1))
    summed_gains = small_sums[: 2 * narrow_rows].reshape(2, narrow_rows)
    summed_keyvalue_bias = small_sums[2 * narrow_rows : 2 * narrow_rows + kv_part]
    summed_down = summed_down[:, :hidden].T
    summed_output = summed_output.T

    gains_update = adam_update(
        summed_gains, norm_gains, norm_gains_first, norm_gains_second, False, token_count
    )
    query_update = adam_update(
        summed_query, query_weight, query_weight_first, query_weight_second, True, token_count
    )
    qbias_update = adam_update(
        summed_query_bias, query_bias, query_bias_first, query_bias_second, False, token_count
    )
    keyvalue_update = adam_update(
        summed_keyvalue,
        keyvalue_weight,
        keyvalue_weight_first,
        keyvalue_weight_second,
        True,
        token_count,
    )
    kvbias_update = adam_update(
        summed_keyvalue_bias,
        keyvalue_bias,
        keyvalue_bias_first,
        keyvalue_bias_second,
        False,
        token_count,
    )
    output_update = adam_update(
        summed_output, output_weight, output_weight_first, output_weight_second, True, token_count
    )
    gateup_update = adam_update(
        summed_gateup, gateup_weight, gateup_weight_first, gateup_weight_second, True, token_count
    )
    down_update = adam_update(
        summed_down, down_weight, down_weight_first, down_weight_second, True, token_count
    )
    return (
        layer_output,
        input_grad,
        *gains_update,
        *query_update,
        *qbias_update,
        *keyvalue_update,
        *kvbias_update,
        *output_update,
        *gateup_update,
        *down_update,
    )


def solution(mesh):
    devices = mesh.devices.reshape(-1, 2, 2, 2, 2)
    split = Mesh(devices, WIDE + NARROW)
    token_matrix = P(WIDE, None)
    token_vector = P(WIDE)
    gains = P(None, WIDE + NARROW)
    query = P(WIDE, NARROW)
    by_narrow = P(NARROW, WIDE)
    keyvalue = P(WIDE + NARROW, None)
    keyvalue_bias = P(WIDE + NARROW)
    gateup = P(WIDE, None, NARROW)
    parameters = (gains, query, by_narrow, keyvalue, keyvalue_bias, by_narrow, gateup, by_narrow)
    in_specs = (token_matrix, token_matrix, token_vector, token_vector)
    out_specs = (token_matrix, token_matrix)
    for spec in parameters:
        in_specs += (spec,) * 3
        out_specs += (spec,) * 2
    return jax.shard_map(local, mesh=split, in_specs=in_specs, out_specs=out_specs, check_vma=False)
```

time: 1810 us -> 917 us (0.51)
  waiting for transfers between devices: 1130 us -> 396 us
  matrix products: 296 us -> 142 us
  blocking collectives: 135 us -> 0 us
  starting transfers between devices: 26.6 us -> 129 us
  Pallas kernels: 0 us -> 26.4 us
    reduce_scatter x5 -> x0, waiting for transfers between devices: 513 us -> none  [the longest x1 226 us: local(): lax.psum_scatter(grad_gateup.astype(jnp.bfloat16), 'wide', scatter_dimens...]
    ppermute x9 -> x69, waiting for transfers between devices: 0.02 us -> 396 us  [swap(): return lax.ppermute(block, axis, [(i, i ^ distance) for i in range(size)])]
    all_gather x5 -> x0, waiting for transfers between devices: 283 us -> none  [the longest x1 195 us: local(): lax.all_gather(gateup_weight.astype(jnp.bfloat16), 'wide', axis=0, tiled=...]
    psum x3 -> x0, waiting for transfers between devices: 245 us -> none  [the longest x1 114 us: local(): lax.psum(jnp.dot(hidden, w_down, preferred_element_type=jnp.float32).asty...]
    dot_general x39 -> x20, matrix products: 296 us -> 142 us  [the longest x10 52.9 us: matmul_nt(): lax.dot_general(left, right, (((1,), (1,)), ((), ())), preferred_element_...]
    ppermute x9 -> x69, starting transfers between devices: 25.8 us -> 129 us  [swap(): return lax.ppermute(block, axis, [(i, i ^ distance) for i in range(size)])]
    unnamed x17 -> x0, waiting for transfers between devices: 88.8 us -> none
    unnamed x2 -> x0, blocking collectives: 78.7 us -> none
  transfers between devices with their start and end apart: 24 -> 69, of which waited for: 10 -> 30; matrix products, arithmetic and copies ran while one was open for 19% -> 26% of each run, Pallas kernels for 0% -> 3%
where the time goes in v1:
time: 917 us; the launch traced here: 905 us
  waiting for transfers between devices  396 us (43%)
  matrix products  142 us (15%)
  starting transfers between devices  129 us (14%)
  other arithmetic  114 us (12%)
  local copies, waits for them, and re-layouts  95.6 us (10%)
  Pallas kernels  26.4 us (3%)
    ppermute x69, waiting for transfers between devices, swap(): return lax.ppermute(block, axis, [(i, i ^ distance) for i in range(size)])  396 us
    ppermute x69, starting transfers between devices, swap(): return lax.ppermute(block, axis, [(i, i ^ distance) for i in range(size)])  129 us
    dot_general x10, matrix products, matmul_nt(): lax.dot_general(left, right, (((1,), (1,)), ((), ())), preferred_element_...  52.9 us
    dot_general x5, matrix products, matmul(): return jnp.dot(left, right, preferred_element_type=jnp.float32)  48.7 us
    dot_general x5, matrix products, matmul_tn(): lax.dot_general(left, right, (((0,), (0,)), ((), ())), preferred_element_...  39.9 us
    unnamed x225, local copies, waits for them, and re-layouts  31.3 us
    select_n x20, other arithmetic, pair(): jnp.where(index == 0, jnp.stack([mine, other]), jnp.stack([other, mine]))  24.6 us
    convert_element_type x19, other arithmetic, low(): return a.astype(jnp.bfloat16)  21.8 us
  transfers between devices with their start and end apart: 69, of which 30 were waited for; matrix products, arithmetic and copies ran while one was open for 26% of the time, Pallas kernels for 3%

profile of v1, /device:TPU:0, one launch (start us, length us, event | category | flops | bytes accessed | tf_op | source)
XLA Modules:
  0.0 905.0 jit_solution(7771658148577127468)
XLA Ops:
  29.4 12.5 %collective-permute-done.3 = bf16[208,512]{1,0:T(8,128)(2,1)S(1)} collective-permute-done((bf16[208,512]{1,0:T(8,128)(2,1)S(1)}, bf16[208,512]{1,0:T(8,128)(2,1)S(1)}, u32[]{:S(2)}, u32[]{:S(2)}) %collective-permute-start.3) | collective-permute-done | bytes 213024 | tf_op jit(solution)/shard_map/ppermute | solution.py:56
  48.7 14.1 %collective-permute-done.5 = bf16[2,208,512]{2,1,0:T(8,128)(2,1)S(1)} collective-permute-done((bf16[2,208,512]{2,1,0:T(8,128)(2,1)S(1)}, bf16[2,208,512]{2,1,0:T(8,128)(2,1)S(1)}, u32[]{:S(2)}, u32[]{:S(2)}) %collective-permute-start.5) | collective-permute-done | bytes 426016 | tf_op jit(solution)/shard_map/ppermute | solution.py:56
  110.8 11.3 %collective-permute-done.12 = bf16[2,192,384]{2,1,0:T(8,128)(2,1)} collective-permute-done((bf16[2,192,384]{2,1,0:T(8,128)(2,1)}, bf16[2,192,384]{2,1,0:T(8,128)(2,1)}, u32[]{:S(2)}, u32[]{:S(2)}) %collective-permute-start.12) | collective-permute-done | bytes 294944 | tf_op jit(solution)/shard_map/ppermute | solution.py:56
  138.3 11.4 %attention_forward.1 = (f32[1024,384]{1,0:T(8,128)}, f32[3,1024,1]{2,1,0:T(8,128)}) custom-call(s32[4]{0:T(128)} %slice.176.starts_ref, s32[1]{0:T(128)} %bitcast.2.place_ref, bf16[1024,384]{1,0:T(8,128)(2,1)} %copy.161.q_ref, bf16[4096,128]{1,0:T(8,128)(2,1)} %get-tuple-element.133.k_ref, bf16[4096,128]{1,0:T(8,128)(2,1)} %get-tuple-element.132.v_ref, ...), custom_call_target="tpu_custom_call" | custom-call | tf_op jit(solution)/shard_map/attention_forward/pallas_call | solution.py:244
  186.7 18.5 %collective-permute-done.21 = bf16[2,192,1152]{2,1,0:T(8,128)(2,1)} collective-permute-done((bf16[2,192,1152]{2,1,0:T(8,128)(2,1)}, bf16[2,192,1152]{2,1,0:T(8,128)(2,1)}, u32[]{:S(2)}, u32[]{:S(2)}) %collective-permute-start.21) | collective-permute-done | bytes 884768 | tf_op jit(solution)/shard_map/ppermute | solution.py:56
  211.8 12.7 %collective-permute-done.15 = bf16[256,1536]{1,0:T(8,128)(2,1)S(1)} collective-permute-done((bf16[256,1536]{1,0:T(8,128)(2,1)S(1)}, bf16[256,1536]{1,0:T(8,128)(2,1)S(1)}, u32[]{:S(2)}, u32[]{:S(2)}) %collective-permute-start.15) | collective-permute-done | bytes 786464 | tf_op jit(solution)/shard_map/ppermute | solution.py:56
  230.8 24.3 %collective-permute-done.22 = bf16[2,192,1152]{2,1,0:T(8,128)(2,1)S(1)} collective-permute-done((bf16[2,192,1152]{2,1,0:T(8,128)(2,1)}, bf16[2,192,1152]{2,1,0:T(8,128)(2,1)S(1)}, u32[]{:S(2)}, u32[]{:S(2)}) %collective-permute-start.22) | collective-permute-done | bytes 884768 | tf_op jit(solution)/shard_map/ppermute | solution.py:56
  255.1 9.8 %collective-permute-start.31 = (bf16[2,192,1152]{2,1,0:T(8,128)(2,1)}, bf16[2,192,1152]{2,1,0:T(8,128)(2,1)S(1)}, u32[]{:S(2)}, u32[]{:S(2)}) collective-permute-start(bf16[2,192,1152]{2,1,0:T(8,128)(2,1)} %collective-permute-done.30), channel_id=1, source_target_pairs={{0,4},{4,0},{1,5},{5,1},{2,6},{6,2},{3,7},{7,3},{8,12},{12,8},{9,1... | collective-permute-start | bytes 2654216 | tf_op jit(solution)/shard_map/ppermute | solution.py:56
  273.8 9.8 %collective-permute-start.23 = (bf16[2,192,1152]{2,1,0:T(8,128)(2,1)S(1)}, bf16[2,192,1152]{2,1,0:T(8,128)(2,1)S(1)}, u32[]{:S(2)}, u32[]{:S(2)}) collective-permute-start(bf16[2,192,1152]{2,1,0:T(8,128)(2,1)S(1)} %collective-permute-done.22), channel_id=1, source_target_pairs={{0,4},{4,0},{1,5},{5,1},{2,6},{6,2},{3,7},{7,3},{8,12},{12,8},{9,1... | collective-permute-start | bytes 2654216 | tf_op jit(solution)/shard_map/ppermute | solution.py:56
  290.6 16.8 %collective-permute-done.18 = bf16[256,1536]{1,0:T(8,128)(2,1)S(1)} collective-permute-done((bf16[256,1536]{1,0:T(8,128)(2,1)S(1)}, bf16[256,1536]{1,0:T(8,128)(2,1)S(1)}, u32[]{:S(2)}, u32[]{:S(2)}) %collective-permute-start.18) | collective-permute-done | bytes 786464 | tf_op jit(solution)/shard_map/ppermute | solution.py:56
  310.3 11.9 %collective-permute-done.27 = bf16[2,192,1152]{2,1,0:T(8,128)(2,1)S(1)} collective-permute-done((bf16[2,192,1152]{2,1,0:T(8,128)(2,1)S(1)}, bf16[2,192,1152]{2,1,0:T(8,128)(2,1)S(1)}, u32[]{:S(2)}, u32[]{:S(2)}) %collective-permute-start.27) | collective-permute-done | bytes 884768 | tf_op jit(solution)/shard_map/ppermute | solution.py:56
  325.4 11.0 %fusion.131 = f32[2048,1152]{1,0:T(8,128)} fusion(bf16[2048,1536]{1,0:T(8,128)(2,1)S(1)} %constant_dynamic-update-slice_fusion, bf16[1536,1152]{1,0:T(8,128)(2,1)S(1)} %bitcast.472), kind=kOutput, calls=%fused_computation.349 | convolution fusion | flops 7247757312 | bytes 19267584 | tf_op jit(solution)/shard_map/dot_general | solution.py:41
  336.4 10.6 %fusion.130 = f32[2048,1152]{1,0:T(8,128)} fusion(bf16[2048,1536]{1,0:T(8,128)(2,1)S(1)} %constant_dynamic-update-slice_fusion, bf16[1536,1152]{1,0:T(8,128)(2,1)S(1)} %bitcast.469), kind=kOutput, calls=%fused_computation.348 | convolution fusion | flops 7247757312 | bytes 19267584 | tf_op jit(solution)/shard_map/dot_general | solution.py:41
  347.0 20.9 %multiply_convert_fusion.1 = (bf16[2048,1152]{1,0:T(8,128)(2,1)}, bf16[2048,1152]{1,0:T(8,128)(2,1)}, bf16[2048,1152]{1,0:T(8,128)(2,1)}) fusion(f32[2048,1152]{1,0:T(8,128)} %fusion.130, f32[2048,1152]{1,0:T(8,128)} %fusion.131, bf16[2048,1536]{1,0:T(8,128)(2,1)} %copy-done.76, bf16[1536,1152]{1,0:T(8,128)(2,1)} %bitcast.475), kind=kOutput, calls=%fused_computation.1 | convolution fusion | flops 7283146752 | bytes 42860544 | tf_op jit(solution)/shard_map/dot_general | solution.py:41
  368.0 12.2 %convolution_convert_fusion = bf16[1536,1152]{1,0:T(8,128)(2,1)S(1)} fusion(bf16[2048,1536]{1,0:T(8,128)(2,1)} %copy-done.76, bf16[2048,1152]{1,0:T(8,128)(2,1)} %get-tuple-element.124), kind=kOutput, calls=%fused_computation.7 | convolution fusion | flops 7249526784 | bytes 14548992 | tf_op jit(solution)/shard_map/dot_general | solution.py:49
  385.9 11.2 %convolution_convert_fusion.2 = bf16[1536,1152]{1,0:T(8,128)(2,1)S(1)} fusion(bf16[2048,1536]{1,0:T(8,128)(2,1)S(1)} %copy-done.78, bf16[2048,1152]{1,0:T(8,128)(2,1)} %get-tuple-element.122), kind=kOutput, calls=%fused_computation.9 | convolution fusion | flops 7249526784 | bytes 14548992 | tf_op jit(solution)/shard_map/dot_general | solution.py:49
  405.2 11.3 %convolution_convert_fusion.1 = bf16[1536,1152]{1,0:T(8,128)(2,1)S(1)} fusion(bf16[2048,1536]{1,0:T(8,128)(2,1)S(1)} %copy-done.78, bf16[2048,1152]{1,0:T(8,128)(2,1)} %get-tuple-element.123), kind=kOutput, calls=%fused_computation.8 | convolution fusion | flops 7249526784 | bytes 14548992 | tf_op jit(solution)/shard_map/dot_general | solution.py:49
  447.2 18.8 %collective-permute-done.66 = bf16[2,2,192,1152]{3,2,1,0:T(8,128)(2,1)} collective-permute-done((bf16[2,2,192,1152]{3,2,1,0:T(8,128)(2,1)}, bf16[2,2,192,1152]{3,2,1,0:T(8,128)(2,1)}, u32[]{:S(2)}, u32[]{:S(2)}) %collective-permute-start.66) | collective-permute-done | bytes 1769504 | tf_op jit(solution)/shard_map/ppermute | solution.py:56
  468.1 35.8 %collective-permute-done.57 = bf16[2,2,192,1152]{3,2,1,0:T(8,128)(2,1)S(1)} collective-permute-done((bf16[2,2,192,1152]{3,2,1,0:T(8,128)(2,1)}, bf16[2,2,192,1152]{3,2,1,0:T(8,128)(2,1)S(1)}, u32[]{:S(2)}, u32[]{:S(2)}) %collective-permute-start.57) | collective-permute-done | bytes 1769504 | tf_op jit(solution)/shard_map/ppermute | solution.py:56
  504.4 35.5 %collective-permute-done.54 = bf16[2,2,192,1152]{3,2,1,0:T(8,128)(2,1)S(1)} collective-permute-done((bf16[2,2,192,1152]{3,2,1,0:T(8,128)(2,1)}, bf16[2,2,192,1152]{3,2,1,0:T(8,128)(2,1)S(1)}, u32[]{:S(2)}, u32[]{:S(2)}) %collective-permute-start.54) | collective-permute-done | bytes 1769504 | tf_op jit(solution)/shard_map/ppermute | solution.py:56
  544.9 16.5 %collective-permute-done.58 = bf16[2,192,1152]{2,1,0:T(8,128)(2,1)S(1)} collective-permute-done((bf16[2,192,1152]{2,1,0:T(8,128)(2,1)S(1)}, bf16[2,192,1152]{2,1,0:T(8,128)(2,1)S(1)}, u32[]{:S(2)}, u32[]{:S(2)}) %collective-permute-start.58) | collective-permute-done | bytes 884768 | tf_op jit(solution)/shard_map/ppermute | solution.py:56
  583.3 23.0 %collective-permute-done.40 = bf16[2,256,1536]{2,1,0:T(8,128)(2,1)S(1)} collective-permute-done((bf16[2,256,1536]{2,1,0:T(8,128)(2,1)S(1)}, bf16[2,256,1536]{2,1,0:T(8,128)(2,1)S(1)}, u32[]{:S(2)}, u32[]{:S(2)}) %collective-permute-start.40) | collective-permute-done | bytes 1572896 | tf_op jit(solution)/shard_map/ppermute | solution.py:56
  609.0 29.8 %collective-permute-done.33 = bf16[2,256,1536]{2,1,0:T(8,128)(2,1)S(1)} collective-permute-done((bf16[2,256,1536]{2,1,0:T(8,128)(2,1)S(1)}, bf16[2,256,1536]{2,1,0:T(8,128)(2,1)S(1)}, u32[]{:S(2)}, u32[]{:S(2)}) %collective-permute-start.33) | collective-permute-done | bytes 1572896 | tf_op jit(solution)/shard_map/ppermute | solution.py:56
  643.7 14.1 %collective-permute-done.34 = bf16[256,1536]{1,0:T(8,128)(2,1)S(1)} collective-permute-done((bf16[256,1536]{1,0:T(8,128)(2,1)S(1)}, bf16[256,1536]{1,0:T(8,128)(2,1)S(1)}, u32[]{:S(2)}, u32[]{:S(2)}) %collective-permute-start.34) | collective-permute-done | bytes 786464 | tf_op jit(solution)/shard_map/ppermute | solution.py:56
  662.5 14.8 %collective-permute-done.42 = bf16[256,1536]{1,0:T(8,128)(2,1)S(1)} collective-permute-done((bf16[256,1536]{1,0:T(8,128)(2,1)S(1)}, bf16[256,1536]{1,0:T(8,128)(2,1)S(1)}, u32[]{:S(2)}, u32[]{:S(2)}) %collective-permute-start.42) | collective-permute-done | bytes 786464 | tf_op jit(solution)/shard_map/ppermute | solution.py:56
  688.6 15.0 %attention_backward.1 = (f32[1024,384]{1,0:T(8,128)}, f32[4096,128]{1,0:T(8,128)}, f32[4096,128]{1,0:T(8,128)}) custom-call(s32[4]{0:T(128)} %slice.176.starts_ref, s32[1]{0:T(128)} %bitcast.2.place_ref, bf16[1024,384]{1,0:T(8,128)(2,1)} %copy.161.q_ref, bf16[4096,128]{1,0:T(8,128)(2,1)} %get-tuple-element.133.k_ref, ...), custom_call_target="tpu_custom_call" | custom-call | tf_op jit(solution)/shard_map/attention_backward/pallas_call | solution.py:308
  730.6 24.2 %collective-permute-start.45 = (bf16[2048,128]{1,0:T(8,128)(2,1)S(1)}, bf16[2048,128]{1,0:T(8,128)(2,1)S(1)}, u32[]{:S(2)}, u32[]{:S(2)}) collective-permute-start(bf16[2048,128]{1,0:T(8,128)(2,1)S(1)} %fusion.63), channel_id=1, source_target_pairs={{0,8},{8,0},{1,9},{9,1},{2,10},{10,2},{3,11},{11,3},{4,12},{12,4},... | collective-permute-start | bytes 1572872 | tf_op jit(solution)/shard_map/ppermute | solution.py:56
  757.6 12.3 %collective-permute-start.63 = (bf16[2,2,192,384]{3,2,1,0:T(8,128)(2,1)}, bf16[2,2,192,384]{3,2,1,0:T(8,128)(2,1)}, u32[]{:S(2)}, u32[]{:S(2)}) collective-permute-start(bf16[2,2,192,384]{3,2,1,0:T(8,128)(2,1)} %dynamic-slice_bitcast_fusion.8), channel_id=1, source_target_pairs={{0,4},{4,0},{1,5},{5,1},{2,6},{6,2},{3,7},{7,3},{8,12},{12,8},{9,1... | collective-permute-start | bytes 1769480 | tf_op jit(solution)/shard_map/ppermute | solution.py:56
  771.9 10.0 %collective-permute-start.46 = (bf16[1024,128]{0,1:T(8,128)(2,1)}, bf16[1024,128]{0,1:T(8,128)(2,1)}, u32[]{:S(2)}, u32[]{:S(2)}) collective-permute-start(bf16[1024,128]{0,1:T(8,128)(2,1)} %bitcast.393), channel_id=1, source_target_pairs={{0,4},{4,0},{1,5},{5,1},{2,6},{6,2},{3,7},{7,3},{8,12},{12,8},{9,1... | collective-permute-start | bytes 786440 | tf_op jit(solution)/shard_map/ppermute | solution.py:56
  827.5 10.2 %collective-permute-done.64 = bf16[2,192,384]{2,1,0:T(8,128)(2,1)S(1)} collective-permute-done((bf16[2,192,384]{2,1,0:T(8,128)(2,1)S(1)}, bf16[2,192,384]{2,1,0:T(8,128)(2,1)S(1)}, u32[]{:S(2)}, u32[]{:S(2)}) %collective-permute-start.64) | collective-permute-done | bytes 294944 | tf_op jit(solution)/shard_map/ppermute | solution.py:56
  859.7 12.0 %collective-permute-done.48 = bf16[256,1536]{1,0:T(8,128)(2,1)} collective-permute-done((bf16[256,1536]{1,0:T(8,128)(2,1)}, bf16[256,1536]{1,0:T(8,128)(2,1)}, u32[]{:S(2)}, u32[]{:S(2)}) %collective-permute-start.48) | collective-permute-done | bytes 786464 | tf_op jit(solution)/shard_map/ppermute | solution.py:56
  883.6 11.9 %collective-permute-done.49 = bf16[256,1536]{1,0:T(8,128)(2,1)S(1)} collective-permute-done((bf16[256,1536]{1,0:T(8,128)(2,1)}, bf16[256,1536]{1,0:T(8,128)(2,1)S(1)}, u32[]{:S(2)}, u32[]{:S(2)}) %collective-permute-start.49) | collective-permute-done | bytes 786464 | tf_op jit(solution)/shard_map/ppermute | solution.py:56
  (568 shorter events, 387.9 us)
Async XLA Ops:
  8.8 96.7 %collective-permute-start.10 = (bf16[192,384]{1,0:T(8,128)(2,1)}, bf16[192,384]{1,0:T(8,128)(2,1)}, u32[]{:S(2)}, u32[]{:S(2)}) collective-permute-start(bf16[192,384]{1,0:T(8,128)(2,1)} %get-tuple-element.160), channel_id=1, source_target_pairs={{0,8},{8,0},{1,9},{9,1},{2,10},{10,2},{3,11},{11,3},{4,12},{12,4},... | collective-permute-start | bytes 442376 | tf_op jit(solution)/shard_map/ppermute | solution.py:56
  15.6 137.8 %collective-permute-start.28 = (bf16[192,1152]{1,0:T(8,128)(2,1)}, bf16[192,1152]{1,0:T(8,128)(2,1)}, u32[]{:S(2)}, u32[]{:S(2)}) collective-permute-start(bf16[192,1152]{1,0:T(8,128)(2,1)} %get-tuple-element.154), channel_id=1, source_target_pairs={{0,8},{8,0},{1,9},{9,1},{2,10},{10,2},{3,11},{11,3},{4,12},{12,4},... | collective-permute-start | bytes 1327112 | tf_op jit(solution)/shard_map/ppermute | solution.py:56
  24.4 143.4 %collective-permute-start.24 = (bf16[192,1152]{1,0:T(8,128)(2,1)}, bf16[192,1152]{1,0:T(8,128)(2,1)}, u32[]{:S(2)}, u32[]{:S(2)}) collective-permute-start(bf16[192,1152]{1,0:T(8,128)(2,1)} %get-tuple-element.151), channel_id=1, source_target_pairs={{0,8},{8,0},{1,9},{9,1},{2,10},{10,2},{3,11},{11,3},{4,12},{12,4},... | collective-permute-start | bytes 1327112 | tf_op jit(solution)/shard_map/ppermute | solution.py:56
  130.2 153.5 %collective-permute-start.37 = (bf16[512,1536]{1,0:T(8,128)(2,1)}, bf16[512,1536]{1,0:T(8,128)(2,1)}, u32[]{:S(2)}, u32[]{:S(2)}) collective-permute-start(bf16[512,1536]{1,0:T(8,128)(2,1)} %pad_maximum_fusion.1), channel_id=1, source_target_pairs={{0,8},{8,0},{1,9},{9,1},{2,10},{10,2},{3,11},{11,3},{4,12},{12,4},... | collective-permute-start | bytes 4718600 | tf_op jit(solution)/shard_map/ppermute | solution.py:56
  155.7 72.3 %collective-permute-start.30 = (bf16[2,192,1152]{2,1,0:T(8,128)(2,1)}, bf16[2,192,1152]{2,1,0:T(8,128)(2,1)}, u32[]{:S(2)}, u32[]{:S(2)}) collective-permute-start(bf16[2,192,1152]{2,1,0:T(8,128)(2,1)} %maximum_select_fusion.12), channel_id=1, source_target_pairs={{0,16},{16,0},{1,17},{17,1},{2,18},{18,2},{3,19},{19,3},{4,20},{20... | collective-permute-start | bytes 2654216 | tf_op jit(solution)/shard_map/ppermute | solution.py:56
  157.5 50.3 %collective-permute-start.29 = (bf16[2,192,1152]{2,1,0:T(8,128)(2,1)}, bf16[2,192,1152]{2,1,0:T(8,128)(2,1)}, u32[]{:S(2)}, u32[]{:S(2)}) collective-permute-start(bf16[2,192,1152]{2,1,0:T(8,128)(2,1)} %maximum_select_fusion.12), channel_id=1, source_target_pairs={{0,4},{4,0},{1,5},{5,1},{2,6},{6,2},{3,7},{7,3},{8,12},{12,8},{9,1... | collective-permute-start | bytes 2654216 | tf_op jit(solution)/shard_map/ppermute | solution.py:56
  167.8 37.3 %collective-permute-start.21 = (bf16[2,192,1152]{2,1,0:T(8,128)(2,1)}, bf16[2,192,1152]{2,1,0:T(8,128)(2,1)}, u32[]{:S(2)}, u32[]{:S(2)}) collective-permute-start(bf16[2,192,1152]{2,1,0:T(8,128)(2,1)} %maximum_select_fusion.8), channel_id=1, source_target_pairs={{0,4},{4,0},{1,5},{5,1},{2,6},{6,2},{3,7},{7,3},{8,12},{12,8},{9,1... | collective-permute-start | bytes 2654216 | tf_op jit(solution)/shard_map/ppermute | solution.py:56
  182.6 72.6 %collective-permute-start.22 = (bf16[2,192,1152]{2,1,0:T(8,128)(2,1)}, bf16[2,192,1152]{2,1,0:T(8,128)(2,1)S(1)}, u32[]{:S(2)}, u32[]{:S(2)}) collective-permute-start(bf16[2,192,1152]{2,1,0:T(8,128)(2,1)} %maximum_select_fusion.8), channel_id=1, source_target_pairs={{0,16},{16,0},{1,17},{17,1},{2,18},{18,2},{3,19},{19,3},{4,20},{20... | collective-permute-start | bytes 2654216 | tf_op jit(solution)/shard_map/ppermute | solution.py:56
  207.8 66.0 %collective-permute-start.26 = (bf16[2,192,1152]{2,1,0:T(8,128)(2,1)S(1)}, bf16[2,192,1152]{2,1,0:T(8,128)(2,1)S(1)}, u32[]{:S(2)}, u32[]{:S(2)}) collective-permute-start(bf16[2,192,1152]{2,1,0:T(8,128)(2,1)S(1)} %copy-done.65), channel_id=1, source_target_pairs={{0,16},{16,0},{1,17},{17,1},{2,18},{18,2},{3,19},{19,3},{4,20},{20... | collective-permute-start | bytes 2654216 | tf_op jit(solution)/shard_map/ppermute | solution.py:56
  224.5 40.5 %collective-permute-start.25 = (bf16[2,192,1152]{2,1,0:T(8,128)(2,1)S(1)}, bf16[2,192,1152]{2,1,0:T(8,128)(2,1)S(1)}, u32[]{:S(2)}, u32[]{:S(2)}) collective-permute-start(bf16[2,192,1152]{2,1,0:T(8,128)(2,1)S(1)} %copy-done.65), channel_id=1, source_target_pairs={{0,4},{4,0},{1,5},{5,1},{2,6},{6,2},{3,7},{7,3},{8,12},{12,8},{9,1... | collective-permute-start | bytes 2654216 | tf_op jit(solution)/shard_map/ppermute | solution.py:56
  228.0 37.2 %collective-permute-start.16 = (bf16[256,1536]{1,0:T(8,128)(2,1)S(1)}, bf16[256,1536]{1,0:T(8,128)(2,1)S(1)}, u32[]{:S(2)}, u32[]{:S(2)}) collective-permute-start(bf16[256,1536]{1,0:T(8,128)(2,1)S(1)} %get-tuple-element.119), channel_id=1, source_target_pairs={{0,2},{2,0},{1,3},{3,1},{4,6},{6,4},{5,7},{7,5},{8,10},{10,8},{9,1... | collective-permute-start | bytes 2359304 | tf_op jit(solution)/shard_map/ppermute | solution.py:56
  255.1 55.0 %collective-permute-start.31 = (bf16[2,192,1152]{2,1,0:T(8,128)(2,1)}, bf16[2,192,1152]{2,1,0:T(8,128)(2,1)S(1)}, u32[]{:S(2)}, u32[]{:S(2)}) collective-permute-start(bf16[2,192,1152]{2,1,0:T(8,128)(2,1)} %collective-permute-done.30), channel_id=1, source_target_pairs={{0,4},{4,0},{1,5},{5,1},{2,6},{6,2},{3,7},{7,3},{8,12},{12,8},{9,1... | collective-permute-start | bytes 2654216 | tf_op jit(solution)/shard_map/ppermute | solution.py:56
  265.1 42.3 %collective-permute-start.18 = (bf16[256,1536]{1,0:T(8,128)(2,1)S(1)}, bf16[256,1536]{1,0:T(8,128)(2,1)S(1)}, u32[]{:S(2)}, u32[]{:S(2)}) collective-permute-start(bf16[256,1536]{1,0:T(8,128)(2,1)S(1)} %collective-permute-done.16), channel_id=1, source_target_pairs={{0,8},{8,0},{1,9},{9,1},{2,10},{10,2},{3,11},{11,3},{4,12},{12,4},... | collective-permute-start | bytes 2359304 | tf_op jit(solution)/shard_map/ppermute | solution.py:56
  283.7 38.5 %collective-permute-start.27 = (bf16[2,192,1152]{2,1,0:T(8,128)(2,1)S(1)}, bf16[2,192,1152]{2,1,0:T(8,128)(2,1)S(1)}, u32[]{:S(2)}, u32[]{:S(2)}) collective-permute-start(bf16[2,192,1152]{2,1,0:T(8,128)(2,1)S(1)} %collective-permute-done.26), channel_id=1, source_target_pairs={{0,4},{4,0},{1,5},{5,1},{2,6},{6,2},{3,7},{7,3},{8,12},{12,8},{9,1... | collective-permute-start | bytes 2654216 | tf_op jit(solution)/shard_map/ppermute | solution.py:56
  424.1 41.9 %collective-permute-start.66 = (bf16[2,2,192,1152]{3,2,1,0:T(8,128)(2,1)}, bf16[2,2,192,1152]{3,2,1,0:T(8,128)(2,1)}, u32[]{:S(2)}, u32[]{:S(2)}) collective-permute-start(bf16[2,2,192,1152]{3,2,1,0:T(8,128)(2,1)} %dynamic-slice_bitcast_fusion), channel_id=1, source_target_pairs={{0,4},{4,0},{1,5},{5,1},{2,6},{6,2},{3,7},{7,3},{8,12},{12,8},{9,1... | collective-permute-start | bytes 5308424 | tf_op jit(solution)/shard_map/ppermute | solution.py:56
  425.9 144.5 %collective-permute-start.32 = (bf16[1024,1536]{1,0:T(8,128)(2,1)}, bf16[1024,1536]{1,0:T(8,128)(2,1)}, u32[]{:S(2)}, u32[]{:S(2)}) collective-permute-start(bf16[1024,1536]{1,0:T(8,128)(2,1)} %convolution_convert_fusion.3), channel_id=1, source_target_pairs={{0,1},{1,0},{2,3},{3,2},{4,5},{5,4},{6,7},{7,6},{8,9},{9,8},{10,11... | collective-permute-start | bytes 9437192 | tf_op jit(solution)/shard_map/ppermute | solution.py:56
  428.6 75.2 %collective-permute-start.57 = (bf16[2,2,192,1152]{3,2,1,0:T(8,128)(2,1)}, bf16[2,2,192,1152]{3,2,1,0:T(8,128)(2,1)S(1)}, u32[]{:S(2)}, u32[]{:S(2)}) collective-permute-start(bf16[2,2,192,1152]{3,2,1,0:T(8,128)(2,1)} %dynamic-slice_bitcast_fusion.1), channel_id=1, source_target_pairs={{0,4},{4,0},{1,5},{5,1},{2,6},{6,2},{3,7},{7,3},{8,12},{12,8},{9,1... | collective-permute-start | bytes 5308424 | tf_op jit(solution)/shard_map/ppermute | solution.py:56
  428.9 111.1 %collective-permute-start.54 = (bf16[2,2,192,1152]{3,2,1,0:T(8,128)(2,1)}, bf16[2,2,192,1152]{3,2,1,0:T(8,128)(2,1)S(1)}, u32[]{:S(2)}, u32[]{:S(2)}) collective-permute-start(bf16[2,2,192,1152]{3,2,1,0:T(8,128)(2,1)} %dynamic-slice_bitcast_fusion.2), channel_id=1, source_target_pairs={{0,4},{4,0},{1,5},{5,1},{2,6},{6,2},{3,7},{7,3},{8,12},{12,8},{9,1... | collective-permute-start | bytes 5308424 | tf_op jit(solution)/shard_map/ppermute | solution.py:56
  447.1 115.3 %collective-permute-start.39 = (bf16[1024,1536]{1,0:T(8,128)(2,1)}, bf16[1024,1536]{1,0:T(8,128)(2,1)S(1)}, u32[]{:S(2)}, u32[]{:S(2)}) collective-permute-start(bf16[1024,1536]{1,0:T(8,128)(2,1)} %add_convert_fusion), channel_id=1, source_target_pairs={{0,1},{1,0},{2,3},{3,2},{4,5},{5,4},{6,7},{7,6},{8,9},{9,8},{10,11... | collective-permute-start | bytes 9437192 | tf_op jit(solution)/shard_map/ppermute | solution.py:56
  468.0 73.4 %collective-permute-start.67 = (bf16[2,192,1152]{2,1,0:T(8,128)(2,1)S(1)}, bf16[2,192,1152]{2,1,0:T(8,128)(2,1)S(1)}, u32[]{:S(2)}, u32[]{:S(2)}) collective-permute-start(bf16[2,192,1152]{2,1,0:T(8,128)(2,1)S(1)} %dynamic-slice_bitcast_fusion.3), channel_id=1, source_target_pairs={{0,16},{16,0},{1,17},{17,1},{2,18},{18,2},{3,19},{19,3},{4,20},{20... | collective-permute-start | bytes 2654216 | tf_op jit(solution)/shard_map/ppermute | solution.py:56
  504.3 57.1 %collective-permute-start.58 = (bf16[2,192,1152]{2,1,0:T(8,128)(2,1)S(1)}, bf16[2,192,1152]{2,1,0:T(8,128)(2,1)S(1)}, u32[]{:S(2)}, u32[]{:S(2)}) collective-permute-start(bf16[2,192,1152]{2,1,0:T(8,128)(2,1)S(1)} %dynamic-slice_bitcast_fusion.4), channel_id=1, source_target_pairs={{0,16},{16,0},{1,17},{17,1},{2,18},{18,2},{3,19},{19,3},{4,20},{20... | collective-permute-start | bytes 2654216 | tf_op jit(solution)/shard_map/ppermute | solution.py:56
  541.3 40.5 %collective-permute-start.55 = (bf16[2,192,1152]{2,1,0:T(8,128)(2,1)}, bf16[2,192,1152]{2,1,0:T(8,128)(2,1)}, u32[]{:S(2)}, u32[]{:S(2)}) collective-permute-start(bf16[2,192,1152]{2,1,0:T(8,128)(2,1)} %dynamic-slice_bitcast_fusion.5), channel_id=1, source_target_pairs={{0,16},{16,0},{1,17},{17,1},{2,18},{18,2},{3,19},{19,3},{4,20},{20... | collective-permute-start | bytes 2654216 | tf_op jit(solution)/shard_map/ppermute | solution.py:56
  542.4 98.8 %collective-permute-start.68 = (bf16[192,1152]{1,0:T(8,128)(2,1)}, bf16[192,1152]{1,0:T(8,128)(2,1)}, u32[]{:S(2)}, u32[]{:S(2)}) collective-permute-start(bf16[192,1152]{1,0:T(8,128)(2,1)} %dynamic-slice_bitcast_fusion.9), channel_id=1, source_target_pairs={{0,8},{8,0},{1,9},{9,1},{2,10},{10,2},{3,11},{11,3},{4,12},{12,4},... | collective-permute-start | bytes 1327112 | tf_op jit(solution)/shard_map/ppermute | solution.py:56
  562.4 98.8 %collective-permute-start.59 = (bf16[192,1152]{1,0:T(8,128)(2,1)}, bf16[192,1152]{1,0:T(8,128)(2,1)}, u32[]{:S(2)}, u32[]{:S(2)}) collective-permute-start(bf16[192,1152]{1,0:T(8,128)(2,1)} %dynamic-slice_bitcast_fusion.10), channel_id=1, source_target_pairs={{0,8},{8,0},{1,9},{9,1},{2,10},{10,2},{3,11},{11,3},{4,12},{12,4},... | collective-permute-start | bytes 1327112 | tf_op jit(solution)/shard_map/ppermute | solution.py:56
  568.9 37.4 %collective-permute-start.40 = (bf16[2,256,1536]{2,1,0:T(8,128)(2,1)S(1)}, bf16[2,256,1536]{2,1,0:T(8,128)(2,1)S(1)}, u32[]{:S(2)}, u32[]{:S(2)}) collective-permute-start(bf16[2,256,1536]{2,1,0:T(8,128)(2,1)S(1)} %fusion.39), channel_id=1, source_target_pairs={{0,2},{2,0},{1,3},{3,1},{4,6},{6,4},{5,7},{7,5},{8,10},{10,8},{9,1... | collective-permute-start | bytes 4718600 | tf_op jit(solution)/shard_map/ppermute | solution.py:56
  578.4 60.3 %collective-permute-start.33 = (bf16[2,256,1536]{2,1,0:T(8,128)(2,1)S(1)}, bf16[2,256,1536]{2,1,0:T(8,128)(2,1)S(1)}, u32[]{:S(2)}, u32[]{:S(2)}) collective-permute-start(bf16[2,256,1536]{2,1,0:T(8,128)(2,1)S(1)} %fusion.38), channel_id=1, source_target_pairs={{0,2},{2,0},{1,3},{3,1},{4,6},{6,4},{5,7},{7,5},{8,10},{10,8},{9,1... | collective-permute-start | bytes 4718600 | tf_op jit(solution)/shard_map/ppermute | solution.py:56
  583.3 79.1 %collective-permute-start.56 = (bf16[192,1152]{1,0:T(8,128)(2,1)S(1)}, bf16[192,1152]{1,0:T(8,128)(2,1)S(1)}, u32[]{:S(2)}, u32[]{:S(2)}) collective-permute-start(bf16[192,1152]{1,0:T(8,128)(2,1)S(1)} %dynamic-slice_bitcast_fusion.11), channel_id=1, source_target_pairs={{0,8},{8,0},{1,9},{9,1},{2,10},{10,2},{3,11},{11,3},{4,12},{12,4},... | collective-permute-start | bytes 1327112 | tf_op jit(solution)/shard_map/ppermute | solution.py:56
  683.3 37.3 %collective-permute-start.35 = (bf16[256,1536]{1,0:T(8,128)(2,1)}, bf16[256,1536]{1,0:T(8,128)(2,1)}, u32[]{:S(2)}, u32[]{:S(2)}) collective-permute-start(bf16[256,1536]{1,0:T(8,128)(2,1)} %get-tuple-element.138), channel_id=1, source_target_pairs={{0,2},{2,0},{1,3},{3,1},{4,6},{6,4},{5,7},{7,5},{8,10},{10,8},{9,1... | collective-permute-start | bytes 2359304 | tf_op jit(solution)/shard_map/ppermute | solution.py:56
  724.1 98.6 %collective-permute-start.36 = (bf16[512,1536]{1,0:T(8,128)(2,1)}, bf16[512,1536]{1,0:T(8,128)(2,1)}, u32[]{:S(2)}, u32[]{:S(2)}) collective-permute-start(bf16[512,1536]{1,0:T(8,128)(2,1)} %bitcast.105), channel_id=1, source_target_pairs={{0,1},{1,0},{2,3},{3,2},{4,5},{5,4},{6,7},{7,6},{8,9},{9,8},{10,11... | collective-permute-start | bytes 4718600 | tf_op jit(solution)/shard_map/ppermute | solution.py:56
  730.6 39.2 %collective-permute-start.45 = (bf16[2048,128]{1,0:T(8,128)(2,1)S(1)}, bf16[2048,128]{1,0:T(8,128)(2,1)S(1)}, u32[]{:S(2)}, u32[]{:S(2)}) collective-permute-start(bf16[2048,128]{1,0:T(8,128)(2,1)S(1)} %fusion.63), channel_id=1, source_target_pairs={{0,8},{8,0},{1,9},{9,1},{2,10},{10,2},{3,11},{11,3},{4,12},{12,4},... | collective-permute-start | bytes 1572872 | tf_op jit(solution)/shard_map/ppermute | solution.py:56
  757.6 43.6 %collective-permute-start.63 = (bf16[2,2,192,384]{3,2,1,0:T(8,128)(2,1)}, bf16[2,2,192,384]{3,2,1,0:T(8,128)(2,1)}, u32[]{:S(2)}, u32[]{:S(2)}) collective-permute-start(bf16[2,2,192,384]{3,2,1,0:T(8,128)(2,1)} %dynamic-slice_bitcast_fusion.8), channel_id=1, source_target_pairs={{0,4},{4,0},{1,5},{5,1},{2,6},{6,2},{3,7},{7,3},{8,12},{12,8},{9,1... | collective-permute-start | bytes 1769480 | tf_op jit(solution)/shard_map/ppermute | solution.py:56
  811.5 36.5 %collective-permute-start.47 = (bf16[512,1536]{1,0:T(8,128)(2,1)}, bf16[512,1536]{1,0:T(8,128)(2,1)}, u32[]{:S(2)}, u32[]{:S(2)}) collective-permute-start(bf16[512,1536]{1,0:T(8,128)(2,1)} %convolution_convert_fusion.4), channel_id=1, source_target_pairs={{0,1},{1,0},{2,3},{3,2},{4,5},{5,4},{6,7},{7,6},{8,9},{9,8},{10,11... | collective-permute-start | bytes 4718600 | tf_op jit(solution)/shard_map/ppermute | solution.py:56
  (142 other events, 2189.2 us)

commit v2 on v1

--- a/solution.py
+++ b/solution.py
@@ -64,81 +64,131 @@
     return jnp.where(index == 0, jnp.stack([mine, other]), jnp.stack([other, mine]))
 
 
-def place_blocks(blocks):
-    lead = tuple(blocks[0][2])
-    tail = blocks[0][0].shape
-    full = jnp.zeros(lead + tail, blocks[0][0].dtype)
-    for block, index, _ in blocks:
-        start = tuple(index) + (0,) * len(tail)
-        full = lax.dynamic_update_slice(full, block.reshape((1,) * len(lead) + tail), start)
-    return full
-
-
-def gather_wide(block):
-    hi, lo, x = (lax.axis_index(name) for name in WIDE)
+def after(value, *needed):
+    return lax.optimization_barrier((value, needed))[0]
+
+
+def wide_columns(block, cut):
+    lo = lax.axis_index("lo")
     count = lax.axis_size("hi")
-    both = pair(block, swap(block, "lo"), lo)
-    lead = (count, 2)
-    columns = [both] + [swap(both, "hi", d) for d in range(1, count)]
-    placed = []
-    for d, column in enumerate(columns):
-        other = swap(column, "x")
-        for at, part in ((x, column), (1 - x, other)):
-            placed.append((part, hi ^ d, at))
-    full = jnp.zeros((count, 2, 2) + block.shape, block.dtype)
-    for part, at_hi, at_x in placed:
-        full = lax.dynamic_update_slice(
-            full, part[None, :, None], (at_hi, 0, at_x) + (0,) * block.ndim
-        )
-    return full.reshape((count * 4,) + block.shape)
-
-
-def scatter_wide(parts):
-    hi, lo, x = (lax.axis_index(name) for name in WIDE)
-    count = lax.axis_size("hi")
-    shape = parts.shape[1:]
-    parts = parts.reshape((count, 2, 2) + shape)
+    mine = [block] + [swap(block, "hi", d) for d in range(1, count)]
+    other = [swap(part, "lo") for part in mine]
+    left = [pair(m[:, :cut], o[:, :cut], lo) for m, o in zip(mine, other)]
+    right = [pair(m[:, cut:], o[:, cut:], lo) for m, o in zip(mine, other)]
+    return left, right
+
+
+def stack_rows(blocks, slots, into=None, count=None):
+    height, width = blocks[0].shape
+    count = len(blocks) if count is None else count
+    olds = [] if into is None else [into]
+
+    def kernel(slot_ref, *refs):
+        out_ref, sem = refs[-2:]
+        copies = []
+        for i, block_ref in enumerate(refs[: len(blocks)]):
+            start = pl.multiple_of(slot_ref[i] * height, 16)
+            copies.append(
+                pltpu.make_async_copy(block_ref, out_ref.at[pl.ds(start, height), :], sem.at[i])
+            )
+        for copy in copies:
+            copy.start()
+        for copy in copies:
+            copy.wait()
+
+    anywhere = pl.BlockSpec(memory_space=pl.ANY)
+    slots = jnp.stack([jnp.asarray(slot, jnp.int32) for slot in slots])
+    return pl.pallas_call(
+        kernel,
+        in_specs=[pl.BlockSpec(memory_space=pltpu.SMEM)]
+        + [pl.BlockSpec(memory_space=pltpu.VMEM)] * len(blocks)
+        + [anywhere] * len(olds),
+        out_specs=anywhere,
+        out_shape=jax.ShapeDtypeStruct((count * height, width), blocks[0].dtype),
+        scratch_shapes=[pltpu.SemaphoreType.DMA((len(blocks),))],
+        input_output_aliases={len(blocks) + 1: 0} if olds else {},
+        name="stack_rows",
+    )(slots, *blocks, *olds)
+
+
+def assemble(columns, others, rows):
+    count = len(columns)
+    _, height, width = columns[0].shape
+    kind = columns[0].dtype
+
+    def kernel(at_ref, *refs):
+        main_ref, extra_ref = refs[-2:]
+        for d in range(count):
+            for k in range(2):
+                part = refs[2 * d + k]
+                for low_bit in range(2):
+                    index = (at_ref[0] ^ d) * 4 + low_bit * 2 + (at_ref[1] ^ k)
+                    start = pl.multiple_of(index * rows, 16)
+                    main_ref[pl.ds(start, rows), :] = part[low_bit, :rows]
+                    extra_ref[index] = part[low_bit, rows:]
+
+    parts = [part for both in zip(columns, others) for part in both]
+    at = jnp.stack([lax.axis_index("hi"), lax.axis_index("x")]).astype(jnp.int32)
+    return pl.pallas_call(
+        kernel,
+        in_specs=[pl.BlockSpec(memory_space=pltpu.SMEM)]
+        + [pl.BlockSpec(memory_space=pltpu.VMEM)] * len(parts),
+        out_specs=[pl.BlockSpec(memory_space=pltpu.VMEM)] * 2,
+        out_shape=[
+            jax.ShapeDtypeStruct((count * 4 * rows, width), kind),
+            jax.ShapeDtypeStruct((count * 4, height - rows, width), kind),
+        ],
+        name="assemble",
+    )(at, *parts)
+
+
+def send_x(parts):
+    x = lax.axis_index("x")
+    parts = parts.reshape((-1, 2, 2) + parts.shape[1:])
     kept = lax.dynamic_index_in_dim(parts, x, axis=2, keepdims=False)
     sent = lax.dynamic_index_in_dim(parts, 1 - x, axis=2, keepdims=False)
-    parts = low(wide_float(kept) + wide_float(swap(sent, "x")))
-    total = wide_float(pick(parts, hi))
-    for d in range(1, count):
-        total = total + wide_float(swap(pick(parts, hi ^ d), "hi", d))
-    kept, sent = pick(total, lo), low(pick(total, 1 - lo))
-    return kept + wide_float(swap(sent, "lo"))
-
-
-def gather_hidden(shard):
-    hi, lo, x = (lax.axis_index(name) for name in WIDE)
-    count = lax.axis_size("hi")
-    rows, half = shard.shape[0], shard.shape[1] // 2
-    mine = lax.dynamic_slice_in_dim(shard, lo * half, half, axis=1)
-    sent = lax.dynamic_slice_in_dim(shard, (1 - lo) * half, half, axis=1)
-    both = pair(mine, swap(sent, "lo"), lo)
-    columns = [both] + [swap(both, "hi", d) for d in range(1, count)]
-    full = jnp.zeros((count, 2, 2, rows, half), shard.dtype)
-    for d, column in enumerate(columns):
-        for at_x, part in ((x, column), (1 - x, swap(column, "x"))):
-            full = lax.dynamic_update_slice(full, part[None, :, None], (hi ^ d, 0, at_x, 0, 0))
-    return full.reshape(count * 4 * rows, half)
-
-
-def scatter_hidden(grad):
-    hi, lo, x = (lax.axis_index(name) for name in WIDE)
-    count = lax.axis_size("hi")
-    rows, half = grad.shape[0] // (count * 4), grad.shape[1]
-    parts = grad.reshape(count, 2, 2, rows, half)
-    kept = lax.dynamic_index_in_dim(parts, x, axis=2, keepdims=False)
-    sent = lax.dynamic_index_in_dim(parts, 1 - x, axis=2, keepdims=False)
-    parts = low(wide_float(kept) + wide_float(swap(sent, "x")))
-    total = wide_float(pick(parts, hi))
-    for d in range(1, count):
-        total = total + wide_float(swap(pick(parts, hi ^ d), "hi", d))
-    total = low(total)
-    mine, other = pick(total, lo), swap(pick(total, 1 - lo), "lo")
-    first = jnp.where(lo == 0, mine, other)
-    second = jnp.where(lo == 0, other, mine)
+    return kept, swap(sent, "x")
+
+
+def send_hi(parts):
+    hi = lax.axis_index("hi")
+    turns = range(1, lax.axis_size("hi"))
+    return [pick(parts, hi)] + [swap(pick(parts, hi ^ d), "hi", d) for d in turns]
+
+
+def send_lo(parts):
+    lo = lax.axis_index("lo")
+    return pick(parts, lo), swap(low(pick(parts, 1 - lo)), "lo")
+
+
+def add_up(parts):
+    return sum(wide_float(part) for part in parts)
+
+
+def send_hidden(total):
+    x = lax.axis_index("x")
+    total = total.reshape((2, -1) + total.shape[1:])
+    return pick(total, x), swap(pick(total, 1 - x), "x")
+
+
+def join_hidden(mine, other):
+    x = lax.axis_index("x")
+    first = jnp.where(x == 0, mine, other)
+    second = jnp.where(x == 0, other, mine)
     return wide_float(jnp.concatenate([first, second], axis=1))
+
+
+def hidden_pair(shards):
+    x = lax.axis_index("x")
+    half = shards[0].shape[1] // 2
+
+    def part(at):
+        return jnp.concatenate(
+            [lax.dynamic_slice_in_dim(shard, at * half, half, axis=1) for shard in shards], axis=1
+        )
+
+    both = pair(part(x), swap(part(1 - x), "x"), x)
+    return both.reshape((-1,) + both.shape[2:])
 
 
 def exchange_narrow(blocks):
@@ -151,28 +201,21 @@
     return pair(near, far, y)
 
 
-def gather_tokens(block):
+def gather_tokens(block, *needed):
     y, c = (lax.axis_index(name) for name in NARROW)
-    both = pair(block, swap(block, "y"), y)
-    both = both.reshape((-1,) + block.shape[1:])
-    every = pair(both, swap(both, "c"), c)
-    return every.reshape((-1,) + block.shape[1:])
+    by_y = after(swap(block, "y"), *needed)
+    own = c * 2 + y
+    return stack_rows(
+        [block, by_y, swap(block, "c"), swap(by_y, "c")], [own, own ^ 1, own ^ 2, own ^ 3]
+    )
 
 
 def rotation(positions):
     half = HD // 2
     freqs = rope_base ** (-2.0 * jnp.arange(half, dtype=jnp.float32) / HD)
     angles = positions.astype(jnp.float32)[:, None] * freqs[None, :]
-    return jnp.cos(angles)[:, None, :], jnp.sin(angles)[:, None, :]
-
-
-def rotate(values, cosine, sine):
-    half = values.shape[-1] // 2
-    first = values[..., :half]
-    second = values[..., half:]
-    return jnp.concatenate(
-        [first * cosine - second * sine, second * cosine + first * sine], axis=-1
-    )
+    cosine, sine = jnp.cos(angles), jnp.sin(angles)
+    return jnp.concatenate([cosine, cosine], axis=1), jnp.concatenate([-sine, sine], axis=1)
 
 
 def rms_back(grad_unit, unit, inverse):
@@ -187,6 +230,87 @@
     if decay:
         update = update + decay_rate * master
     return (grad, update)
+
+
+def project(layer_input, weight, bias, cosine, sine, kv_cosine, kv_sine, heads):
+    tokens = layer_input.shape[0]
+    width = weight.shape[1]
+    block = 256
+    scale = HD ** (-0.5)
+
+    def kernel(x_ref, w_ref, b_ref, c_ref, s_ref, kc_ref, ks_ref, a_ref, q_ref, kv_ref):
+        x = wide_float(x_ref[...])
+        inverse = lax.rsqrt(jnp.mean(x * x, axis=1, keepdims=True) + norm_eps)
+        normed = low(x * inverse)
+        a_ref[...] = normed
+        linear = matmul(normed, w_ref[...]) + b_ref[...]
+        for h in range(heads + 1):
+            part = linear[:, h * HD : (h + 1) * HD]
+            turned = pltpu.roll(part, HD // 2, axis=1)
+            if h < heads:
+                out = (part * c_ref[...] + turned * s_ref[...]) * scale
+                q_ref[:, h * HD : (h + 1) * HD] = low(out)
+            else:
+                kv_ref[...] = low(part * kc_ref[...] + turned * ks_ref[...])
+
+    def by_tokens(columns):
+        return pl.BlockSpec((block, columns), lambda i: (i, 0))
+
+    def whole(a):
+        return pl.BlockSpec(a.shape, lambda i: (0, 0))
+
+    return pl.pallas_call(
+        kernel,
+        grid=(tokens // block,),
+        in_specs=[by_tokens(D), whole(weight), whole(bias)] + [by_tokens(HD)] * 4,
+        out_specs=[by_tokens(D), by_tokens(heads * HD), by_tokens(HD)],
+        out_shape=[
+            jax.ShapeDtypeStruct((tokens, D), jnp.bfloat16),
+            jax.ShapeDtypeStruct((tokens, heads * HD), jnp.bfloat16),
+            jax.ShapeDtypeStruct((tokens, HD), jnp.bfloat16),
+        ],
+        name="project",
+    )(layer_input, weight, bias, cosine, sine, kv_cosine, kv_sine)
+
+
+def feed_forward(tokens_in, grads_in, w_gateup, half, at, count, into=None):
+    tokens = tokens_in.shape[0]
+    block = 512
+    olds = [] if into is None else list(into)
+    skip = at // block
+
+    def kernel(b_ref, g_ref, wgu_ref, *refs):
+        hid_ref, dgu_ref = refs[-2:]
+        both = matmul(b_ref[...], wgu_ref[...])
+        gate, upward = both[:, :half], both[:, half:]
+        grad = wide_float(g_ref[...])
+        logistic = jax.nn.sigmoid(gate)
+        active = gate * logistic
+        hid_ref[...] = low(active * upward)
+        slope = logistic + active * (1.0 - logistic)
+        dgu_ref[:, :half] = low(grad * upward * slope)
+        dgu_ref[:, half:] = low(grad * active)
+
+    def by_tokens(columns):
+        return pl.BlockSpec((block, columns), lambda i: (i + skip, 0))
+
+    return pl.pallas_call(
+        kernel,
+        grid=(count // block,),
+        in_specs=[
+            by_tokens(D),
+            by_tokens(half),
+            pl.BlockSpec(w_gateup.shape, lambda i: (0, 0), pipeline_mode=pl.Buffered(1)),
+        ]
+        + [pl.BlockSpec(memory_space=pl.ANY)] * len(olds),
+        out_specs=[by_tokens(half), by_tokens(2 * half)],
+        out_shape=[
+            jax.ShapeDtypeStruct((tokens, half), jnp.bfloat16),
+            jax.ShapeDtypeStruct((tokens, 2 * half), jnp.bfloat16),
+        ],
+        input_output_aliases={3: 0, 4: 1} if olds else {},
+        name="feed_forward",
+    )(tokens_in, grads_in, w_gateup, *olds)
 
 
 def stacked_heads(ref, heads):
@@ -258,7 +382,9 @@
     )(starts, place, queries, keys, values, begins)
 
 
-def attention_backward(queries, keys, values, begins, starts, place, grads, lse, outputs):
+def attention_backward(
+    queries, keys, values, begins, starts, place, grads, lse, outputs, cosine, sine
+):
     tokens, columns = queries.shape
     heads = columns // HD
     length = keys.shape[0]
@@ -266,7 +392,7 @@
 
     def kernel(
         starts_ref, place_ref, q_ref, k_ref, v_ref, begin_ref, g_ref, lse_ref, o_ref,
-        dq_ref, dk_ref, dv_ref,
+        c_ref, s_ref, dq_ref, dk_ref, dv_ref,
     ):
         step = pl.program_id(0)
 
@@ -301,7 +427,10 @@
         last = (base + BLOCK_Q - 1) // BLOCK_K
         dq = lax.fori_loop(first, last + 1, body, jnp.zeros((rows, HD), jnp.float32))
         for h in range(heads):
-            dq_ref[:, h * HD : (h + 1) * HD] = dq[h * BLOCK_Q : (h + 1) * BLOCK_Q]
+            part = dq[h * BLOCK_Q : (h + 1) * BLOCK_Q]
+            turned = pltpu.roll(part, HD // 2, axis=1)
+            part = (part * c_ref[...] - turned * s_ref[...]) * HD ** (-0.5)
+            dq_ref[:, h * HD : (h + 1) * HD] = low(part)
 
     block = pl.BlockSpec((BLOCK_Q, columns), lambda i, *_: (i, 0))
     whole = pl.BlockSpec((length, HD), lambda i, *_: (0, 0))
@@ -318,17 +447,19 @@
                 block,
                 pl.BlockSpec((heads, BLOCK_Q, 1), lambda i, *_: (0, i, 0)),
                 block,
+                pl.BlockSpec((BLOCK_Q, HD), lambda i, *_: (i, 0)),
+                pl.BlockSpec((BLOCK_Q, HD), lambda i, *_: (i, 0)),
             ],
             out_specs=[block, whole, whole],
         ),
         out_shape=[
-            jax.ShapeDtypeStruct((tokens, columns), jnp.float32),
+            jax.ShapeDtypeStruct((tokens, columns), jnp.bfloat16),
             jax.ShapeDtypeStruct((length, HD), jnp.float32),
             jax.ShapeDtypeStruct((length, HD), jnp.float32),
         ],
         compiler_params=pltpu.CompilerParams(dimension_semantics=("arbitrary",)),
         name="attention_backward",
-    )(starts, place, queries, keys, values, begins, grads, lse, outputs)
+    )(starts, place, queries, keys, values, begins, grads, lse, outputs, cosine, sine)
 
 
 def local(
@@ -366,7 +497,6 @@
     tokens = layer_input.shape[0]
     quarter = tokens // 4
     heads = query_bias.shape[0]
-    head_scale = HD ** (-0.5)
     token_count = float(tokens * wide)
     rows = D // wide
     narrow_rows = rows // 4
@@ -387,41 +517,45 @@
     blocks = exchange_narrow(blocks).reshape(4, narrow_rows + 16, HD)
     kv_mine = blocks[:, :narrow_rows].reshape(rows, HD)
     small_row = blocks[:, narrow_rows].reshape(1, 4 * HD)
+    row_gains = wide_float(blocks[:, narrow_rows, : 2 * narrow_rows])
+    row_gains = jnp.transpose(row_gains.reshape(4, 2, narrow_rows), (1, 0, 2)).reshape(2, rows, 1)
     bias_row = jnp.pad(low(query_bias).reshape(1, -1), ((0, 0), (0, 4 * HD - heads * bias_part)))
     extra = jnp.pad(jnp.concatenate([small_row, bias_row]), ((0, 14), (0, 0)))
-    packed = jnp.concatenate(
-        [jnp.concatenate([low(query_weight), kv_mine], axis=1), extra], axis=0
-    )
-    packed = gather_wide(packed)
-    w_qkv = packed[:, :rows].reshape(D, 4 * HD)
-    small_all = wide_float(packed[:, rows]).reshape(wide, 4, HD)
+    my_qkv = wide_float(jnp.concatenate([low(query_weight), kv_mine], axis=1))
+    packed = jnp.concatenate([low(my_qkv * row_gains[0]), extra], axis=0)
+    side = jnp.pad(low(output_weight).T, ((0, 16), (0, 0)))
+    packed = jnp.concatenate([packed, side], axis=1)
+    columns, out_columns = wide_columns(packed, 4 * HD)
+    others = [swap(column, "x") for column in columns]
+    out_others = [swap(column, "x") for column in after(out_columns, others)]
+    w_qkv, small_all = assemble(columns, others, rows)
+    small_all = wide_float(small_all)
+    b_query = small_all[:, 1, : heads * bias_part].reshape(wide, heads, bias_part)
+    small_all = small_all[:, 0].reshape(wide, 4, HD)
     gains = small_all[:, :, : 2 * narrow_rows].reshape(wide, 4, 2, narrow_rows)
     gains = jnp.transpose(gains, (2, 0, 1, 3)).reshape(2, D)
     b_kv = small_all[:, :, 2 * narrow_rows : 2 * narrow_rows + kv_part].reshape(2 * KV, HD)
-    b_query = wide_float(packed[:, rows + 1, : heads * bias_part]).reshape(wide, heads, bias_part)
     b_query = jnp.transpose(b_query, (1, 0, 2)).reshape(heads * HD)
     b_qkv = jnp.concatenate([b_query, pick(b_kv, column_block)])
-    gain_one, gain_two = gains[0], gains[1]
-
-    w_output = gather_wide(low(output_weight).T)
-    w_output = w_output.reshape(D, heads * HD)
+    gain_two = gains[1]
 
     def padded(shard):
         return jnp.pad(low(shard), ((0, 0), (0, padding)))
 
-    w_gate = gather_hidden(padded(gateup_weight[:, 0]))
-    w_up = gather_hidden(padded(gateup_weight[:, 1]))
-    w_down = gather_hidden(padded(down_weight.T))
-
-    input_float = wide_float(layer_input)
-    inverse_one = lax.rsqrt(jnp.mean(input_float * input_float, axis=-1, keepdims=True) + norm_eps)
-    normed_one = low(input_float * inverse_one * gain_one)
-    linear = (matmul(normed_one, w_qkv) + b_qkv).reshape(tokens, 4, HD)
+    down_shard = hidden_pair([padded(down_weight.T)])
+    w_down = lax.all_gather(after(down_shard, columns), ("hi", "lo"), axis=0, tiled=True)
+    gateup_shard = hidden_pair(
+        after([padded(gateup_weight[:, 0]), padded(gateup_weight[:, 1])], packed)
+    )
+    w_gateup = lax.all_gather(gateup_shard, ("hi", "lo"), axis=0, tiled=True)
+
     cosine, sine = rotation(positions)
     kv_cosine = jnp.where(c == 0, cosine, 1.0)
     kv_sine = jnp.where(c == 0, sine, 0.0)
-    queries = low(rotate(linear[:, :heads], cosine, sine) * head_scale).reshape(tokens, heads * HD)
-    kv_own = low(rotate(linear[:, heads:], kv_cosine, kv_sine)).reshape(tokens, HD)
+    normed_one, queries, kv_own = project(
+        layer_input, w_qkv, b_qkv[None], cosine, sine, kv_cosine, kv_sine, heads
+    )
+    kv_own = after(kv_own, gateup_shard)
     both = pair(kv_own, swap(kv_own, "x"), x)
     kv_row = pair(both, swap(both, "lo"), lo).reshape(4 * tokens, HD)
     kv_other = swap(kv_row, "c")
@@ -431,128 +565,190 @@
     starts = begins[::BLOCK_Q]
     begins = begins[:, None]
     place = (lo * 2 + x).reshape(1).astype(jnp.int32)
+    grad_blocks = grad_out.reshape(4, quarter, D)
+    grad_near = [pick(grad_blocks, own ^ d) for d in range(4)]
+    grad_far = [swap(part, "x") for part in after(grad_near[:2], kv_row)]
     attention, log_total = attention_forward(queries, keys, values, begins, starts, place)
+    w_output, _ = assemble(*after((out_columns, out_others), attention), rows)
+    grad_far = after(grad_far, attention)
+    ff_grad = stack_rows(grad_near + grad_far + [swap(part, "c") for part in grad_far], range(8))
     attention_low = low(attention)
 
     def halves(block):
         split = block.reshape(2, -1, block.shape[-1])
         return pick(split, c), pick(split, 1 - c)
 
-    def scatter_narrow(kept, sent):
-        total = (kept + wide_float(swap(low(sent), "c"))).reshape(2, quarter, D)
-        return pick(total, y) + wide_float(swap(low(pick(total, 1 - y)), "y"))
+    def send_core(kept, sent):
+        return (kept + wide_float(swap(low(sent), "c"))).reshape(2, quarter, D)
+
+    def send_y(total):
+        return pick(total, y), swap(low(pick(total, 1 - y)), "y")
 
     attention_kept, attention_sent = halves(attention_low)
     sent = matmul_nt(attention_sent, w_output)
-    attention_out = scatter_narrow(matmul_nt(attention_kept, w_output), sent)
-    residual = wide_float(pick(layer_input.reshape(4, quarter, D), own)) + attention_out
+    out_total = send_core(matmul_nt(attention_kept, w_output), sent)
+    out_parts = send_y(out_total)
+
+    grad_hidden = low(matmul(after(ff_grad, out_total), w_down))
+    out_parts = after(out_parts, grad_hidden)
+    residual = wide_float(pick(layer_input.reshape(4, quarter, D), own)) + add_up(out_parts)
     inverse_two = lax.rsqrt(jnp.mean(residual * residual, axis=-1, keepdims=True) + norm_eps)
     unit_two = residual * inverse_two
     normed_two = low(unit_two * gain_two)
 
     by_y = swap(normed_two, "y")
-    by_lo = swap(normed_two, "lo")
-    by_both = swap(by_y, "lo")
-    core_tokens = jnp.concatenate([normed_two, by_y, by_lo, by_both])
-    ff_input = jnp.concatenate([core_tokens, swap(core_tokens, "c")])
-    grad_blocks = grad_out.reshape(4, quarter, D)
-    grad_own = pick(grad_blocks, own)
-    grad_near = jnp.concatenate([grad_own, pick(grad_blocks, c * 2 + 1 - y)])
-    grad_far = swap(grad_near, "lo")
-    grad_core = jnp.concatenate(
-        [pick(grad_blocks, (1 - c) * 2 + y), pick(grad_blocks, (1 - c) * 2 + 1 - y)]
-    )
-    ff_grad = jnp.concatenate([grad_near, grad_far, grad_core, swap(grad_far, "c")])
-
-    gate = matmul(ff_input, w_gate)
-    upward = matmul(ff_input, w_up)
-    grad_hidden = matmul(ff_grad, w_down)
-    logistic = jax.nn.sigmoid(gate)
-    active = gate * logistic
-    hidden_low = low(active * upward)
-    grad_gate = low(grad_hidden * upward * logistic * (1.0 + gate * (1.0 - logistic)))
-    grad_upward = low(grad_hidden * active)
-
-    def scatter_group(kept, sent):
-        total = kept + wide_float(swap(low(sent), "c"))
-        total = total.reshape(2, 2, quarter, D)
-        total = total[:, 0] + wide_float(swap(low(total[:, 1]), "y"))
-        return total[0] + wide_float(swap(low(total[1]), "lo"))
-
+    by_x = swap(normed_two, "x")
+    by_both = [swap(by_y[:, : D // 2], "x"), swap(by_x[:, D // 2 :], "y")]
     count = 4 * quarter
-
-    def feed_back(at):
-        part = slice(at * count, (at + 1) * count)
-        return matmul_nt(grad_gate[part], w_gate) + matmul_nt(grad_upward[part], w_up)
-
-    grad_sent = feed_back(1)
-    grad_normed_two = scatter_group(feed_back(0), grad_sent)
-    grad_residual = wide_float(grad_own) + rms_back(
+    ff_input = stack_rows(
+        [normed_two, by_y, swap(normed_two, "c"), swap(by_y, "c")], range(4), count=8
+    )
+    firsts = feed_forward(ff_input, grad_hidden, w_gateup, half, 0, count)
+    by_x, by_both = after((by_x, by_both), firsts[0])
+    by_both = jnp.concatenate(by_both, axis=1)
+    ff_input = stack_rows(
+        [by_x, by_both, swap(by_x, "c"), swap(by_both, "c")], range(4, 8), into=ff_input, count=8
+    )
+    hidden_all, both_all = feed_forward(
+        ff_input, grad_hidden, w_gateup, half, count, count, into=firsts
+    )
+
+    half_d = D // 2
+
+    def join_core(sums):
+        return wide_float(sums[: 2 * quarter]) + wide_float(swap(sums[2 * quarter :], "c"))
+
+    def first_sends(far_sums, near_sums):
+        to_x = low(far_sums[:, :half_d])
+        to_y = low(jnp.concatenate([near_sums[quarter:, half_d:], far_sums[quarter:, half_d:]]))
+        return to_x, to_y
+
+    def second_sends(far_sums, near_sums, from_x, from_y):
+        left = near_sums[:, :half_d] + wide_float(from_x)
+        right = near_sums[:quarter, half_d:] + wide_float(from_y[:quarter])
+        to_x = low(far_sums[:quarter, half_d:] + wide_float(from_y[quarter:]))
+        return (left[:quarter], right), (low(left[quarter:]), to_x)
+
+    def finish_sums(kept, from_y, from_x):
+        return jnp.concatenate([kept[0] + wide_float(from_y), kept[1] + wide_float(from_x)], axis=1)
+
+    feed_far = low(matmul_nt(both_all[count:], w_gateup))
+    feed_near = low(matmul_nt(after(both_all, feed_far)[:count], w_gateup))
+
+    def over_rows(grad):
+        return lax.psum_scatter(grad, ("hi", "lo"), scatter_dimension=0, tiled=True)
+
+    far_sums, near_sums = join_core(feed_far), join_core(feed_near)
+    to_x, to_y = first_sends(far_sums, near_sums)
+    from_x, from_y = swap(to_x, "x"), swap(to_y, "y")
+    ff_late, both_late = after((ff_input, both_all), to_x, to_y)
+    grad_gateup = low(matmul_tn(ff_late, both_late))
+    from_x, from_y = after((from_x, from_y), grad_gateup)
+    kept, (to_y, to_x) = second_sends(far_sums, near_sums, from_x, from_y)
+    from_x, from_y = swap(to_x, "x"), swap(to_y, "y")
+    ff_late, hidden_all = after((ff_grad, hidden_all), to_x, to_y)
+    grad_down = low(matmul_tn(ff_late, hidden_all))
+    from_x, from_y = after((from_x, from_y), grad_down)
+    rows_gateup, rows_down = over_rows(grad_gateup), over_rows(grad_down)
+    grad_normed_two = finish_sums(kept, from_y, from_x)
+    grad_residual = wide_float(grad_near[0]) + rms_back(
         grad_normed_two * gain_two, unit_two, inverse_two
     )
-    residual_low = gather_tokens(low(grad_residual))
-
-    mlp_sent = matmul_nt(hidden_low[count:], w_down)
-    mlp_out = scatter_group(matmul_nt(hidden_low[:count], w_down), mlp_sent)
-    layer_output = gather_tokens(low(residual + mlp_out))
-
-    summed_down = scatter_hidden(low(matmul_tn(ff_grad, hidden_low)))
-    summed_gate = scatter_hidden(low(matmul_tn(ff_input, grad_gate)))
-    summed_up = scatter_hidden(low(matmul_tn(ff_input, grad_upward)))
+
+    residual_own = low(grad_residual)
+    hidden_all = after(hidden_all, residual_own)
+    mlp_far = low(matmul_nt(hidden_all[count:], w_down))
+    mlp_near = low(matmul_nt(after(hidden_all, mlp_far)[:count], w_down))
+    residual_low = gather_tokens(residual_own, mlp_near)
 
     grad_attention = low(matmul(residual_low, w_output))
-    summed_output = scatter_wide(
-        low(matmul_tn(residual_low, attention_low)).reshape(wide, rows, heads * HD)
-    )
+    rows_output = over_rows(low(matmul_tn(residual_low, attention_low)))
+    mlp_far, mlp_near = after((mlp_far, mlp_near), residual_low)
+    mlp_far, mlp_near = join_core(mlp_far), join_core(mlp_near)
+    to_x, to_y = first_sends(mlp_far, mlp_near)
+    from_x, from_y = swap(to_x, "x"), swap(to_y, "y")
+    grad_attention = after(grad_attention, to_x, to_y)
     grad_queries, grad_keys, grad_values = attention_backward(
-        queries, keys, values, begins, starts, place, grad_attention, log_total, attention
+        queries, keys, values, begins, starts, place, grad_attention, log_total, attention,
+        cosine, sine,
     )
     kv_sent = low(jnp.where(c == 0, grad_values, grad_keys))
     kv_grad = jnp.where(c == 0, grad_keys, grad_values) + wide_float(swap(kv_sent, "c"))
     kv_grad = kv_grad.reshape(2, 2 * tokens, HD)
     kv_grad = pick(kv_grad, lo) + wide_float(swap(low(pick(kv_grad, 1 - lo)), "lo"))
     kv_grad = kv_grad.reshape(2, tokens, HD)
+    kv_grad = after(kv_grad, rows_gateup)
+    from_x, from_y = after((from_x, from_y), kv_grad)
+    mlp_kept, (to_y, to_x) = second_sends(mlp_far, mlp_near, from_x, from_y)
+    from_x, from_y = swap(to_x, "x"), swap(to_y, "y")
     kv_grad = pick(kv_grad, x) + wide_float(swap(low(pick(kv_grad, 1 - x)), "x"))
-    kv_grad = rotate(kv_grad[:, None], kv_cosine, -kv_sine)
-    query_grad = rotate(
-        grad_queries.reshape(tokens, heads, HD) * head_scale, cosine, -sine
-    )
-    grad_linear = low(jnp.concatenate([query_grad, kv_grad], axis=1)).reshape(tokens, 4 * HD)
-
-    linear_kept, linear_sent = halves(grad_linear)
-    part_sent = matmul_nt(linear_sent, w_qkv)
-    grad_normed_one = scatter_narrow(matmul_nt(linear_kept, w_qkv), part_sent)
+    turned = jnp.concatenate([kv_grad[:, HD // 2 :], kv_grad[:, : HD // 2]], axis=1)
+    grad_kv = low(kv_grad * kv_cosine - turned * kv_sine)
+
+    w_query, w_kv = w_qkv[:, : heads * HD], w_qkv[:, heads * HD :]
+
+    def input_part(kv_part_grad, query_part_grad):
+        return matmul_nt(query_part_grad, w_query) + matmul_nt(kv_part_grad, w_kv)
+
+    query_kept, query_sent = halves(grad_queries)
+    kv_kept, kv_sent = halves(grad_kv)
+    part_sent = low(input_part(kv_sent, query_sent))
+    part_kept = input_part(kv_kept, query_kept)
+    part_total = send_core(part_kept, part_sent)
+    part_parts = after(send_y(part_total), rows_down)
+    rows_gateup, rows_down = after((rows_gateup, rows_down), grad_kv)
+    parts_gateup = send_hidden(rows_gateup)
+    parts_down = send_hidden(rows_down)
+    parts_output = send_hidden(after(rows_output, part_total))
+    from_x, from_y = after((from_x, from_y), part_total)
+    layer_output = gather_tokens(low(residual + finish_sums(mlp_kept, from_y, from_x)))
+    grad_normed_one = add_up(part_parts)
     own_input = wide_float(pick(layer_input.reshape(4, quarter, D), own))
     own_inverse = lax.rsqrt(jnp.mean(own_input * own_input, axis=-1, keepdims=True) + norm_eps)
     input_grad = gather_tokens(
         low(
             grad_residual
-            + rms_back(grad_normed_one * gain_one, own_input * own_inverse, own_inverse)
+            + rms_back(grad_normed_one, own_input * own_inverse, own_inverse)
         )
     )
 
-    grad_qkv = low(matmul_tn(normed_one, grad_linear)).reshape(wide, rows, 4 * HD)
-    bias_sums = jnp.sum(wide_float(grad_linear), axis=0).reshape(4, HD)
-    bias_query = jnp.transpose(bias_sums[:heads].reshape(heads, wide, bias_part), (1, 0, 2))
-    bias_query = bias_query.reshape(wide, heads * bias_part)
+    sums_query = low(matmul_tn(normed_one, grad_queries)).reshape(wide, rows, heads * HD)
+    hi_query = send_hi(low(add_up(after(send_x(sums_query), part_total))))
+    lo_query = send_lo(add_up(after(hi_query, part_total)))
+    grad_kv_weight = low(matmul_tn(normed_one, grad_kv)).reshape(wide, rows, HD)
+    bias_query = jnp.sum(wide_float(grad_queries), axis=0).reshape(heads, wide, bias_part)
+    bias_query = jnp.transpose(bias_query, (1, 0, 2)).reshape(wide, heads * bias_part)
     bias_kv = lax.dynamic_update_slice(
-        jnp.zeros((2 * KV, HD), jnp.float32), bias_sums[heads:], (column_block, 0)
+        jnp.zeros((2 * KV, HD), jnp.float32),
+        jnp.sum(wide_float(grad_kv), axis=0, keepdims=True),
+        (column_block, 0),
     ).reshape(wide, 4 * kv_part)
     bias_all = jnp.concatenate([bias_query, bias_kv], axis=1)
-    bias_all = jnp.pad(bias_all, ((0, 0), (0, 4 * HD - bias_all.shape[1])))
+    bias_all = jnp.pad(bias_all, ((0, 0), (0, HD - bias_all.shape[1])))
     extra = jnp.pad(low(bias_all)[:, None], ((0, 0), (0, 15), (0, 0)))
-    summed = scatter_wide(jnp.concatenate([grad_qkv, extra], axis=1))
-    summed_query = summed[:rows, : heads * HD]
-    summed_kv = summed[:rows, heads * HD :]
+    x_kv = send_x(jnp.concatenate([grad_kv_weight, extra], axis=1))
+    hi_kv = send_hi(low(add_up(after(x_kv, part_total))))
+    summed = add_up(send_lo(add_up(hi_kv)))
+    parts_down, parts_gateup = after((parts_down, parts_gateup), part_total)
+    summed_down = join_hidden(*parts_down)
+    summed_gate = join_hidden(*(part[:, :half] for part in parts_gateup))
+    summed_up = join_hidden(*(part[:, half:] for part in parts_gateup))
+    summed_output = add_up(
+        after(parts_output, part_total)
+    )
+    summed_query = add_up(lo_query)
+    summed_kv = summed[:rows]
     summed_query_bias = summed[rows, : heads * bias_part].reshape(heads, bias_part)
     kv_bias = summed[rows, heads * bias_part : heads * bias_part + 4 * kv_part]
 
-    my_gains = lax.dynamic_slice_in_dim(gains, (hi * 4 + lo * 2 + x) * rows, rows, axis=1)
-    my_w = wide_float(lax.dynamic_slice_in_dim(w_qkv, (hi * 4 + lo * 2 + x) * rows, rows, axis=0))
-    grad_gain_one = jnp.sum(summed[:rows] * my_w, axis=1) / my_gains[0]
+    grad_gain_one = jnp.sum(
+        summed_query * my_qkv[:, : heads * HD], axis=1
+    ) + jnp.sum(summed_kv * my_qkv[:, heads * HD :], axis=1)
+    summed_query = summed_query * row_gains[0]
+    summed_kv = summed_kv * row_gains[0]
     summed_gateup = jnp.stack([summed_gate[:, :hidden], summed_up[:, :hidden]], axis=1)
     grad_gain_two = (
-        jnp.sum(summed_gateup * wide_float(low(gateup_weight)), axis=(1, 2)) / my_gains[1]
+        jnp.sum(summed_gateup * wide_float(low(gateup_weight)), axis=(1, 2)) / row_gains[1, :, 0]
     )
     gain_parts = jnp.stack([grad_gain_one, grad_gain_two]).reshape(2, 4, narrow_rows)
     gain_parts = jnp.transpose(gain_parts, (1, 0, 2)).reshape(4, 2 * narrow_rows)

time: 917 us -> 695 us (0.76)
  waiting for transfers between devices: 396 us -> 244 us
  Pallas kernels: 26.4 us -> 90.9 us
  matrix products: 142 us -> 101 us
  starting transfers between devices: 129 us -> 90.5 us
  other arithmetic: 114 us -> 79.2 us
  local copies, waits for them, and re-layouts: 95.6 us -> 66.2 us
  between operations: 3.25 us -> 16 us
    ppermute x69 -> x67, waiting for transfers between devices: 396 us -> 237 us  [swap(): return lax.ppermute(block, axis, [(i, i ^ distance) for i in range(size)])]
    pallas_call x0 -> x11, Pallas kernels: none -> 64 us  [the longest x2 28 us: feed_forward(): pl.pallas_call(kernel, grid=(count // block,), in_specs=[by_tokens(D), by...]
    ppermute x69 -> x67, starting transfers between devices: 129 us -> 90.3 us  [swap(): return lax.ppermute(block, axis, [(i, i ^ distance) for i in range(size)])]
    dot_general x5 -> x2, matrix products: 48.7 us -> 15.5 us  [matmul(): return jnp.dot(left, right, preferred_element_type=jnp.float32)]
    select_n x20 -> x15, other arithmetic: 24.6 us -> 6.3 us  [pair(): jnp.where(index == 0, jnp.stack([mine, other]), jnp.stack([other, mine]))]
    dynamic_update_slice x16 -> x1, local copies, waits for them, and re-layouts: 16.8 us -> 0.04 us  [local(): lax.dynamic_update_slice(jnp.zeros((2 * KV, HD), jnp.float32), jnp.sum(wi...]
    convert_element_type x19 -> x17, other arithmetic: 21.8 us -> 18 us  [low(): return a.astype(jnp.bfloat16)]
    unnamed x225 -> x227, local copies, waits for them, and re-layouts: 31.3 us -> 32.2 us
  transfers between devices with their start and end apart: 69 -> 72, of which waited for: 30 -> 30; matrix products, arithmetic and copies ran while one was open for 26% -> 28% of each run, Pallas kernels for 3% -> 10%
where the time goes in v2:
time: 695 us; the launch traced here: 687 us
  waiting for transfers between devices  244 us (35%)
  matrix products  101 us (15%)
  Pallas kernels  90.9 us (13%)
  starting transfers between devices  90.5 us (13%)
  other arithmetic  79.2 us (11%)
  local copies, waits for them, and re-layouts  66.2 us (10%)
  between operations  16 us (2%)
    ppermute x67, waiting for transfers between devices, swap(): return lax.ppermute(block, axis, [(i, i ^ distance) for i in range(size)])  237 us
    ppermute x67, starting transfers between devices, swap(): return lax.ppermute(block, axis, [(i, i ^ distance) for i in range(size)])  90.3 us
    dot_general x10, matrix products, matmul_nt(): lax.dot_general(left, right, (((1,), (1,)), ((), ())), preferred_element_...  46.3 us
    dot_general x5, matrix products, matmul_tn(): lax.dot_general(left, right, (((0,), (0,)), ((), ())), preferred_element_...  39 us
    unnamed x227, local copies, waits for them, and re-layouts  32.2 us
    pallas_call x2, Pallas kernels, feed_forward(): pl.pallas_call(kernel, grid=(count // block,), in_specs=[by_tokens(D), by...  28 us
    pallas_call x6, Pallas kernels, stack_rows(): pl.pallas_call(kernel, in_specs=[pl.BlockSpec(memory_space=pltpu.SMEM)] +...  23.5 us
    convert_element_type x17, other arithmetic, low(): return a.astype(jnp.bfloat16)  18 us
  transfers between devices with their start and end apart: 72, of which 30 were waited for; matrix products, arithmetic and copies ran while one was open for 28% of the time, Pallas kernels for 10%

profile of v2, /device:TPU:0, one launch (start us, length us, event | category | flops | bytes accessed | tf_op | source)
XLA Modules:
  0.0 687.0 jit_solution(3533591298798707191)
XLA Ops:
  23.9 12.8 %collective-permute-done.5 = bf16[208,896]{1,0:T(8,128)(2,1)} collective-permute-done((bf16[208,896]{1,0:T(8,128)(2,1)S(1)}, bf16[208,896]{1,0:T(8,128)(2,1)}, u32[]{:S(2)}, u32[]{:S(2)}) %collective-permute-start.5) | collective-permute-done | bytes 372768 | tf_op jit(solution)/shard_map/ppermute | solution.py:56
  56.1 14.9 %collective-permute-done.8 = bf16[192,2304]{1,0:T(8,128)(2,1)S(1)} collective-permute-done((bf16[192,2304]{1,0:T(8,128)(2,1)S(1)}, bf16[192,2304]{1,0:T(8,128)(2,1)S(1)}, u32[]{:S(2)}, u32[]{:S(2)}) %collective-permute-start.8) | collective-permute-done | bytes 884768 | tf_op jit(solution)/shard_map/ppermute | solution.py:56
  72.4 7.7 %collective-permute-done.4.refs_1_ = bf16[2,208,512]{2,1,0:T(8,128)(2,1)S(1)} collective-permute-done((bf16[2,208,512]{2,1,0:T(8,128)(2,1)S(1)}, bf16[2,208,512]{2,1,0:T(8,128)(2,1)S(1)}, u32[]{:S(2)}, u32[]{:S(2)}) %collective-permute-start.4) | collective-permute-done | bytes 426016 | tf_op jit(solution)/shard_map/ppermute | solution.py:56
  80.1 6.3 collective-permute-done.7.refs_3_
  92.6 7.1 %project.1 = (bf16[1024,1536]{1,0:T(8,128)(2,1)}, bf16[1024,384]{1,0:T(8,128)(2,1)}, bf16[1024,128]{1,0:T(8,128)(2,1)}) custom-call(bf16[1024,1536]{1,0:T(8,128)(2,1)} %x_ref.1, bf16[1536,512]{1,0:T(8,128)(2,1)} %get-tuple-element.90.w_ref, f32[1,512]{1,0:T(1,128)} %bitcast.297, f32[1024,128]{1,0:T(8,128)} %get-tuple-element.291.c_ref, ...), custom_call_target="tpu_custom_call" | custom-call | tf_op jit(solution)/shard_map/project/pallas_call | solution.py:262
  101.4 5.0 collective-permute-done.9
  112.4 16.1 %collective-permute-done.10 = bf16[2,1024,128]{2,1,0:T(8,128)(2,1)S(1)} collective-permute-done((bf16[2,1024,128]{2,1,0:T(8,128)(2,1)S(1)}, bf16[2,1024,128]{2,1,0:T(8,128)(2,1)S(1)}, u32[]{:S(2)}, u32[]{:S(2)}) %collective-permute-start.10) | collective-permute-done | bytes 524320 | tf_op jit(solution)/shard_map/ppermute | solution.py:56
  140.3 11.4 %attention_forward.1 = (f32[1024,384]{1,0:T(8,128)}, f32[3,1024,1]{2,1,0:T(8,128)}) custom-call(s32[4]{0:T(128)} %slice.237.starts_ref, s32[1]{0:T(128)} %bitcast.6.place_ref, bf16[1024,384]{1,0:T(8,128)(2,1)} %get-tuple-element.92.q_ref, bf16[4096,128]{1,0:T(8,128)(2,1)} %get-tuple-element.242.k_ref, bf16[4096,128]{1,0:T(8,128)(2,1)} %get-tuple-element.241.v_ref, ...), custom_call_target="tpu_custom_call" | custom-call | tf_op jit(solution)/shard_map/attention_forward/pallas_call | solution.py:368
  159.4 8.3 %collective-permute-done.16.refs_4_ = bf16[256,1536]{1,0:T(8,128)(2,1)} collective-permute-done((bf16[256,1536]{1,0:T(8,128)(2,1)S(1)}, bf16[256,1536]{1,0:T(8,128)(2,1)}, u32[]{:S(2)}, u32[]{:S(2)}) %collective-permute-start.16) | collective-permute-done | bytes 786464 | tf_op jit(solution)/shard_map/ppermute | solution.py:56
  167.7 16.4 %collective-permute-done.17.refs_5_ = bf16[256,1536]{1,0:T(8,128)(2,1)} collective-permute-done((bf16[256,1536]{1,0:T(8,128)(2,1)}, bf16[256,1536]{1,0:T(8,128)(2,1)}, u32[]{:S(2)}, u32[]{:S(2)}) %collective-permute-start.17) | collective-permute-done | bytes 786464 | tf_op jit(solution)/shard_map/ppermute | solution.py:56
  188.6 5.7 stack_rows.6
  198.6 12.9 %convolution_convert_fusion.2.g_ref = bf16[2048,1152]{1,0:T(8,128)(2,1)} fusion(bf16[2048,1536]{1,0:T(8,128)(2,1)} %stack_rows.6, bf16[1536,1152]{1,0:T(8,128)(2,1)} %all-gather.3.cloned.1.call-done), kind=kOutput, calls=%fused_computation.2 | convolution fusion | flops 7250116608 | bytes 14548992 | tf_op jit(solution)/shard_map/dot_general | solution.py:41
  211.5 5.1 collective-permute-done.15
  223.1 15.9 %collective-permute-done.22.refs_1_ = bf16[256,1536]{1,0:T(8,128)(2,1)S(1)} collective-permute-done((bf16[256,1536]{1,0:T(8,128)(2,1)S(1)}, bf16[256,1536]{1,0:T(8,128)(2,1)S(1)}, u32[]{:S(2)}, u32[]{:S(2)}) %collective-permute-start.22) | collective-permute-done | bytes 786464 | tf_op jit(solution)/shard_map/ppermute | solution.py:56
  249.6 6.4 all-gather.5.cloned.1.call-done.wgu_ref
  256.0 13.9 %feed_forward.2 = (bf16[2048,1152]{1,0:T(8,128)(2,1)}, bf16[2048,2304]{1,0:T(8,128)(2,1)}) custom-call(bf16[2048,1536]{1,0:T(8,128)(2,1)} %stack_rows.7.b_ref.refs_4_, bf16[2048,1152]{1,0:T(8,128)(2,1)} %convolution_convert_fusion.2.g_ref, bf16[1536,2304]{1,0:T(8,128)(2,1)} %all-gather.5.cloned.1.call-done.wgu_ref), custom_call_target="tpu_custom_call" | custom-call | tf_op jit(solution)/shard_map/feed_forward/pallas_call | solution.py:297
  277.2 14.1 %feed_forward.3 = (bf16[2048,1152]{1,0:T(8,128)(2,1)}, bf16[2048,2304]{1,0:T(8,128)(2,1)}) custom-call(bf16[2048,1536]{1,0:T(8,128)(2,1)} %stack_rows.8.b_ref, bf16[2048,1152]{1,0:T(8,128)(2,1)} %convolution_convert_fusion.2.g_ref, bf16[1536,2304]{1,0:T(8,128)(2,1)} %all-gather.5.cloned.1.call-done.wgu_ref, ...), custom_call_target="tpu_custom_call", output_to_operand_aliasing={{0}: (3, {}), {1}: (4, {})} | custom-call | tf_op jit(solution)/shard_map/feed_forward/pallas_call | solution.py:297
  291.3 11.3 %fusion.4 = bf16[1024,1536]{1,0:T(8,128)(2,1)S(1)} fusion(bf16[1536,2304]{1,0:T(8,128)(2,1)} %all-gather.5.cloned.1.call-done.wgu_ref, bf16[2048,2304]{1,0:T(8,128)(2,1)} %get-tuple-element.122), kind=kOutput, calls=%fused_computation.7 | convolution fusion | flops 7249330176 | bytes 14942208 | tf_op jit(solution)/shard_map/dot_general | solution.py:45
  303.2 9.7 %fusion.7 = bf16[1024,1536]{1,0:T(8,128)(2,1)S(1)} fusion(bf16[1536,2304]{1,0:T(8,128)(2,1)} %all-gather.5.cloned.1.call-done.wgu_ref, bf16[2048,2304]{1,0:T(8,128)(2,1)S(1)} %copy-done.9), kind=kOutput, calls=%fused_computation.8 | convolution fusion | flops 7249330176 | bytes 14942208 | tf_op jit(solution)/shard_map/dot_general | solution.py:45
  318.8 17.5 %convolution_convert_fusion = bf16[1536,2304]{1,0:T(8,128)(2,1)} fusion(bf16[2048,1536]{1,0:T(8,128)(2,1)S(1)} %bitcast.237, bf16[2048,2304]{1,0:T(8,128)(2,1)S(1)} %copy-done.9), kind=kOutput, calls=%fused_computation | convolution fusion | flops 14499053568 | bytes 22806528 | tf_op jit(solution)/shard_map/dot_general | solution.py:49
  339.3 16.6 %collective-permute-done.30 = bf16[512,768]{1,0:T(8,128)(2,1)S(1)} collective-permute-done((bf16[512,768]{1,0:T(8,128)(2,1)S(1)}, bf16[512,768]{1,0:T(8,128)(2,1)S(1)}, u32[]{:S(2)}, u32[]{:S(2)}) %collective-permute-start.30) | collective-permute-done | bytes 786464 | tf_op jit(solution)/shard_map/ppermute | solution.py:56
  363.8 13.1 %convolution_convert_fusion.1 = bf16[1536,1152]{1,0:T(8,128)(2,1)} fusion(bf16[2048,1536]{1,0:T(8,128)(2,1)} %stack_rows.6, bf16[2048,1152]{1,0:T(8,128)(2,1)} %get-tuple-element.130), kind=kOutput, calls=%fused_computation.1 | convolution fusion | flops 7249526784 | bytes 14548992 | tf_op jit(solution)/shard_map/dot_general | solution.py:49
  383.1 8.0 %convolution_convert_fusion.4 = bf16[1024,1536]{1,0:T(8,128)(2,1)} fusion(bf16[1536,1152]{1,0:T(8,128)(2,1)S(1)} %copy-done.106, bf16[2048,1152]{1,0:T(8,128)(2,1)} %get-tuple-element.130), kind=kOutput, calls=%fused_computation.10 | convolution fusion | flops 3625451520 | bytes 9043968 | tf_op jit(solution)/shard_map/dot_general | solution.py:45
  391.2 5.6 convolution_convert_fusion.3
  419.2 15.5 %attention_backward.1 = (bf16[1024,384]{1,0:T(8,128)(2,1)}, f32[4096,128]{1,0:T(8,128)}, f32[4096,128]{1,0:T(8,128)}) custom-call(s32[4]{0:T(128)} %slice.237.starts_ref, s32[1]{0:T(128)} %bitcast.6.place_ref, bf16[1024,384]{1,0:T(8,128)(2,1)} %get-tuple-element.92.q_ref, bf16[4096,128]{1,0:T(8,128)(2,1)} %get-tuple-element.242.k_ref, ...), custom_call_target="tpu_custom_call" | custom-call | tf_op jit(solution)/shard_map/attention_backward/pallas_call | solution.py:437
  444.5 13.1 %collective-permute-start.40 = (bf16[512,768]{1,0:T(8,128)(2,1)}, bf16[512,768]{1,0:T(8,128)(2,1)}, u32[]{:S(2)}, u32[]{:S(2)}) collective-permute-start(bf16[512,768]{1,0:T(8,128)(2,1)} %slice.342), channel_id=1, source_target_pairs={{0,4},{4,0},{1,5},{5,1},{2,6},{6,2},{3,7},{7,3},{8,12},{12,8},{9,1... | collective-permute-start | bytes 2359304 | tf_op jit(solution)/shard_map/ppermute | solution.py:56
  462.5 21.8 %collective-permute-start.43 = (bf16[2048,128]{1,0:T(8,128)(2,1)}, bf16[2048,128]{1,0:T(8,128)(2,1)}, u32[]{:S(2)}, u32[]{:S(2)}) collective-permute-start(bf16[2048,128]{1,0:T(8,128)(2,1)} %fusion.41), channel_id=1, source_target_pairs={{0,8},{8,0},{1,9},{9,1},{2,10},{10,2},{3,11},{11,3},{4,12},{12,4},... | collective-permute-start | bytes 1572872 | tf_op jit(solution)/shard_map/ppermute | solution.py:56
  488.2 41.3 %collective-permute-done.43 = bf16[2048,128]{1,0:T(8,128)(2,1)} collective-permute-done((bf16[2048,128]{1,0:T(8,128)(2,1)}, bf16[2048,128]{1,0:T(8,128)(2,1)}, u32[]{:S(2)}, u32[]{:S(2)}) %collective-permute-start.43) | collective-permute-done | bytes 524320 | tf_op jit(solution)/shard_map/ppermute | solution.py:56
  538.9 10.1 %collective-permute-done.46 = bf16[1024,128]{1,0:T(8,128)(2,1)S(1)} collective-permute-done((bf16[1024,128]{1,0:T(8,128)(2,1)S(1)}, bf16[1024,128]{1,0:T(8,128)(2,1)S(1)}, u32[]{:S(2)}, u32[]{:S(2)}) %collective-permute-start.46) | collective-permute-done | bytes 262176 | tf_op jit(solution)/shard_map/ppermute | solution.py:56
  577.6 16.9 %collective-permute-done.62 = bf16[192,2304]{1,0:T(8,128)(2,1)S(1)} collective-permute-done((bf16[192,2304]{1,0:T(8,128)(2,1)S(1)}, bf16[192,2304]{1,0:T(8,128)(2,1)S(1)}, u32[]{:S(2)}, u32[]{:S(2)}) %collective-permute-start.62) | collective-permute-done | bytes 884768 | tf_op jit(solution)/shard_map/ppermute | solution.py:56
  634.6 5.1 collective-permute-done.60
  651.6 15.7 %collective-permute-done.52.refs_1_ = bf16[256,1536]{1,0:T(8,128)(2,1)S(1)} collective-permute-done((bf16[256,1536]{1,0:T(8,128)(2,1)S(1)}, bf16[256,1536]{1,0:T(8,128)(2,1)S(1)}, u32[]{:S(2)}, u32[]{:S(2)}) %collective-permute-start.52) | collective-permute-done | bytes 786464 | tf_op jit(solution)/shard_map/ppermute | solution.py:56
  (567 shorter events, 269.8 us)
Async XLA Ops:
  7.2 191.4 %all-gather.3.cloned.1.call-start = ((), (), s32[]{:S(2)}) async-start(), calls=%async_computation.3 | async-start | bytes 4423680 | tf_op jit(solution)/shard_map/all_gather | solution.py:546
  47.5 208.5 %all-gather.5.cloned.1.call-start = ((), (), s32[]{:S(2)}) async-start(), calls=%async_computation.4 | async-start | bytes 8847360 | tf_op jit(solution)/shard_map/all_gather | solution.py:550
  48.3 22.6 %collective-permute-start.8 = (bf16[192,2304]{1,0:T(8,128)(2,1)S(1)}, bf16[192,2304]{1,0:T(8,128)(2,1)S(1)}, u32[]{:S(2)}, u32[]{:S(2)}) collective-permute-start(bf16[192,2304]{1,0:T(8,128)(2,1)S(1)} %pad_maximum_fusion.3), channel_id=1, source_target_pairs={{0,4},{4,0},{1,5},{5,1},{2,6},{6,2},{3,7},{7,3},{8,12},{12,8},{9,1... | collective-permute-start | bytes 2654216 | tf_op jit(solution)/shard_map/ppermute | solution.py:56
  54.0 26.1 %collective-permute-start.4 = (bf16[2,208,512]{2,1,0:T(8,128)(2,1)S(1)}, bf16[2,208,512]{2,1,0:T(8,128)(2,1)S(1)}, u32[]{:S(2)}, u32[]{:S(2)}) collective-permute-start(bf16[2,208,512]{2,1,0:T(8,128)(2,1)S(1)} %copy-done.50), channel_id=1, source_target_pairs={{0,4},{4,0},{1,5},{5,1},{2,6},{6,2},{3,7},{7,3},{8,12},{12,8},{9,1... | collective-permute-start | bytes 1277960 | tf_op jit(solution)/shard_map/ppermute | solution.py:56
  54.5 31.9 %collective-permute-start.7 = (bf16[2,208,512]{2,1,0:T(8,128)(2,1)S(1)}, bf16[2,208,512]{2,1,0:T(8,128)(2,1)S(1)}, u32[]{:S(2)}, u32[]{:S(2)}) collective-permute-start(bf16[2,208,512]{2,1,0:T(8,128)(2,1)S(1)} %copy-done.51), channel_id=1, source_target_pairs={{0,4},{4,0},{1,5},{5,1},{2,6},{6,2},{3,7},{7,3},{8,12},{12,8},{9,1... | collective-permute-start | bytes 1277960 | tf_op jit(solution)/shard_map/ppermute | solution.py:56
  101.3 429.3 %reduce-scatter.4.cloned.1.call-start = ((), (), s32[]{:S(2)}) async-start(), calls=%async_computation.5 | async-start | bytes 8847360 | tf_op jit(solution)/shard_map/reduce_scatter | solution.py:639
  106.5 22.0 %collective-permute-start.10 = (bf16[2,1024,128]{2,1,0:T(8,128)(2,1)S(1)}, bf16[2,1024,128]{2,1,0:T(8,128)(2,1)S(1)}, u32[]{:S(2)}, u32[]{:S(2)}) collective-permute-start(bf16[2,1024,128]{2,1,0:T(8,128)(2,1)S(1)} %maximum_select_fusion.4), channel_id=1, source_target_pairs={{0,8},{8,0},{1,9},{9,1},{2,10},{10,2},{3,11},{11,3},{4,12},{12,4},... | collective-permute-start | bytes 1572872 | tf_op jit(solution)/shard_map/ppermute | solution.py:56
  133.4 19.8 %collective-permute-start.12 = (bf16[2,208,384]{2,1,0:T(8,128)(2,1)S(1)}, bf16[2,208,384]{2,1,0:T(8,128)(2,1)}, u32[]{:S(2)}, u32[]{:S(2)}) collective-permute-start(bf16[2,208,384]{2,1,0:T(8,128)(2,1)S(1)} %maximum_select_fusion.7.refs_0_), channel_id=1, source_target_pairs={{0,4},{4,0},{1,5},{5,1},{2,6},{6,2},{3,7},{7,3},{8,12},{12,8},{9,1... | collective-permute-start | bytes 958472 | tf_op jit(solution)/shard_map/ppermute | solution.py:56
  135.5 32.1 %collective-permute-start.16 = (bf16[256,1536]{1,0:T(8,128)(2,1)S(1)}, bf16[256,1536]{1,0:T(8,128)(2,1)}, u32[]{:S(2)}, u32[]{:S(2)}) collective-permute-start(bf16[256,1536]{1,0:T(8,128)(2,1)S(1)} %get-tuple-element.105.refs_0_), channel_id=1, source_target_pairs={{0,4},{4,0},{1,5},{5,1},{2,6},{6,2},{3,7},{7,3},{8,12},{12,8},{9,1... | collective-permute-start | bytes 2359304 | tf_op jit(solution)/shard_map/ppermute | solution.py:56
  137.0 47.1 %collective-permute-start.17 = (bf16[256,1536]{1,0:T(8,128)(2,1)}, bf16[256,1536]{1,0:T(8,128)(2,1)}, u32[]{:S(2)}, u32[]{:S(2)}) collective-permute-start(bf16[256,1536]{1,0:T(8,128)(2,1)} %get-tuple-element.106.refs_1_), channel_id=1, source_target_pairs={{0,4},{4,0},{1,5},{5,1},{2,6},{6,2},{3,7},{7,3},{8,12},{12,8},{9,1... | collective-permute-start | bytes 2359304 | tf_op jit(solution)/shard_map/ppermute | solution.py:56
  159.4 35.0 %collective-permute-start.14 = (bf16[512,1536]{1,0:T(8,128)(2,1)}, bf16[512,1536]{1,0:T(8,128)(2,1)}, u32[]{:S(2)}, u32[]{:S(2)}) collective-permute-start(bf16[512,1536]{1,0:T(8,128)(2,1)} %convolution_convert_fusion.5), channel_id=1, source_target_pairs={{0,1},{1,0},{2,3},{3,2},{4,5},{5,4},{6,7},{7,6},{8,9},{9,8},{10,11... | collective-permute-start | bytes 4718600 | tf_op jit(solution)/shard_map/ppermute | solution.py:56
  221.6 19.7 %collective-permute-start.21 = (bf16[256,1536]{1,0:T(8,128)(2,1)S(1)}, bf16[256,1536]{1,0:T(8,128)(2,1)S(1)}, u32[]{:S(2)}, u32[]{:S(2)}) collective-permute-start(bf16[256,1536]{1,0:T(8,128)(2,1)S(1)} %multiply_convert_fusion.refs_0_), channel_id=1, source_target_pairs={{0,4},{4,0},{1,5},{5,1},{2,6},{6,2},{3,7},{7,3},{8,12},{12,8},{9,1... | collective-permute-start | bytes 2359304 | tf_op jit(solution)/shard_map/ppermute | solution.py:56
  223.1 20.6 %collective-permute-start.25 = (bf16[256,1536]{1,0:T(8,128)(2,1)S(1)}, bf16[256,1536]{1,0:T(8,128)(2,1)S(1)}, u32[]{:S(2)}, u32[]{:S(2)}) collective-permute-start(bf16[256,1536]{1,0:T(8,128)(2,1)S(1)} %multiply_convert_fusion.refs_0_), channel_id=1, source_target_pairs={{0,1},{1,0},{2,3},{3,2},{4,5},{5,4},{6,7},{7,6},{8,9},{9,8},{10,11... | collective-permute-start | bytes 2359304 | tf_op jit(solution)/shard_map/ppermute | solution.py:56
  239.9 30.0 %collective-permute-start.23 = (bf16[256,768]{1,0:T(8,128)(2,1)}, bf16[256,768]{1,0:T(8,128)(2,1)S(1)}, u32[]{:S(2)}, u32[]{:S(2)}) collective-permute-start(bf16[256,768]{1,0:T(8,128)(2,1)} %slice.327), channel_id=1, source_target_pairs={{0,4},{4,0},{1,5},{5,1},{2,6},{6,2},{3,7},{7,3},{8,12},{12,8},{9,1... | collective-permute-start | bytes 1179656 | tf_op jit(solution)/shard_map/ppermute | solution.py:56
  242.2 27.7 %collective-permute-start.24 = (bf16[256,768]{1,0:T(8,128)(2,1)}, bf16[256,768]{1,0:T(8,128)(2,1)}, u32[]{:S(2)}, u32[]{:S(2)}) collective-permute-start(bf16[256,768]{1,0:T(8,128)(2,1)} %slice.328), channel_id=1, source_target_pairs={{0,2},{2,0},{1,3},{3,1},{4,6},{6,4},{5,7},{7,5},{8,10},{10,8},{9,1... | collective-permute-start | bytes 1179656 | tf_op jit(solution)/shard_map/ppermute | solution.py:56
  336.3 222.3 %reduce-scatter.6.cloned.1.call-start = ((), (), s32[]{:S(2)}) async-start(), calls=%async_computation.6 | async-start | bytes 4423680 | tf_op jit(solution)/shard_map/reduce_scatter | solution.py:639
  377.0 232.3 %reduce-scatter.8.cloned.1.call-start = ((), (), s32[]{:S(2)}) async-start(), calls=%async_computation.7 | async-start | bytes 1474560 | tf_op jit(solution)/shard_map/reduce_scatter | solution.py:639
  436.6 21.5 %collective-permute-start.42 = (bf16[4096,128]{1,0:T(8,128)(2,1)S(1)}, bf16[4096,128]{1,0:T(8,128)(2,1)}, u32[]{:S(2)}, u32[]{:S(2)}) collective-permute-start(bf16[4096,128]{1,0:T(8,128)(2,1)S(1)} %select_convert_fusion), channel_id=1, source_target_pairs={{0,1},{1,0},{2,3},{3,2},{4,5},{5,4},{6,7},{7,6},{8,9},{9,8},{10,11... | collective-permute-start | bytes 3145736 | tf_op jit(solution)/shard_map/ppermute | solution.py:56
  444.5 86.1 %collective-permute-start.40 = (bf16[512,768]{1,0:T(8,128)(2,1)}, bf16[512,768]{1,0:T(8,128)(2,1)}, u32[]{:S(2)}, u32[]{:S(2)}) collective-permute-start(bf16[512,768]{1,0:T(8,128)(2,1)} %slice.342), channel_id=1, source_target_pairs={{0,4},{4,0},{1,5},{5,1},{2,6},{6,2},{3,7},{7,3},{8,12},{12,8},{9,1... | collective-permute-start | bytes 2359304 | tf_op jit(solution)/shard_map/ppermute | solution.py:56
  457.6 73.1 %collective-permute-start.41 = (bf16[512,768]{1,0:T(8,128)(2,1)}, bf16[512,768]{1,0:T(8,128)(2,1)}, u32[]{:S(2)}, u32[]{:S(2)}) collective-permute-start(bf16[512,768]{1,0:T(8,128)(2,1)} %pad_maximum_fusion.5), channel_id=1, source_target_pairs={{0,2},{2,0},{1,3},{3,1},{4,6},{6,4},{5,7},{7,5},{8,10},{10,8},{9,1... | collective-permute-start | bytes 2359304 | tf_op jit(solution)/shard_map/ppermute | solution.py:56
  462.5 66.9 %collective-permute-start.43 = (bf16[2048,128]{1,0:T(8,128)(2,1)}, bf16[2048,128]{1,0:T(8,128)(2,1)}, u32[]{:S(2)}, u32[]{:S(2)}) collective-permute-start(bf16[2048,128]{1,0:T(8,128)(2,1)} %fusion.41), channel_id=1, source_target_pairs={{0,8},{8,0},{1,9},{9,1},{2,10},{10,2},{3,11},{11,3},{4,12},{12,4},... | collective-permute-start | bytes 1572872 | tf_op jit(solution)/shard_map/ppermute | solution.py:56
  487.8 114.7 %collective-permute-start.58 = (bf16[2,2,192,384]{3,2,1,0:T(8,128)(2,1)}, bf16[2,2,192,384]{3,2,1,0:T(8,128)(2,1)}, u32[]{:S(2)}, u32[]{:S(2)}) collective-permute-start(bf16[2,2,192,384]{3,2,1,0:T(8,128)(2,1)} %get-tuple-element.253), channel_id=1, source_target_pairs={{0,4},{4,0},{1,5},{5,1},{2,6},{6,2},{3,7},{7,3},{8,12},{12,8},{9,1... | collective-permute-start | bytes 1769480 | tf_op jit(solution)/shard_map/ppermute | solution.py:56
  532.7 33.6 %collective-permute-start.44 = (bf16[256,768]{1,0:T(8,128)(2,1)}, bf16[256,768]{1,0:T(8,128)(2,1)}, u32[]{:S(2)}, u32[]{:S(2)}) collective-permute-start(bf16[256,768]{1,0:T(8,128)(2,1)} %fusion.38), channel_id=1, source_target_pairs={{0,4},{4,0},{1,5},{5,1},{2,6},{6,2},{3,7},{7,3},{8,12},{12,8},{9,1... | collective-permute-start | bytes 1179656 | tf_op jit(solution)/shard_map/ppermute | solution.py:56
  537.4 30.0 %collective-permute-start.45 = (bf16[256,768]{1,0:T(8,128)(2,1)}, bf16[256,768]{1,0:T(8,128)(2,1)}, u32[]{:S(2)}, u32[]{:S(2)}) collective-permute-start(bf16[256,768]{1,0:T(8,128)(2,1)} %slice.447), channel_id=1, source_target_pairs={{0,2},{2,0},{1,3},{3,1},{4,6},{6,4},{5,7},{7,5},{8,10},{10,8},{9,1... | collective-permute-start | bytes 1179656 | tf_op jit(solution)/shard_map/ppermute | solution.py:56
  566.4 28.1 %collective-permute-start.62 = (bf16[192,2304]{1,0:T(8,128)(2,1)S(1)}, bf16[192,2304]{1,0:T(8,128)(2,1)S(1)}, u32[]{:S(2)}, u32[]{:S(2)}) collective-permute-start(bf16[192,2304]{1,0:T(8,128)(2,1)S(1)} %get-tuple-element.249), channel_id=1, source_target_pairs={{0,4},{4,0},{1,5},{5,1},{2,6},{6,2},{3,7},{7,3},{8,12},{12,8},{9,1... | collective-permute-start | bytes 2654216 | tf_op jit(solution)/shard_map/ppermute | solution.py:56
  571.6 79.8 %collective-permute-start.48 = (bf16[256,1536]{1,0:T(8,128)(2,1)}, bf16[256,1536]{1,0:T(8,128)(2,1)}, u32[]{:S(2)}, u32[]{:S(2)}) collective-permute-start(bf16[256,1536]{1,0:T(8,128)(2,1)} %fusion.30.refs_0_), channel_id=1, source_target_pairs={{0,2},{2,0},{1,3},{3,1},{4,6},{6,4},{5,7},{7,5},{8,10},{10,8},{9,1... | collective-permute-start | bytes 2359304 | tf_op jit(solution)/shard_map/ppermute | solution.py:56
  573.4 97.8 %collective-permute-start.49 = (bf16[256,1536]{1,0:T(8,128)(2,1)}, bf16[256,1536]{1,0:T(8,128)(2,1)}, u32[]{:S(2)}, u32[]{:S(2)}) collective-permute-start(bf16[256,1536]{1,0:T(8,128)(2,1)} %fusion.30.refs_0_), channel_id=1, source_target_pairs={{0,1},{1,0},{2,3},{3,2},{4,5},{5,4},{6,7},{7,6},{8,9},{9,8},{10,11... | collective-permute-start | bytes 2359304 | tf_op jit(solution)/shard_map/ppermute | solution.py:56
  576.1 67.9 %collective-permute-start.51 = (bf16[256,1536]{1,0:T(8,128)(2,1)}, bf16[256,1536]{1,0:T(8,128)(2,1)}, u32[]{:S(2)}, u32[]{:S(2)}) collective-permute-start(bf16[256,1536]{1,0:T(8,128)(2,1)} %fusion.36), channel_id=1, source_target_pairs={{0,2},{2,0},{1,3},{3,1},{4,6},{6,4},{5,7},{7,5},{8,10},{10,8},{9,1... | collective-permute-start | bytes 2359304 | tf_op jit(solution)/shard_map/ppermute | solution.py:56
  594.4 28.6 %collective-permute-start.56 = (bf16[2,208,128]{2,1,0:T(8,128)(2,1)}, bf16[2,208,128]{2,1,0:T(8,128)(2,1)}, u32[]{:S(2)}, u32[]{:S(2)}) collective-permute-start(bf16[2,208,128]{2,1,0:T(8,128)(2,1)} %dynamic-slice_bitcast_fusion.18), channel_id=1, source_target_pairs={{0,16},{16,0},{1,17},{17,1},{2,18},{18,2},{3,19},{19,3},{4,20},{20... | collective-permute-start | bytes 319496 | tf_op jit(solution)/shard_map/ppermute | solution.py:56
  604.8 27.8 %collective-permute-start.59 = (bf16[2,192,384]{2,1,0:T(8,128)(2,1)}, bf16[2,192,384]{2,1,0:T(8,128)(2,1)}, u32[]{:S(2)}, u32[]{:S(2)}) collective-permute-start(bf16[2,192,384]{2,1,0:T(8,128)(2,1)} %get-tuple-element.266), channel_id=1, source_target_pairs={{0,16},{16,0},{1,17},{17,1},{2,18},{18,2},{3,19},{19,3},{4,20},{20... | collective-permute-start | bytes 884744 | tf_op jit(solution)/shard_map/ppermute | solution.py:56
  651.1 23.7 %collective-permute-start.53 = (bf16[256,1536]{1,0:T(8,128)(2,1)S(1)}, bf16[256,1536]{1,0:T(8,128)(2,1)S(1)}, u32[]{:S(2)}, u32[]{:S(2)}) collective-permute-start(bf16[256,1536]{1,0:T(8,128)(2,1)S(1)} %fusion.28.refs_0_), channel_id=1, source_target_pairs={{0,1},{1,0},{2,3},{3,2},{4,5},{5,4},{6,7},{7,6},{8,9},{9,8},{10,11... | collective-permute-start | bytes 2359304 | tf_op jit(solution)/shard_map/ppermute | solution.py:56
  651.5 19.7 %collective-permute-start.50 = (bf16[256,1536]{1,0:T(8,128)(2,1)}, bf16[256,1536]{1,0:T(8,128)(2,1)}, u32[]{:S(2)}, u32[]{:S(2)}) collective-permute-start(bf16[256,1536]{1,0:T(8,128)(2,1)} %collective-permute-done.48.refs_1_), channel_id=1, source_target_pairs={{0,1},{1,0},{2,3},{3,2},{4,5},{5,4},{6,7},{7,6},{8,9},{9,8},{10,11... | collective-permute-start | bytes 2359304 | tf_op jit(solution)/shard_map/ppermute | solution.py:56
  (151 other events, 1332.5 us)
Sparse Core Ops, SparseCore 0:
  47.6 76.0 all-gather.2
  125.8 130.0 all-gather.4
  336.4 121.7 reduce-scatter.3
  460.9 77.9 reduce-scatter.5
  541.1 29.3 reduce-scatter.7

commit v3 on v2

--- a/solution.py
+++ b/solution.py
@@ -2,6 +2,7 @@
 import jax.numpy as jnp
 from jax import lax
 from jax.experimental import pallas as pl
+from jax.experimental.layout import Layout, with_layout_constraint
 from jax.experimental.pallas import tpu as pltpu
 from jax.sharding import Mesh
 from jax.sharding import PartitionSpec as P
@@ -202,8 +203,11 @@
 
 
 def gather_tokens(block, *needed):
+    return spread_core(block, after(swap(block, "y"), *needed))
+
+
+def spread_core(block, by_y):
     y, c = (lax.axis_index(name) for name in NARROW)
-    by_y = after(swap(block, "y"), *needed)
     own = c * 2 + y
     return stack_rows(
         [block, by_y, swap(block, "c"), swap(by_y, "c")], [own, own ^ 1, own ^ 2, own ^ 3]
@@ -458,6 +462,9 @@
             jax.ShapeDtypeStruct((length, HD), jnp.float32),
         ],
         compiler_params=pltpu.CompilerParams(dimension_semantics=("arbitrary",)),
+        cost_estimate=pl.CostEstimate(
+            flops=20 * tokens * tokens * columns, transcendentals=0, bytes_accessed=0
+        ),
         name="attention_backward",
     )(starts, place, queries, keys, values, begins, grads, lse, outputs, cosine, sine)
 
@@ -545,7 +552,7 @@
     down_shard = hidden_pair([padded(down_weight.T)])
     w_down = lax.all_gather(after(down_shard, columns), ("hi", "lo"), axis=0, tiled=True)
     gateup_shard = hidden_pair(
-        after([padded(gateup_weight[:, 0]), padded(gateup_weight[:, 1])], packed)
+        after([padded(gateup_weight[:, 0]), padded(gateup_weight[:, 1])], others)
     )
     w_gateup = lax.all_gather(gateup_shard, ("hi", "lo"), axis=0, tiled=True)
 
@@ -555,9 +562,9 @@
     normed_one, queries, kv_own = project(
         layer_input, w_qkv, b_qkv[None], cosine, sine, kv_cosine, kv_sine, heads
     )
-    kv_own = after(kv_own, gateup_shard)
-    both = pair(kv_own, swap(kv_own, "x"), x)
-    kv_row = pair(both, swap(both, "lo"), lo).reshape(4 * tokens, HD)
+    both = after(pair(kv_own, swap(kv_own, "lo"), lo), gateup_shard)
+    by_place = pair(both, swap(both, "x"), x)
+    kv_row = jnp.transpose(by_place, (1, 0, 2, 3)).reshape(4 * tokens, HD)
     kv_other = swap(kv_row, "c")
     keys = jnp.where(c == 0, kv_row, kv_other)
     values = jnp.where(c == 0, kv_other, kv_row)
@@ -579,19 +586,17 @@
         return pick(split, c), pick(split, 1 - c)
 
     def send_core(kept, sent):
-        return (kept + wide_float(swap(low(sent), "c"))).reshape(2, quarter, D)
-
-    def send_y(total):
-        return pick(total, y), swap(low(pick(total, 1 - y)), "y")
+        return kept + wide_float(swap(low(sent), "c"))
 
     attention_kept, attention_sent = halves(attention_low)
     sent = matmul_nt(attention_sent, w_output)
     out_total = send_core(matmul_nt(attention_kept, w_output), sent)
-    out_parts = send_y(out_total)
-
+    out_split = out_total.reshape(2, quarter, D)
+    out_other = swap(low(pick(out_split, 1 - y)), "y")
     grad_hidden = low(matmul(after(ff_grad, out_total), w_down))
-    out_parts = after(out_parts, grad_hidden)
-    residual = wide_float(pick(layer_input.reshape(4, quarter, D), own)) + add_up(out_parts)
+    out_other = after(out_other, grad_hidden)
+    residual = wide_float(pick(layer_input.reshape(4, quarter, D), own))
+    residual = residual + pick(out_split, y) + wide_float(out_other)
     inverse_two = lax.rsqrt(jnp.mean(residual * residual, axis=-1, keepdims=True) + norm_eps)
     unit_two = residual * inverse_two
     normed_two = low(unit_two * gain_two)
@@ -632,6 +637,8 @@
     def finish_sums(kept, from_y, from_x):
         return jnp.concatenate([kept[0] + wide_float(from_y), kept[1] + wide_float(from_x)], axis=1)
 
+    grad_gateup = low(matmul_tn(ff_input, both_all))
+    both_all = after(both_all, grad_gateup)
     feed_far = low(matmul_nt(both_all[count:], w_gateup))
     feed_near = low(matmul_nt(after(both_all, feed_far)[:count], w_gateup))
 
@@ -641,49 +648,51 @@
     far_sums, near_sums = join_core(feed_far), join_core(feed_near)
     to_x, to_y = first_sends(far_sums, near_sums)
     from_x, from_y = swap(to_x, "x"), swap(to_y, "y")
-    ff_late, both_late = after((ff_input, both_all), to_x, to_y)
-    grad_gateup = low(matmul_tn(ff_late, both_late))
-    from_x, from_y = after((from_x, from_y), grad_gateup)
+    hidden_late = after(hidden_all, to_x, to_y)
+    mlp_far = low(matmul_nt(hidden_late[count:], w_down))
+    mlp_near = low(matmul_nt(after(hidden_late, mlp_far)[:count], w_down))
+    from_x, from_y = after((from_x, from_y), mlp_near)
     kept, (to_y, to_x) = second_sends(far_sums, near_sums, from_x, from_y)
     from_x, from_y = swap(to_x, "x"), swap(to_y, "y")
-    ff_late, hidden_all = after((ff_grad, hidden_all), to_x, to_y)
-    grad_down = low(matmul_tn(ff_late, hidden_all))
-    from_x, from_y = after((from_x, from_y), grad_down)
-    rows_gateup, rows_down = over_rows(grad_gateup), over_rows(grad_down)
     grad_normed_two = finish_sums(kept, from_y, from_x)
     grad_residual = wide_float(grad_near[0]) + rms_back(
         grad_normed_two * gain_two, unit_two, inverse_two
     )
-
     residual_own = low(grad_residual)
-    hidden_all = after(hidden_all, residual_own)
-    mlp_far = low(matmul_nt(hidden_all[count:], w_down))
-    mlp_near = low(matmul_nt(after(hidden_all, mlp_far)[:count], w_down))
-    residual_low = gather_tokens(residual_own, mlp_near)
+    ff_late, hidden_all = after((ff_grad, hidden_all), swap(residual_own, "c"))
+    grad_down = low(matmul_tn(ff_late, hidden_all))
+    rows_gateup, rows_down = over_rows(grad_gateup), over_rows(grad_down)
+    mlp_far, mlp_near = after((mlp_far, mlp_near), residual_own)
+    mlp_far, mlp_near = low(join_core(mlp_far)), join_core(mlp_near)
+    residual_low = gather_tokens(residual_own, grad_down, mlp_near)
 
     grad_attention = low(matmul(residual_low, w_output))
-    rows_output = over_rows(low(matmul_tn(residual_low, attention_low)))
-    mlp_far, mlp_near = after((mlp_far, mlp_near), residual_low)
-    mlp_far, mlp_near = join_core(mlp_far), join_core(mlp_near)
-    to_x, to_y = first_sends(mlp_far, mlp_near)
-    from_x, from_y = swap(to_x, "x"), swap(to_y, "y")
-    grad_attention = after(grad_attention, to_x, to_y)
+    x_output = send_x(
+        low(matmul_tn(residual_low, attention_low)).reshape(wide, rows, heads * HD)
+    )
+    from_far = swap(after(mlp_far, residual_low), "x")
     grad_queries, grad_keys, grad_values = attention_backward(
         queries, keys, values, begins, starts, place, grad_attention, log_total, attention,
         cosine, sine,
     )
     kv_sent = low(jnp.where(c == 0, grad_values, grad_keys))
+    kv_sent, from_far, x_output = after((kv_sent, from_far, x_output), grad_queries, rows_gateup)
+    rows_output = over_rows(low(add_up(x_output)).reshape(-1, heads * HD))
+    mlp_sums = mlp_near + wide_float(from_far)
+    from_y = swap(low(mlp_sums[quarter:]), "y")
     kv_grad = jnp.where(c == 0, grad_keys, grad_values) + wide_float(swap(kv_sent, "c"))
-    kv_grad = kv_grad.reshape(2, 2 * tokens, HD)
+    kv_grad = kv_grad.reshape(2, 2, tokens, HD)
+    kv_kept, kv_sent = (
+        lax.dynamic_index_in_dim(kv_grad, at, axis=1, keepdims=False) for at in (x, 1 - x)
+    )
+    kv_grad = kv_kept + wide_float(swap(low(kv_sent), "x"))
+    parts_gateup = send_hidden(after(rows_gateup, kv_grad))
+    from_y = after(from_y, kv_grad)
+    layer_own = low(residual + mlp_sums[:quarter] + wide_float(from_y))
     kv_grad = pick(kv_grad, lo) + wide_float(swap(low(pick(kv_grad, 1 - lo)), "lo"))
-    kv_grad = kv_grad.reshape(2, tokens, HD)
-    kv_grad = after(kv_grad, rows_gateup)
-    from_x, from_y = after((from_x, from_y), kv_grad)
-    mlp_kept, (to_y, to_x) = second_sends(mlp_far, mlp_near, from_x, from_y)
-    from_x, from_y = swap(to_x, "x"), swap(to_y, "y")
-    kv_grad = pick(kv_grad, x) + wide_float(swap(low(pick(kv_grad, 1 - x)), "x"))
     turned = jnp.concatenate([kv_grad[:, HD // 2 :], kv_grad[:, : HD // 2]], axis=1)
     grad_kv = low(kv_grad * kv_cosine - turned * kv_sine)
+    grad_kv = after(grad_kv, parts_gateup)
 
     w_query, w_kv = w_qkv[:, : heads * HD], w_qkv[:, heads * HD :]
 
@@ -695,51 +704,41 @@
     part_sent = low(input_part(kv_sent, query_sent))
     part_kept = input_part(kv_kept, query_kept)
     part_total = send_core(part_kept, part_sent)
-    part_parts = after(send_y(part_total), rows_down)
-    rows_gateup, rows_down = after((rows_gateup, rows_down), grad_kv)
-    parts_gateup = send_hidden(rows_gateup)
-    parts_down = send_hidden(rows_down)
-    parts_output = send_hidden(after(rows_output, part_total))
-    from_x, from_y = after((from_x, from_y), part_total)
-    layer_output = gather_tokens(low(residual + finish_sums(mlp_kept, from_y, from_x)))
-    grad_normed_one = add_up(part_parts)
-    own_input = wide_float(pick(layer_input.reshape(4, quarter, D), own))
-    own_inverse = lax.rsqrt(jnp.mean(own_input * own_input, axis=-1, keepdims=True) + norm_eps)
-    input_grad = gather_tokens(
-        low(
-            grad_residual
-            + rms_back(grad_normed_one, own_input * own_inverse, own_inverse)
-        )
-    )
-
-    sums_query = low(matmul_tn(normed_one, grad_queries)).reshape(wide, rows, heads * HD)
-    hi_query = send_hi(low(add_up(after(send_x(sums_query), part_total))))
-    lo_query = send_lo(add_up(after(hi_query, part_total)))
+    part_other = swap(low(part_total), "y")
+    layer_by_y = swap(after(layer_own, part_other), "y")
+    grad_normed_one = part_total + wide_float(part_other)
+    core_input = wide_float(pick(layer_input.reshape(2, 2 * quarter, D), c))
+    core_inverse = lax.rsqrt(jnp.mean(core_input * core_input, axis=-1, keepdims=True) + norm_eps)
+    core_grad = wide_float(pick(residual_low.reshape(2, 2 * quarter, D), c)) + rms_back(
+        grad_normed_one, core_input * core_inverse, core_inverse
+    )
+    core_grad = low(core_grad)
+    input_grad = stack_rows([core_grad, swap(core_grad, "c")], [c, 1 - c])
+    layer_output = spread_core(layer_own, after(layer_by_y, core_grad))
+
+    grad_query_weight = low(matmul_tn(normed_one, grad_queries)).reshape(wide, rows, heads * HD)
     grad_kv_weight = low(matmul_tn(normed_one, grad_kv)).reshape(wide, rows, HD)
     bias_query = jnp.sum(wide_float(grad_queries), axis=0).reshape(heads, wide, bias_part)
     bias_query = jnp.transpose(bias_query, (1, 0, 2)).reshape(wide, heads * bias_part)
-    bias_kv = lax.dynamic_update_slice(
-        jnp.zeros((2 * KV, HD), jnp.float32),
-        jnp.sum(wide_float(grad_kv), axis=0, keepdims=True),
-        (column_block, 0),
-    ).reshape(wide, 4 * kv_part)
+    kv_sums = jnp.sum(wide_float(grad_kv), axis=0, keepdims=True)
+    bias_kv = jnp.where(jnp.arange(2 * KV)[:, None] == column_block, kv_sums, 0.0)
+    bias_kv = bias_kv.reshape(wide, 4 * kv_part)
     bias_all = jnp.concatenate([bias_query, bias_kv], axis=1)
     bias_all = jnp.pad(bias_all, ((0, 0), (0, HD - bias_all.shape[1])))
-    extra = jnp.pad(low(bias_all)[:, None], ((0, 0), (0, 15), (0, 0)))
-    x_kv = send_x(jnp.concatenate([grad_kv_weight, extra], axis=1))
-    hi_kv = send_hi(low(add_up(after(x_kv, part_total))))
-    summed = add_up(send_lo(add_up(hi_kv)))
-    parts_down, parts_gateup = after((parts_down, parts_gateup), part_total)
-    summed_down = join_hidden(*parts_down)
+    extra = jnp.pad(low(bias_all)[:, None], ((0, 0), (0, 15), (0, 3 * HD)))
+    grad_qkv = jnp.concatenate([grad_query_weight, grad_kv_weight], axis=2)
+    x_qkv = send_x(jnp.concatenate([grad_qkv, extra], axis=1))
+    sums_qkv = low(add_up(after(x_qkv, part_total, rows_output, rows_down)))
+    summed = wide_float(over_rows(sums_qkv.reshape(-1, 4 * HD)))
+    summed_query = summed[:rows, : heads * HD]
+    summed_kv = summed[:rows, heads * HD :]
+    summed_query_bias = summed[rows, : heads * bias_part].reshape(heads, bias_part)
+    kv_bias = summed[rows, heads * bias_part : heads * bias_part + 4 * kv_part]
+    parts_gateup = after(parts_gateup, sums_qkv)
+    parts_down = send_hidden(after(rows_down, sums_qkv))
     summed_gate = join_hidden(*(part[:, :half] for part in parts_gateup))
     summed_up = join_hidden(*(part[:, half:] for part in parts_gateup))
-    summed_output = add_up(
-        after(parts_output, part_total)
-    )
-    summed_query = add_up(lo_query)
-    summed_kv = summed[:rows]
-    summed_query_bias = summed[rows, : heads * bias_part].reshape(heads, bias_part)
-    kv_bias = summed[rows, heads * bias_part : heads * bias_part + 4 * kv_part]
+    summed_output = wide_float(after(rows_output, core_grad))
 
     grad_gain_one = jnp.sum(
         summed_query * my_qkv[:, : heads * HD], axis=1
@@ -747,6 +746,7 @@
     summed_query = summed_query * row_gains[0]
     summed_kv = summed_kv * row_gains[0]
     summed_gateup = jnp.stack([summed_gate[:, :hidden], summed_up[:, :hidden]], axis=1)
+    summed_gateup = with_layout_constraint(summed_gateup, Layout((0, 1, 2)))
     grad_gain_two = (
         jnp.sum(summed_gateup * wide_float(low(gateup_weight)), axis=(1, 2)) / row_gains[1, :, 0]
     )
@@ -762,7 +762,6 @@
     small_sums = jnp.sum(last[:, :, narrow_rows], axis=(0, 1))
     summed_gains = small_sums[: 2 * narrow_rows].reshape(2, narrow_rows)
     summed_keyvalue_bias = small_sums[2 * narrow_rows : 2 * narrow_rows + kv_part]
-    summed_down = summed_down[:, :hidden].T
     summed_output = summed_output.T
 
     gains_update = adam_update(
@@ -796,6 +795,7 @@
     gateup_update = adam_update(
         summed_gateup, gateup_weight, gateup_weight_first, gateup_weight_second, True, token_count
     )
+    summed_down = join_hidden(*after(parts_down, core_grad))[:, :hidden].T
     down_update = adam_update(
         summed_down, down_weight, down_weight_first, down_weight_second, True, token_count
     )

time: 695 us -> 624 us (0.90)
  waiting for transfers between devices: 244 us -> 207 us
  starting transfers between devices: 90.5 us -> 57.2 us
  local copies, waits for them, and re-layouts: 66.2 us -> 50.6 us
  other arithmetic: 79.2 us -> 88.2 us
    ppermute x67 -> x58, waiting for transfers between devices: 237 us -> 199 us  [swap(): return lax.ppermute(block, axis, [(i, i ^ distance) for i in range(size)])]
    ppermute x67 -> x58, starting transfers between devices: 90.3 us -> 56.7 us  [swap(): return lax.ppermute(block, axis, [(i, i ^ distance) for i in range(size)])]
    unnamed x227 -> x183, local copies, waits for them, and re-layouts: 32.2 us -> 16.2 us
    add x5, other arithmetic: 12.3 us -> 21.5 us  [adam_update(): update = update + decay_rate * master]
    convert_element_type x17 -> x18, other arithmetic: 18 us -> 25.1 us  [low(): return a.astype(jnp.bfloat16)]
  transfers between devices with their start and end apart: 72 -> 64, of which waited for: 30 -> 33; matrix products, arithmetic and copies ran while one was open for 28% -> 33% of each run, Pallas kernels for 10% -> 11%
where the time goes in v3:
time: 624 us; the launch traced here: 614 us
  waiting for transfers between devices  207 us (33%)
  matrix products  104 us (17%)
  Pallas kernels  91 us (15%)
  other arithmetic  88.2 us (14%)
  starting transfers between devices  57.2 us (9%)
  local copies, waits for them, and re-layouts  50.6 us (8%)
  between operations  16.2 us (3%)
    ppermute x58, waiting for transfers between devices, swap(): return lax.ppermute(block, axis, [(i, i ^ distance) for i in range(size)])  199 us
    ppermute x58, starting transfers between devices, swap(): return lax.ppermute(block, axis, [(i, i ^ distance) for i in range(size)])  56.7 us
    dot_general x10, matrix products, matmul_nt(): lax.dot_general(left, right, (((1,), (1,)), ((), ())), preferred_element_...  45.6 us
    dot_general x5, matrix products, matmul_tn(): lax.dot_general(left, right, (((0,), (0,)), ((), ())), preferred_element_...  42.8 us
    pallas_call x2, Pallas kernels, feed_forward(): pl.pallas_call(kernel, grid=(count // block,), in_specs=[by_tokens(D), by...  28 us
    convert_element_type x18, other arithmetic, low(): return a.astype(jnp.bfloat16)  25.1 us
    pallas_call x6, Pallas kernels, stack_rows(): pl.pallas_call(kernel, in_specs=[pl.BlockSpec(memory_space=pltpu.SMEM)] +...  23.6 us
    add x5, other arithmetic, adam_update(): update = update + decay_rate * master  21.5 us
  transfers between devices with their start and end apart: 64, of which 33 were waited for; matrix products, arithmetic and copies ran while one was open for 33% of the time, Pallas kernels for 11%

profile of v3, /device:TPU:0, one launch (start us, length us, event | category | flops | bytes accessed | tf_op | source)
XLA Modules:
  0.0 614.0 jit_solution(17234216979001230144)
XLA Ops:
  24.8 13.0 %collective-permute-done.5 = bf16[208,896]{1,0:T(8,128)(2,1)} collective-permute-done((bf16[208,896]{1,0:T(8,128)(2,1)S(1)}, bf16[208,896]{1,0:T(8,128)(2,1)}, u32[]{:S(2)}, u32[]{:S(2)}) %collective-permute-start.5) | collective-permute-done | bytes 372768 | tf_op jit(solution)/shard_map/ppermute | solution.py:57
  43.2 5.0 collective-permute-done.6
  57.7 8.0 %collective-permute-done.4.refs_1_ = bf16[2,208,512]{2,1,0:T(8,128)(2,1)S(1)} collective-permute-done((bf16[2,208,512]{2,1,0:T(8,128)(2,1)S(1)}, bf16[2,208,512]{2,1,0:T(8,128)(2,1)S(1)}, u32[]{:S(2)}, u32[]{:S(2)}) %collective-permute-start.4) | collective-permute-done | bytes 426016 | tf_op jit(solution)/shard_map/ppermute | solution.py:57
  66.4 6.2 %collective-permute-done.7.refs_3_ = bf16[2,208,512]{2,1,0:T(8,128)(2,1)} collective-permute-done((bf16[2,208,512]{2,1,0:T(8,128)(2,1)S(1)}, bf16[2,208,512]{2,1,0:T(8,128)(2,1)}, u32[]{:S(2)}, u32[]{:S(2)}) %collective-permute-start.7) | collective-permute-done | bytes 426016 | tf_op jit(solution)/shard_map/ppermute | solution.py:57
  81.6 7.1 %project.1 = (bf16[1024,1536]{1,0:T(8,128)(2,1)}, bf16[1024,384]{1,0:T(8,128)(2,1)}, bf16[1024,128]{1,0:T(8,128)(2,1)}) custom-call(bf16[1024,1536]{1,0:T(8,128)(2,1)} %x_ref.1, bf16[1536,512]{1,0:T(8,128)(2,1)} %get-tuple-element.81.w_ref, f32[1,512]{1,0:T(1,128)} %bitcast.281, f32[1024,128]{1,0:T(8,128)} %get-tuple-element.210.c_ref, ...), custom_call_target="tpu_custom_call" | custom-call | tf_op jit(solution)/shard_map/project/pallas_call | solution.py:266
  95.5 21.6 %collective-permute-done.8 = bf16[1024,128]{1,0:T(8,128)(2,1)S(1)} collective-permute-done((bf16[1024,128]{1,0:T(8,128)(2,1)}, bf16[1024,128]{1,0:T(8,128)(2,1)S(1)}, u32[]{:S(2)}, u32[]{:S(2)}) %collective-permute-start.8) | collective-permute-done | bytes 262176 | tf_op jit(solution)/shard_map/ppermute | solution.py:57
  121.7 9.2 %collective-permute-done.10 = bf16[2,1024,128]{2,1,0:T(8,128)(2,1)S(1)} collective-permute-done((bf16[2,1024,128]{2,1,0:T(8,128)(2,1)S(1)}, bf16[2,1024,128]{2,1,0:T(8,128)(2,1)S(1)}, u32[]{:S(2)}, u32[]{:S(2)}) %collective-permute-start.10) | collective-permute-done | bytes 524320 | tf_op jit(solution)/shard_map/ppermute | solution.py:57
  143.1 11.4 %attention_forward.1 = (f32[1024,384]{1,0:T(8,128)}, f32[3,1024,1]{2,1,0:T(8,128)}) custom-call(s32[4]{0:T(128)} %slice.213.starts_ref, s32[1]{0:T(128)} %bitcast.5.place_ref, bf16[1024,384]{1,0:T(8,128)(2,1)} %get-tuple-element.83.q_ref, bf16[4096,128]{1,0:T(8,128)(2,1)} %get-tuple-element.165.k_ref, bf16[4096,128]{1,0:T(8,128)(2,1)} %get-tuple-element.164.v_ref, ...), custom_call_target="tpu_custom_call" | custom-call | tf_op jit(solution)/shard_map/attention_forward/pallas_call | solution.py:372
  162.1 8.5 %collective-permute-done.16.refs_4_ = bf16[256,1536]{1,0:T(8,128)(2,1)} collective-permute-done((bf16[256,1536]{1,0:T(8,128)(2,1)S(1)}, bf16[256,1536]{1,0:T(8,128)(2,1)}, u32[]{:S(2)}, u32[]{:S(2)}) %collective-permute-start.16) | collective-permute-done | bytes 786464 | tf_op jit(solution)/shard_map/ppermute | solution.py:57
  170.6 16.1 %collective-permute-done.17.refs_5_ = bf16[256,1536]{1,0:T(8,128)(2,1)} collective-permute-done((bf16[256,1536]{1,0:T(8,128)(2,1)S(1)}, bf16[256,1536]{1,0:T(8,128)(2,1)}, u32[]{:S(2)}, u32[]{:S(2)}) %collective-permute-start.17) | collective-permute-done | bytes 786464 | tf_op jit(solution)/shard_map/ppermute | solution.py:57
  191.2 5.7 stack_rows.6
  202.7 13.0 %convolution_convert_fusion.2.g_ref = bf16[2048,1152]{1,0:T(8,128)(2,1)} fusion(bf16[2048,1536]{1,0:T(8,128)(2,1)} %stack_rows.6, bf16[1536,1152]{1,0:T(8,128)(2,1)} %all-gather.3.cloned.1.call-done), kind=kOutput, calls=%fused_computation.2 | convolution fusion | flops 7250116608 | bytes 14548992 | tf_op jit(solution)/shard_map/dot_general | solution.py:42
  215.7 5.1 collective-permute-done.15
  224.5 17.0 %collective-permute-done.22.refs_1_ = bf16[256,1536]{1,0:T(8,128)(2,1)S(1)} collective-permute-done((bf16[256,1536]{1,0:T(8,128)(2,1)S(1)}, bf16[256,1536]{1,0:T(8,128)(2,1)S(1)}, u32[]{:S(2)}, u32[]{:S(2)}) %collective-permute-start.22) | collective-permute-done | bytes 786464 | tf_op jit(solution)/shard_map/ppermute | solution.py:57
  255.0 13.9 %feed_forward.2 = (bf16[2048,1152]{1,0:T(8,128)(2,1)}, bf16[2048,2304]{1,0:T(8,128)(2,1)}) custom-call(bf16[2048,1536]{1,0:T(8,128)(2,1)} %stack_rows.7.b_ref.refs_4_, bf16[2048,1152]{1,0:T(8,128)(2,1)} %convolution_convert_fusion.2.g_ref, bf16[1536,2304]{1,0:T(8,128)(2,1)} %all-gather.5.cloned.1.call-done.wgu_ref), custom_call_target="tpu_custom_call" | custom-call | tf_op jit(solution)/shard_map/feed_forward/pallas_call | solution.py:301
  277.3 14.1 %feed_forward.3 = (bf16[2048,1152]{1,0:T(8,128)(2,1)}, bf16[2048,2304]{1,0:T(8,128)(2,1)}) custom-call(bf16[2048,1536]{1,0:T(8,128)(2,1)} %stack_rows.8.b_ref, bf16[2048,1152]{1,0:T(8,128)(2,1)} %convolution_convert_fusion.2.g_ref, bf16[1536,2304]{1,0:T(8,128)(2,1)} %all-gather.5.cloned.1.call-done.wgu_ref, ...), custom_call_target="tpu_custom_call", output_to_operand_aliasing={{0}: (3, {}), {1}: (4, {})} | custom-call | tf_op jit(solution)/shard_map/feed_forward/pallas_call | solution.py:301
  291.4 20.6 %convolution_convert_fusion = bf16[1536,2304]{1,0:T(8,128)(2,1)} fusion(bf16[2048,1536]{1,0:T(8,128)(2,1)} %stack_rows.8.b_ref, bf16[2048,2304]{1,0:T(8,128)(2,1)} %get-tuple-element.111), kind=kOutput, calls=%fused_computation | convolution fusion | flops 14499053568 | bytes 22806528 | tf_op jit(solution)/shard_map/dot_general | solution.py:50
  312.1 11.6 %fusion.4 = bf16[1024,1536]{1,0:T(8,128)(2,1)S(1)} fusion(bf16[1536,2304]{1,0:T(8,128)(2,1)} %all-gather.5.cloned.1.call-done.wgu_ref, bf16[2048,2304]{1,0:T(8,128)(2,1)} %get-tuple-element.111), kind=kOutput, calls=%fused_computation.9 | convolution fusion | flops 7249330176 | bytes 14942208 | tf_op jit(solution)/shard_map/dot_general | solution.py:46
  324.2 11.1 %fusion.7 = bf16[1024,1536]{1,0:T(8,128)(2,1)S(1)} fusion(bf16[1536,2304]{1,0:T(8,128)(2,1)} %all-gather.5.cloned.1.call-done.wgu_ref, bf16[2048,2304]{1,0:T(8,128)(2,1)} %get-tuple-element.111), kind=kOutput, calls=%fused_computation.10 | convolution fusion | flops 7249330176 | bytes 14942208 | tf_op jit(solution)/shard_map/dot_general | solution.py:46
  345.6 5.6 convolution_convert_fusion.3
  351.2 5.0 collective-permute-done.31
  362.6 7.3 %collective-permute-done.33 = bf16[256,768]{1,0:T(8,128)(2,1)S(1)} collective-permute-done((bf16[256,768]{1,0:T(8,128)(2,1)S(1)}, bf16[256,768]{1,0:T(8,128)(2,1)S(1)}, u32[]{:S(2)}, u32[]{:S(2)}) %collective-permute-start.33) | collective-permute-done | bytes 393248 | tf_op jit(solution)/shard_map/ppermute | solution.py:57
  376.3 10.3 %convolution_convert_fusion.1 = bf16[1536,1152]{1,0:T(8,128)(2,1)} fusion(bf16[2048,1536]{1,0:T(8,128)(2,1)S(1)} %bitcast.235, bf16[2048,1152]{1,0:T(8,128)(2,1)S(1)} %bitcast.237), kind=kOutput, calls=%fused_computation.1 | convolution fusion | flops 7249526784 | bytes 14548992 | tf_op jit(solution)/shard_map/dot_general | solution.py:50
  386.6 6.6 %collective-permute-done.36.refs_1_ = bf16[256,1536]{1,0:T(8,128)(2,1)} collective-permute-done((bf16[256,1536]{1,0:T(8,128)(2,1)S(1)}, bf16[256,1536]{1,0:T(8,128)(2,1)}, u32[]{:S(2)}, u32[]{:S(2)}) %collective-permute-start.36) | collective-permute-done | bytes 786464 | tf_op jit(solution)/shard_map/ppermute | solution.py:57
  410.6 15.5 %attention_backward.1 = (bf16[1024,384]{1,0:T(8,128)(2,1)}, f32[4096,128]{1,0:T(8,128)}, f32[4096,128]{1,0:T(8,128)}) custom-call(s32[4]{0:T(128)} %slice.213.starts_ref, s32[1]{0:T(128)} %bitcast.5.place_ref, bf16[1024,384]{1,0:T(8,128)(2,1)} %get-tuple-element.83.q_ref, bf16[4096,128]{1,0:T(8,128)(2,1)} %get-tuple-element.165.k_ref, ...), custom_call_target="tpu_custom_call" | custom-call | flops 8053063680 | tf_op jit(solution)/shard_map/attention_backward/pallas_call | solution.py:441
  429.0 21.8 %collective-permute-done.41 = bf16[2,2,192,384]{3,2,1,0:T(8,128)(2,1)} collective-permute-done((bf16[2,2,192,384]{3,2,1,0:T(8,128)(2,1)}, bf16[2,2,192,384]{3,2,1,0:T(8,128)(2,1)}, u32[]{:S(2)}, u32[]{:S(2)}) %collective-permute-start.41) | collective-permute-done | bytes 589856 | tf_op jit(solution)/shard_map/ppermute | solution.py:57
  457.7 5.0 convolution_convert_fusion.6
  470.0 8.4 %collective-permute-done.44 = bf16[2,1024,128]{2,1,0:T(8,128)(2,1)S(1)} collective-permute-done((bf16[2,1024,128]{2,1,0:T(8,128)(2,1)S(1)}, bf16[2,1024,128]{2,1,0:T(8,128)(2,1)S(1)}, u32[]{:S(2)}, u32[]{:S(2)}) %collective-permute-start.44) | collective-permute-done | bytes 524320 | tf_op jit(solution)/shard_map/ppermute | solution.py:57
  479.2 11.3 %collective-permute-start.45 = (bf16[1024,128]{1,0:T(8,128)(2,1)}, bf16[1024,128]{1,0:T(8,128)(2,1)}, u32[]{:S(2)}, u32[]{:S(2)}) collective-permute-start(bf16[1024,128]{1,0:T(8,128)(2,1)} %fusion.54), channel_id=1, source_target_pairs={{0,8},{8,0},{1,9},{9,1},{2,10},{10,2},{3,11},{11,3},{4,12},{12,4},... | collective-permute-start | bytes 786440 | tf_op jit(solution)/shard_map/ppermute | solution.py:57
  495.9 11.9 %collective-permute-done.45 = bf16[1024,128]{1,0:T(8,128)(2,1)} collective-permute-done((bf16[1024,128]{1,0:T(8,128)(2,1)}, bf16[1024,128]{1,0:T(8,128)(2,1)}, u32[]{:S(2)}, u32[]{:S(2)}) %collective-permute-start.45) | collective-permute-done | bytes 262176 | tf_op jit(solution)/shard_map/ppermute | solution.py:57
  533.5 9.0 %collective-permute-done.53 = bf16[2,2,208,512]{3,2,1,0:T(8,128)(2,1)} collective-permute-done((bf16[2,2,208,512]{3,2,1,0:T(8,128)(2,1)}, bf16[2,2,208,512]{3,2,1,0:T(8,128)(2,1)}, u32[]{:S(2)}, u32[]{:S(2)}) %collective-permute-start.53) | collective-permute-done | bytes 852000 | tf_op jit(solution)/shard_map/ppermute | solution.py:57
  550.5 14.7 %multiply_add_fusion = (f32[192,2,2240]{2,1,0:T(2,128)}, f32[192,2,2240]{2,1,0:T(2,128)S(1)}) fusion(f32[192,2,2240]{2,1,0:T(2,128)S(1)} %copy-done.1, f32[192,2,2240]{2,1,0:T(2,128)S(1)} %copy-done.19, f32[192,2,2240]{2,1,0:T(2,128)S(1)} %copy-done.20, bf16[192,1,2240]{2,1,0:T(2,128)(2,1)S(1)} %copy.78, bf16[192,1,2240]{2,1,0:T(2,128)(2,1)S(1)} %copy.77), kind=kLoop, calls=%fused_computation.15 | loop fusion | flops 15482880 | bytes 18923520 | tf_op jit(solution)/shard_map/add | solution.py:235
  (499 shorter events, 247.3 us)
Async XLA Ops:
  7.2 195.5 %all-gather.3.cloned.1.call-start = ((), (), s32[]{:S(2)}) async-start(), calls=%async_computation.4 | async-start | bytes 4423680 | tf_op jit(solution)/shard_map/all_gather | solution.py:553
  17.6 20.2 %collective-permute-start.5 = (bf16[208,896]{1,0:T(8,128)(2,1)S(1)}, bf16[208,896]{1,0:T(8,128)(2,1)}, u32[]{:S(2)}, u32[]{:S(2)}) collective-permute-start(bf16[208,896]{1,0:T(8,128)(2,1)S(1)} %pad_maximum_fusion.7), channel_id=1, source_target_pairs={{0,16},{16,0},{1,17},{17,1},{2,18},{18,2},{3,19},{19,3},{4,20},{20... | collective-permute-start | bytes 1118216 | tf_op jit(solution)/shard_map/ppermute | solution.py:57
  49.1 205.9 %all-gather.5.cloned.1.call-start = ((), (), s32[]{:S(2)}) async-start(), calls=%async_computation.5 | async-start | bytes 8847360 | tf_op jit(solution)/shard_map/all_gather | solution.py:557
  72.9 19.5 %collective-permute-start.9 = (bf16[192,2304]{1,0:T(8,128)(2,1)S(1)}, bf16[192,2304]{1,0:T(8,128)(2,1)}, u32[]{:S(2)}, u32[]{:S(2)}) collective-permute-start(bf16[192,2304]{1,0:T(8,128)(2,1)S(1)} %pad_maximum_fusion.3), channel_id=1, source_target_pairs={{0,4},{4,0},{1,5},{5,1},{2,6},{6,2},{3,7},{7,3},{8,12},{12,8},{9,1... | collective-permute-start | bytes 2654216 | tf_op jit(solution)/shard_map/ppermute | solution.py:57
  88.6 28.5 %collective-permute-start.8 = (bf16[1024,128]{1,0:T(8,128)(2,1)}, bf16[1024,128]{1,0:T(8,128)(2,1)S(1)}, u32[]{:S(2)}, u32[]{:S(2)}) collective-permute-start(bf16[1024,128]{1,0:T(8,128)(2,1)} %get-tuple-element.84), channel_id=1, source_target_pairs={{0,8},{8,0},{1,9},{9,1},{2,10},{10,2},{3,11},{11,3},{4,12},{12,4},... | collective-permute-start | bytes 786440 | tf_op jit(solution)/shard_map/ppermute | solution.py:57
  95.5 355.3 %reduce-scatter.5.cloned.1.call-start = ((), (), s32[]{:S(2)}) async-start(), calls=%async_computation.6 | async-start | bytes 8847360 | tf_op jit(solution)/shard_map/reduce_scatter | solution.py:646
  136.3 19.7 %collective-permute-start.12 = (bf16[2,208,384]{2,1,0:T(8,128)(2,1)S(1)}, bf16[2,208,384]{2,1,0:T(8,128)(2,1)}, u32[]{:S(2)}, u32[]{:S(2)}) collective-permute-start(bf16[2,208,384]{2,1,0:T(8,128)(2,1)S(1)} %maximum_select_fusion.6.refs_0_), channel_id=1, source_target_pairs={{0,4},{4,0},{1,5},{5,1},{2,6},{6,2},{3,7},{7,3},{8,12},{12,8},{9,1... | collective-permute-start | bytes 958472 | tf_op jit(solution)/shard_map/ppermute | solution.py:57
  136.8 19.2 %collective-permute-start.13 = (bf16[2,208,384]{2,1,0:T(8,128)(2,1)S(1)}, bf16[2,208,384]{2,1,0:T(8,128)(2,1)}, u32[]{:S(2)}, u32[]{:S(2)}) collective-permute-start(bf16[2,208,384]{2,1,0:T(8,128)(2,1)S(1)} %maximum_select_fusion.7.refs_2_), channel_id=1, source_target_pairs={{0,4},{4,0},{1,5},{5,1},{2,6},{6,2},{3,7},{7,3},{8,12},{12,8},{9,1... | collective-permute-start | bytes 958472 | tf_op jit(solution)/shard_map/ppermute | solution.py:57
  138.4 32.2 %collective-permute-start.16 = (bf16[256,1536]{1,0:T(8,128)(2,1)S(1)}, bf16[256,1536]{1,0:T(8,128)(2,1)}, u32[]{:S(2)}, u32[]{:S(2)}) collective-permute-start(bf16[256,1536]{1,0:T(8,128)(2,1)S(1)} %get-tuple-element.96.refs_0_), channel_id=1, source_target_pairs={{0,4},{4,0},{1,5},{5,1},{2,6},{6,2},{3,7},{7,3},{8,12},{12,8},{9,1... | collective-permute-start | bytes 2359304 | tf_op jit(solution)/shard_map/ppermute | solution.py:57
  138.9 47.8 %collective-permute-start.17 = (bf16[256,1536]{1,0:T(8,128)(2,1)S(1)}, bf16[256,1536]{1,0:T(8,128)(2,1)}, u32[]{:S(2)}, u32[]{:S(2)}) collective-permute-start(bf16[256,1536]{1,0:T(8,128)(2,1)S(1)} %get-tuple-element.97.refs_1_), channel_id=1, source_target_pairs={{0,4},{4,0},{1,5},{5,1},{2,6},{6,2},{3,7},{7,3},{8,12},{12,8},{9,1... | collective-permute-start | bytes 2359304 | tf_op jit(solution)/shard_map/ppermute | solution.py:57
  162.1 34.8 %collective-permute-start.14 = (bf16[512,1536]{1,0:T(8,128)(2,1)}, bf16[512,1536]{1,0:T(8,128)(2,1)}, u32[]{:S(2)}, u32[]{:S(2)}) collective-permute-start(bf16[512,1536]{1,0:T(8,128)(2,1)} %convolution_convert_fusion.5), channel_id=1, source_target_pairs={{0,1},{1,0},{2,3},{3,2},{4,5},{5,4},{6,7},{7,6},{8,9},{9,8},{10,11... | collective-permute-start | bytes 4718600 | tf_op jit(solution)/shard_map/ppermute | solution.py:57
  201.2 19.6 %collective-permute-start.15 = (bf16[256,1536]{1,0:T(8,128)(2,1)S(1)}, bf16[256,1536]{1,0:T(8,128)(2,1)S(1)}, u32[]{:S(2)}, u32[]{:S(2)}) collective-permute-start(bf16[256,1536]{1,0:T(8,128)(2,1)S(1)} %fusion.31), channel_id=1, source_target_pairs={{0,2},{2,0},{1,3},{3,1},{4,6},{6,4},{5,7},{7,5},{8,10},{10,8},{9,1... | collective-permute-start | bytes 2359304 | tf_op jit(solution)/shard_map/ppermute | solution.py:57
  222.6 18.9 %collective-permute-start.22 = (bf16[256,1536]{1,0:T(8,128)(2,1)S(1)}, bf16[256,1536]{1,0:T(8,128)(2,1)S(1)}, u32[]{:S(2)}, u32[]{:S(2)}) collective-permute-start(bf16[256,1536]{1,0:T(8,128)(2,1)S(1)} %multiply_convert_fusion.refs_0_), channel_id=1, source_target_pairs={{0,2},{2,0},{1,3},{3,1},{4,6},{6,4},{5,7},{7,5},{8,10},{10,8},{9,1... | collective-permute-start | bytes 2359304 | tf_op jit(solution)/shard_map/ppermute | solution.py:57
  224.5 20.6 %collective-permute-start.25 = (bf16[256,1536]{1,0:T(8,128)(2,1)S(1)}, bf16[256,1536]{1,0:T(8,128)(2,1)S(1)}, u32[]{:S(2)}, u32[]{:S(2)}) collective-permute-start(bf16[256,1536]{1,0:T(8,128)(2,1)S(1)} %multiply_convert_fusion.refs_0_), channel_id=1, source_target_pairs={{0,1},{1,0},{2,3},{3,2},{4,5},{5,4},{6,7},{7,6},{8,9},{9,8},{10,11... | collective-permute-start | bytes 2359304 | tf_op jit(solution)/shard_map/ppermute | solution.py:57
  242.4 26.5 %collective-permute-start.23 = (bf16[256,768]{1,0:T(8,128)(2,1)}, bf16[256,768]{1,0:T(8,128)(2,1)}, u32[]{:S(2)}, u32[]{:S(2)}) collective-permute-start(bf16[256,768]{1,0:T(8,128)(2,1)} %slice.296), channel_id=1, source_target_pairs={{0,4},{4,0},{1,5},{5,1},{2,6},{6,2},{3,7},{7,3},{8,12},{12,8},{9,1... | collective-permute-start | bytes 1179656 | tf_op jit(solution)/shard_map/ppermute | solution.py:57
  243.7 25.2 %collective-permute-start.24 = (bf16[256,768]{1,0:T(8,128)(2,1)}, bf16[256,768]{1,0:T(8,128)(2,1)}, u32[]{:S(2)}, u32[]{:S(2)}) collective-permute-start(bf16[256,768]{1,0:T(8,128)(2,1)} %slice.297), channel_id=1, source_target_pairs={{0,2},{2,0},{1,3},{3,1},{4,6},{6,4},{5,7},{7,5},{8,10},{10,8},{9,1... | collective-permute-start | bytes 1179656 | tf_op jit(solution)/shard_map/ppermute | solution.py:57
  312.0 218.3 %reduce-scatter.9.cloned.1.call-start = ((), (), s32[]{:S(2)}) async-start(), calls=%async_computation.8 | async-start | bytes 4423680 | tf_op jit(solution)/shard_map/reduce_scatter | solution.py:646
  336.4 19.9 %collective-permute-start.31 = (bf16[512,768]{1,0:T(8,128)(2,1)S(1)}, bf16[512,768]{1,0:T(8,128)(2,1)S(1)}, u32[]{:S(2)}, u32[]{:S(2)}) collective-permute-start(bf16[512,768]{1,0:T(8,128)(2,1)S(1)} %slice.300), channel_id=1, source_target_pairs={{0,4},{4,0},{1,5},{5,1},{2,6},{6,2},{3,7},{7,3},{8,12},{12,8},{9,1... | collective-permute-start | bytes 2359304 | tf_op jit(solution)/shard_map/ppermute | solution.py:57
  339.5 19.6 %collective-permute-start.32 = (bf16[512,768]{1,0:T(8,128)(2,1)S(1)}, bf16[512,768]{1,0:T(8,128)(2,1)S(1)}, u32[]{:S(2)}, u32[]{:S(2)}) collective-permute-start(bf16[512,768]{1,0:T(8,128)(2,1)S(1)} %pad_maximum_fusion.4), channel_id=1, source_target_pairs={{0,2},{2,0},{1,3},{3,1},{4,6},{6,4},{5,7},{7,5},{8,10},{10,8},{9,1... | collective-permute-start | bytes 2359304 | tf_op jit(solution)/shard_map/ppermute | solution.py:57
  373.1 20.1 %collective-permute-start.36 = (bf16[256,1536]{1,0:T(8,128)(2,1)S(1)}, bf16[256,1536]{1,0:T(8,128)(2,1)}, u32[]{:S(2)}, u32[]{:S(2)}) collective-permute-start(bf16[256,1536]{1,0:T(8,128)(2,1)S(1)} %add_convert_fusion.2.refs_0_), channel_id=1, source_target_pairs={{0,2},{2,0},{1,3},{3,1},{4,6},{6,4},{5,7},{7,5},{8,10},{10,8},{9,1... | collective-permute-start | bytes 2359304 | tf_op jit(solution)/shard_map/ppermute | solution.py:57
  393.8 139.7 %reduce-scatter.7.cloned.1.call-start = ((), (), s32[]{:S(2)}) async-start(), calls=%async_computation.7 | async-start | bytes 737280 | tf_op jit(solution)/shard_map/reduce_scatter | solution.py:646
  400.9 49.8 %collective-permute-start.40 = (bf16[512,1536]{1,0:T(8,128)(2,1)}, bf16[512,1536]{1,0:T(8,128)(2,1)}, u32[]{:S(2)}, u32[]{:S(2)}) collective-permute-start(bf16[512,1536]{1,0:T(8,128)(2,1)} %add_convert_fusion), channel_id=1, source_target_pairs={{0,4},{4,0},{1,5},{5,1},{2,6},{6,2},{3,7},{7,3},{8,12},{12,8},{9,1... | collective-permute-start | bytes 4718600 | tf_op jit(solution)/shard_map/ppermute | solution.py:57
  407.3 43.4 %collective-permute-start.41 = (bf16[2,2,192,384]{3,2,1,0:T(8,128)(2,1)}, bf16[2,2,192,384]{3,2,1,0:T(8,128)(2,1)}, u32[]{:S(2)}, u32[]{:S(2)}) collective-permute-start(bf16[2,2,192,384]{3,2,1,0:T(8,128)(2,1)} %get-tuple-element.176), channel_id=1, source_target_pairs={{0,4},{4,0},{1,5},{5,1},{2,6},{6,2},{3,7},{7,3},{8,12},{12,8},{9,1... | collective-permute-start | bytes 1769480 | tf_op jit(solution)/shard_map/ppermute | solution.py:57
  469.4 26.5 %collective-permute-start.42 = (bf16[256,1536]{1,0:T(8,128)(2,1)}, bf16[256,1536]{1,0:T(8,128)(2,1)}, u32[]{:S(2)}, u32[]{:S(2)}) collective-permute-start(bf16[256,1536]{1,0:T(8,128)(2,1)} %slice.405), channel_id=1, source_target_pairs={{0,2},{2,0},{1,3},{3,1},{4,6},{6,4},{5,7},{7,5},{8,10},{10,8},{9,1... | collective-permute-start | bytes 2359304 | tf_op jit(solution)/shard_map/ppermute | solution.py:57
  479.2 28.6 %collective-permute-start.45 = (bf16[1024,128]{1,0:T(8,128)(2,1)}, bf16[1024,128]{1,0:T(8,128)(2,1)}, u32[]{:S(2)}, u32[]{:S(2)}) collective-permute-start(bf16[1024,128]{1,0:T(8,128)(2,1)} %fusion.54), channel_id=1, source_target_pairs={{0,8},{8,0},{1,9},{9,1},{2,10},{10,2},{3,11},{11,3},{4,12},{12,4},... | collective-permute-start | bytes 786440 | tf_op jit(solution)/shard_map/ppermute | solution.py:57
  491.8 21.2 %collective-permute-start.46 = (bf16[192,2304]{1,0:T(8,128)(2,1)}, bf16[192,2304]{1,0:T(8,128)(2,1)}, u32[]{:S(2)}, u32[]{:S(2)}) collective-permute-start(bf16[192,2304]{1,0:T(8,128)(2,1)} %get-tuple-element.170), channel_id=1, source_target_pairs={{0,4},{4,0},{1,5},{5,1},{2,6},{6,2},{3,7},{7,3},{8,12},{12,8},{9,1... | collective-permute-start | bytes 2654216 | tf_op jit(solution)/shard_map/ppermute | solution.py:57
  495.6 90.9 %reduce-scatter.11.cloned.1.call-start = ((), (), s32[]{:S(2)}) async-start(), calls=%async_computation.9 | async-start | bytes 1064960 | tf_op jit(solution)/shard_map/reduce_scatter | solution.py:646
  520.8 21.7 %collective-permute-start.53 = (bf16[2,2,208,512]{3,2,1,0:T(8,128)(2,1)}, bf16[2,2,208,512]{3,2,1,0:T(8,128)(2,1)}, u32[]{:S(2)}, u32[]{:S(2)}) collective-permute-start(bf16[2,2,208,512]{3,2,1,0:T(8,128)(2,1)} %get-tuple-element.174), channel_id=1, source_target_pairs={{0,4},{4,0},{1,5},{5,1},{2,6},{6,2},{3,7},{7,3},{8,12},{12,8},{9,1... | collective-permute-start | bytes 2555912 | tf_op jit(solution)/shard_map/ppermute | solution.py:57
  524.6 72.9 %collective-permute-start.50 = (bf16[256,1536]{1,0:T(8,128)(2,1)}, bf16[256,1536]{1,0:T(8,128)(2,1)}, u32[]{:S(2)}, u32[]{:S(2)}) collective-permute-start(bf16[256,1536]{1,0:T(8,128)(2,1)} %fusion.25.refs_0_), channel_id=1, source_target_pairs={{0,1},{1,0},{2,3},{3,2},{4,5},{5,4},{6,7},{7,6},{8,9},{9,8},{10,11... | collective-permute-start | bytes 2359304 | tf_op jit(solution)/shard_map/ppermute | solution.py:57
  529.8 41.9 %collective-permute-start.48 = (bf16[512,1536]{1,0:T(8,128)(2,1)}, bf16[512,1536]{1,0:T(8,128)(2,1)}, u32[]{:S(2)}, u32[]{:S(2)}) collective-permute-start(bf16[512,1536]{1,0:T(8,128)(2,1)} %get-tuple-element.208), channel_id=1, source_target_pairs={{0,2},{2,0},{1,3},{3,1},{4,6},{6,4},{5,7},{7,5},{8,10},{10,8},{9,1... | collective-permute-start | bytes 4718600 | tf_op jit(solution)/shard_map/ppermute | solution.py:57
  571.7 22.4 %collective-permute-start.49 = (bf16[256,1536]{1,0:T(8,128)(2,1)}, bf16[256,1536]{1,0:T(8,128)(2,1)}, u32[]{:S(2)}, u32[]{:S(2)}) collective-permute-start(bf16[256,1536]{1,0:T(8,128)(2,1)} %fusion.25.refs_0_), channel_id=1, source_target_pairs={{0,2},{2,0},{1,3},{3,1},{4,6},{6,4},{5,7},{7,5},{8,10},{10,8},{9,1... | collective-permute-start | bytes 2359304 | tf_op jit(solution)/shard_map/ppermute | solution.py:57
  579.4 22.6 %collective-permute-start.52 = (bf16[512,1536]{1,0:T(8,128)(2,1)}, bf16[512,1536]{1,0:T(8,128)(2,1)S(1)}, u32[]{:S(2)}, u32[]{:S(2)}) collective-permute-start(bf16[512,1536]{1,0:T(8,128)(2,1)} %fusion.18.refs_0_), channel_id=1, source_target_pairs={{0,1},{1,0},{2,3},{3,2},{4,5},{5,4},{6,7},{7,6},{8,9},{9,8},{10,11... | collective-permute-start | bytes 4718600 | tf_op jit(solution)/shard_map/ppermute | solution.py:57
  (122 other events, 908.9 us)
Sparse Core Ops, SparseCore 0:
  49.2 74.9 all-gather.2
  126.4 128.5 all-gather.4
  312.2 121.7 reduce-scatter.4
  436.7 72.3 reduce-scatter.8
  511.2 22.2 reduce-scatter.6
  545.2 21.3 reduce-scatter.10

commit v4 on v3

--- a/solution.py
+++ b/solution.py
@@ -26,7 +26,7 @@
 
 WIDE = ("hi", "lo", "x")
 NARROW = ("y", "c")
-BLOCK_Q = 256
+BLOCK_Q = 512
 BLOCK_K = 512
 
 
@@ -179,7 +179,7 @@
     return wide_float(jnp.concatenate([first, second], axis=1))
 
 
-def hidden_pair(shards):
+def hidden_halves(shards):
     x = lax.axis_index("x")
     half = shards[0].shape[1] // 2
 
@@ -188,7 +188,11 @@
             [lax.dynamic_slice_in_dim(shard, at * half, half, axis=1) for shard in shards], axis=1
         )
 
-    both = pair(part(x), swap(part(1 - x), "x"), x)
+    return part(x), swap(part(1 - x), "x")
+
+
+def join_rows(mine, other):
+    both = pair(mine, other, lax.axis_index("x"))
     return both.reshape((-1,) + both.shape[2:])
 
 
@@ -317,6 +321,20 @@
     )(tokens_in, grads_in, w_gateup, *olds)
 
 
+def over_blocks(first_begin, last_begin, base, run, carry):
+    first = first_begin // BLOCK_K
+    end = (base + BLOCK_Q - 1) // BLOCK_K + 1
+    clear = jnp.minimum((last_begin + BLOCK_K - 1) // BLOCK_K, end)
+    clear_end = jnp.maximum((base + 1) // BLOCK_K, clear)
+    before = clear - first
+
+    def edge(t, carry):
+        return run(jnp.where(t < before, first + t, clear_end + t - before), carry, True)
+
+    carry = lax.fori_loop(clear, clear_end, lambda j, carry: run(j, carry, False), carry)
+    return lax.fori_loop(0, before + end - clear_end, edge, carry)
+
+
 def stacked_heads(ref, heads):
     return jnp.concatenate([ref[:, h * HD : (h + 1) * HD] for h in range(heads)], axis=0)
 
@@ -335,14 +353,15 @@
         row = jnp.concatenate([row] * heads, axis=0)
         begin = jnp.concatenate([begin_ref[...]] * heads, axis=0)
 
-        def body(j, carry):
+        def run(j, carry, masked):
             top, total, acc = carry
             at = pl.multiple_of(j * BLOCK_K, BLOCK_K)
             k = k_ref[pl.ds(at, BLOCK_K), :]
             v = v_ref[pl.ds(at, BLOCK_K), :]
             s = matmul_nt(q, k)
-            col = at + lax.broadcasted_iota(jnp.int32, (1, BLOCK_K), 1)
-            s = jnp.where((col <= row) & (col >= begin), s, masked_score)
+            if masked:
+                col = at + lax.broadcasted_iota(jnp.int32, (1, BLOCK_K), 1)
+                s = jnp.where((col <= row) & (col >= begin), s, masked_score)
             new_top = jnp.maximum(top, jnp.max(s, axis=1, keepdims=True))
             p = jnp.exp(s - new_top)
             scale = jnp.exp(top - new_top)
@@ -350,12 +369,11 @@
             acc = scale * acc + matmul(low(p), v)
             return new_top, total, acc
 
-        first = starts_ref[step] // BLOCK_K
-        last = (base + BLOCK_Q - 1) // BLOCK_K
-        top, total, acc = lax.fori_loop(
-            first,
-            last + 1,
-            body,
+        top, total, acc = over_blocks(
+            starts_ref[2 * step],
+            starts_ref[2 * step + 1],
+            base,
+            run,
             (
                 jnp.full((rows, 1), masked_score, jnp.float32),
                 jnp.zeros((rows, 1), jnp.float32),
@@ -414,22 +432,39 @@
         row = jnp.concatenate([row] * heads, axis=0)
         begin = jnp.concatenate([begin_ref[...]] * heads, axis=0)
 
-        def body(j, dq):
+        def less(a, column):
+            high = low(-column)
+            middle = low(-column - wide_float(high))
+            last = low(-column - wide_float(high) - wide_float(middle))
+            lane = lax.broadcasted_iota(jnp.int32, (rows, HD), 1)
+            parts = jnp.where(lane == 1, middle, jnp.where(lane == 2, last, jnp.zeros_like(last)))
+            return jnp.concatenate([a, jnp.where(lane == 0, high, parts)], axis=1)
+
+        q_less = less(q, lse)
+        g_less = less(g, delta)
+        ones = jnp.ones((BLOCK_K, HD), jnp.bfloat16)
+
+        def run(j, dq, masked):
             at = pl.multiple_of(j * BLOCK_K, BLOCK_K)
             k = k_ref[pl.ds(at, BLOCK_K), :]
             v = v_ref[pl.ds(at, BLOCK_K), :]
-            col = at + lax.broadcasted_iota(jnp.int32, (1, BLOCK_K), 1)
-            s = jnp.where((col <= row) & (col >= begin), matmul_nt(q, k), masked_score)
-            p = jnp.exp(s - lse)
-            dp = matmul_nt(g, v)
-            ds = low(p * (dp - delta))
+            s = matmul_nt(q_less, jnp.concatenate([k, ones], axis=1))
+            if masked:
+                col = at + lax.broadcasted_iota(jnp.int32, (1, BLOCK_K), 1)
+                s = jnp.where((col <= row) & (col >= begin), s, masked_score)
+            p = jnp.exp(s)
+            ds = low(p * matmul_nt(g_less, jnp.concatenate([v, ones], axis=1)))
             dk_ref[pl.ds(at, BLOCK_K), :] += matmul_tn(ds, q)
             dv_ref[pl.ds(at, BLOCK_K), :] += matmul_tn(low(p), g)
             return dq + matmul(ds, k)
 
-        first = starts_ref[step] // BLOCK_K
-        last = (base + BLOCK_Q - 1) // BLOCK_K
-        dq = lax.fori_loop(first, last + 1, body, jnp.zeros((rows, HD), jnp.float32))
+        dq = over_blocks(
+            starts_ref[2 * step],
+            starts_ref[2 * step + 1],
+            base,
+            run,
+            jnp.zeros((rows, HD), jnp.float32),
+        )
         for h in range(heads):
             part = dq[h * BLOCK_Q : (h + 1) * BLOCK_Q]
             turned = pltpu.roll(part, HD // 2, axis=1)
@@ -549,12 +584,11 @@
     def padded(shard):
         return jnp.pad(low(shard), ((0, 0), (0, padding)))
 
-    down_shard = hidden_pair([padded(down_weight.T)])
+    down_shard = join_rows(*hidden_halves([padded(down_weight.T)]))
     w_down = lax.all_gather(after(down_shard, columns), ("hi", "lo"), axis=0, tiled=True)
-    gateup_shard = hidden_pair(
+    gateup_halves = hidden_halves(
         after([padded(gateup_weight[:, 0]), padded(gateup_weight[:, 1])], others)
     )
-    w_gateup = lax.all_gather(gateup_shard, ("hi", "lo"), axis=0, tiled=True)
 
     cosine, sine = rotation(positions)
     kv_cosine = jnp.where(c == 0, cosine, 1.0)
@@ -562,6 +596,8 @@
     normed_one, queries, kv_own = project(
         layer_input, w_qkv, b_qkv[None], cosine, sine, kv_cosine, kv_sine, heads
     )
+    gateup_shard = join_rows(*after(gateup_halves, kv_own))
+    w_gateup = lax.all_gather(gateup_shard, ("hi", "lo"), axis=0, tiled=True)
     both = after(pair(kv_own, swap(kv_own, "lo"), lo), gateup_shard)
     by_place = pair(both, swap(both, "x"), x)
     kv_row = jnp.transpose(by_place, (1, 0, 2, 3)).reshape(4 * tokens, HD)
@@ -569,7 +605,7 @@
     keys = jnp.where(c == 0, kv_row, kv_other)
     values = jnp.where(c == 0, kv_other, kv_row)
     begins = segment_ids - hi * (4 * tokens)
-    starts = begins[::BLOCK_Q]
+    starts = jnp.stack([begins[::BLOCK_Q], begins[BLOCK_Q - 1 :: BLOCK_Q]], axis=1).reshape(-1)
     begins = begins[:, None]
     place = (lo * 2 + x).reshape(1).astype(jnp.int32)
     grad_blocks = grad_out.reshape(4, quarter, D)

time: 624 us -> 618 us (level)
  waiting for transfers between devices: 207 us -> 200 us
    ppermute x58, waiting for transfers between devices: 199 us -> 191 us  [swap(): return lax.ppermute(block, axis, [(i, i ^ distance) for i in range(size)])]
  transfers between devices with their start and end apart: 64 -> 64, of which waited for: 33 -> 32; matrix products, arithmetic and copies ran while one was open for 33% -> 33% of each run, Pallas kernels for 11% -> 12%
where the time goes in v4:
time: 618 us; the launch traced here: 608 us
  waiting for transfers between devices  200 us (32%)
  matrix products  104 us (17%)
  Pallas kernels  91.7 us (15%)
  other arithmetic  88.4 us (14%)
  starting transfers between devices  56.6 us (9%)
  local copies, waits for them, and re-layouts  50.7 us (8%)
  between operations  16.2 us (3%)
    ppermute x58, waiting for transfers between devices, swap(): return lax.ppermute(block, axis, [(i, i ^ distance) for i in range(size)])  191 us
    ppermute x58, starting transfers between devices, swap(): return lax.ppermute(block, axis, [(i, i ^ distance) for i in range(size)])  56.2 us
    dot_general x10, matrix products, matmul_nt(): lax.dot_general(left, right, (((1,), (1,)), ((), ())), preferred_element_...  45.4 us
    dot_general x5, matrix products, matmul_tn(): lax.dot_general(left, right, (((0,), (0,)), ((), ())), preferred_element_...  43 us
    pallas_call x2, Pallas kernels, feed_forward(): pl.pallas_call(kernel, grid=(count // block,), in_specs=[by_tokens(D), by...  28 us
    convert_element_type x18, other arithmetic, low(): return a.astype(jnp.bfloat16)  25.1 us
    pallas_call x6, Pallas kernels, stack_rows(): pl.pallas_call(kernel, in_specs=[pl.BlockSpec(memory_space=pltpu.SMEM)] +...  23.6 us
    add x5, other arithmetic, adam_update(): update = update + decay_rate * master  21.5 us
  transfers between devices with their start and end apart: 64, of which 32 were waited for; matrix products, arithmetic and copies ran while one was open for 33% of the time, Pallas kernels for 12%

profile of v4, /device:TPU:0, one launch (start us, length us, event | category | flops | bytes accessed | tf_op | source)
XLA Modules:
  0.0 608.2 jit_solution(1583866772284260558)
XLA Ops:
  24.8 13.0 %collective-permute-done.5 = bf16[208,896]{1,0:T(8,128)(2,1)} collective-permute-done((bf16[208,896]{1,0:T(8,128)(2,1)S(1)}, bf16[208,896]{1,0:T(8,128)(2,1)}, u32[]{:S(2)}, u32[]{:S(2)}) %collective-permute-start.5) | collective-permute-done | bytes 372768 | tf_op jit(solution)/shard_map/ppermute | solution.py:57
  43.2 5.0 collective-permute-done.6
  57.7 8.0 %collective-permute-done.4.refs_1_ = bf16[2,208,512]{2,1,0:T(8,128)(2,1)S(1)} collective-permute-done((bf16[2,208,512]{2,1,0:T(8,128)(2,1)S(1)}, bf16[2,208,512]{2,1,0:T(8,128)(2,1)S(1)}, u32[]{:S(2)}, u32[]{:S(2)}) %collective-permute-start.4) | collective-permute-done | bytes 426016 | tf_op jit(solution)/shard_map/ppermute | solution.py:57
  66.4 6.2 %collective-permute-done.7.refs_3_ = bf16[2,208,512]{2,1,0:T(8,128)(2,1)} collective-permute-done((bf16[2,208,512]{2,1,0:T(8,128)(2,1)S(1)}, bf16[2,208,512]{2,1,0:T(8,128)(2,1)}, u32[]{:S(2)}, u32[]{:S(2)}) %collective-permute-start.7) | collective-permute-done | bytes 426016 | tf_op jit(solution)/shard_map/ppermute | solution.py:57
  81.7 7.1 %project.1 = (bf16[1024,1536]{1,0:T(8,128)(2,1)}, bf16[1024,384]{1,0:T(8,128)(2,1)}, bf16[1024,128]{1,0:T(8,128)(2,1)}) custom-call(bf16[1024,1536]{1,0:T(8,128)(2,1)} %x_ref.1, bf16[1536,512]{1,0:T(8,128)(2,1)} %get-tuple-element.83.w_ref, f32[1,512]{1,0:T(1,128)} %bitcast.283, f32[1024,128]{1,0:T(8,128)} %get-tuple-element.214.c_ref, ...), custom_call_target="tpu_custom_call" | custom-call | tf_op jit(solution)/shard_map/project/pallas_call | solution.py:270
  97.3 23.5 %collective-permute-done.8 = bf16[1024,128]{1,0:T(8,128)(2,1)S(1)} collective-permute-done((bf16[1024,128]{1,0:T(8,128)(2,1)S(1)}, bf16[1024,128]{1,0:T(8,128)(2,1)S(1)}, u32[]{:S(2)}, u32[]{:S(2)}) %collective-permute-start.8) | collective-permute-done | bytes 262176 | tf_op jit(solution)/shard_map/ppermute | solution.py:57
  125.9 6.9 %collective-permute-done.10 = bf16[2,1024,128]{2,1,0:T(8,128)(2,1)S(1)} collective-permute-done((bf16[2,1024,128]{2,1,0:T(8,128)(2,1)S(1)}, bf16[2,1024,128]{2,1,0:T(8,128)(2,1)S(1)}, u32[]{:S(2)}, u32[]{:S(2)}) %collective-permute-start.10) | collective-permute-done | bytes 524320 | tf_op jit(solution)/shard_map/ppermute | solution.py:57
  144.9 12.1 %attention_forward.1 = (f32[1024,384]{1,0:T(8,128)}, f32[3,1024,1]{2,1,0:T(8,128)}) custom-call(s32[4]{0:T(128)} %reshape.479.starts_ref, s32[1]{0:T(128)} %bitcast.7.place_ref, bf16[1024,384]{1,0:T(8,128)(2,1)} %get-tuple-element.85.q_ref, bf16[4096,128]{1,0:T(8,128)(2,1)} %get-tuple-element.169.k_ref, bf16[4096,128]{1,0:T(8,128)(2,1)} %get-tuple-element.168.v_ref, ...), custom_call_target="tpu_custom_call" | custom-call | tf_op jit(solution)/shard_map/attention_forward/pallas_call | solution.py:390
  164.6 7.7 %collective-permute-done.16.refs_4_ = bf16[256,1536]{1,0:T(8,128)(2,1)} collective-permute-done((bf16[256,1536]{1,0:T(8,128)(2,1)S(1)}, bf16[256,1536]{1,0:T(8,128)(2,1)}, u32[]{:S(2)}, u32[]{:S(2)}) %collective-permute-start.16) | collective-permute-done | bytes 786464 | tf_op jit(solution)/shard_map/ppermute | solution.py:57
  172.3 16.4 %collective-permute-done.17.refs_5_ = bf16[256,1536]{1,0:T(8,128)(2,1)} collective-permute-done((bf16[256,1536]{1,0:T(8,128)(2,1)S(1)}, bf16[256,1536]{1,0:T(8,128)(2,1)}, u32[]{:S(2)}, u32[]{:S(2)}) %collective-permute-start.17) | collective-permute-done | bytes 786464 | tf_op jit(solution)/shard_map/ppermute | solution.py:57
  193.3 5.7 stack_rows.6
  204.9 13.0 %convolution_convert_fusion.2.g_ref = bf16[2048,1152]{1,0:T(8,128)(2,1)} fusion(bf16[2048,1536]{1,0:T(8,128)(2,1)} %stack_rows.6, bf16[1536,1152]{1,0:T(8,128)(2,1)} %all-gather.3.cloned.1.call-done), kind=kOutput, calls=%fused_computation.2 | convolution fusion | flops 7250116608 | bytes 14548992 | tf_op jit(solution)/shard_map/dot_general | solution.py:42
  217.9 5.0 collective-permute-done.15
  227.7 15.8 %collective-permute-done.22.refs_1_ = bf16[256,1536]{1,0:T(8,128)(2,1)S(1)} collective-permute-done((bf16[256,1536]{1,0:T(8,128)(2,1)S(1)}, bf16[256,1536]{1,0:T(8,128)(2,1)S(1)}, u32[]{:S(2)}, u32[]{:S(2)}) %collective-permute-start.22) | collective-permute-done | bytes 786464 | tf_op jit(solution)/shard_map/ppermute | solution.py:57
  255.0 14.1 %feed_forward.2 = (bf16[2048,1152]{1,0:T(8,128)(2,1)}, bf16[2048,2304]{1,0:T(8,128)(2,1)}) custom-call(bf16[2048,1536]{1,0:T(8,128)(2,1)} %stack_rows.7.b_ref.refs_4_, bf16[2048,1152]{1,0:T(8,128)(2,1)} %convolution_convert_fusion.2.g_ref, bf16[1536,2304]{1,0:T(8,128)(2,1)} %all-gather.5.cloned.1.call-done.wgu_ref), custom_call_target="tpu_custom_call" | custom-call | tf_op jit(solution)/shard_map/feed_forward/pallas_call | solution.py:305
  277.4 13.9 %feed_forward.3 = (bf16[2048,1152]{1,0:T(8,128)(2,1)}, bf16[2048,2304]{1,0:T(8,128)(2,1)}) custom-call(bf16[2048,1536]{1,0:T(8,128)(2,1)} %stack_rows.8.b_ref, bf16[2048,1152]{1,0:T(8,128)(2,1)} %convolution_convert_fusion.2.g_ref, bf16[1536,2304]{1,0:T(8,128)(2,1)} %all-gather.5.cloned.1.call-done.wgu_ref, ...), custom_call_target="tpu_custom_call", output_to_operand_aliasing={{0}: (3, {}), {1}: (4, {})} | custom-call | tf_op jit(solution)/shard_map/feed_forward/pallas_call | solution.py:305
  291.3 20.6 %convolution_convert_fusion = bf16[1536,2304]{1,0:T(8,128)(2,1)} fusion(bf16[2048,1536]{1,0:T(8,128)(2,1)} %stack_rows.8.b_ref, bf16[2048,2304]{1,0:T(8,128)(2,1)} %get-tuple-element.115), kind=kOutput, calls=%fused_computation | convolution fusion | flops 14499053568 | bytes 22806528 | tf_op jit(solution)/shard_map/dot_general | solution.py:50
  312.0 11.4 %fusion.4 = bf16[1024,1536]{1,0:T(8,128)(2,1)S(1)} fusion(bf16[1536,2304]{1,0:T(8,128)(2,1)} %all-gather.5.cloned.1.call-done.wgu_ref, bf16[2048,2304]{1,0:T(8,128)(2,1)} %get-tuple-element.115), kind=kOutput, calls=%fused_computation.9 | convolution fusion | flops 7249330176 | bytes 14942208 | tf_op jit(solution)/shard_map/dot_general | solution.py:46
  324.0 11.1 %fusion.7 = bf16[1024,1536]{1,0:T(8,128)(2,1)S(1)} fusion(bf16[1536,2304]{1,0:T(8,128)(2,1)} %all-gather.5.cloned.1.call-done.wgu_ref, bf16[2048,2304]{1,0:T(8,128)(2,1)} %get-tuple-element.115), kind=kOutput, calls=%fused_computation.10 | convolution fusion | flops 7249330176 | bytes 14942208 | tf_op jit(solution)/shard_map/dot_general | solution.py:46
  345.4 5.6 convolution_convert_fusion.3
  351.0 5.0 collective-permute-done.31
  362.4 7.3 %collective-permute-done.33 = bf16[256,768]{1,0:T(8,128)(2,1)S(1)} collective-permute-done((bf16[256,768]{1,0:T(8,128)(2,1)S(1)}, bf16[256,768]{1,0:T(8,128)(2,1)S(1)}, u32[]{:S(2)}, u32[]{:S(2)}) %collective-permute-start.33) | collective-permute-done | bytes 393248 | tf_op jit(solution)/shard_map/ppermute | solution.py:57
  376.1 10.5 %convolution_convert_fusion.1 = bf16[1536,1152]{1,0:T(8,128)(2,1)} fusion(bf16[2048,1536]{1,0:T(8,128)(2,1)S(1)} %bitcast.236, bf16[2048,1152]{1,0:T(8,128)(2,1)S(1)} %bitcast.238), kind=kOutput, calls=%fused_computation.1 | convolution fusion | flops 7249526784 | bytes 14548992 | tf_op jit(solution)/shard_map/dot_general | solution.py:50
  386.6 6.4 %collective-permute-done.36.refs_1_ = bf16[256,1536]{1,0:T(8,128)(2,1)} collective-permute-done((bf16[256,1536]{1,0:T(8,128)(2,1)S(1)}, bf16[256,1536]{1,0:T(8,128)(2,1)}, u32[]{:S(2)}, u32[]{:S(2)}) %collective-permute-start.36) | collective-permute-done | bytes 786464 | tf_op jit(solution)/shard_map/ppermute | solution.py:57
  410.4 15.7 %attention_backward.1 = (bf16[1024,384]{1,0:T(8,128)(2,1)}, f32[4096,128]{1,0:T(8,128)}, f32[4096,128]{1,0:T(8,128)}) custom-call(s32[4]{0:T(128)} %reshape.479.starts_ref, s32[1]{0:T(128)} %bitcast.7.place_ref, bf16[1024,384]{1,0:T(8,128)(2,1)} %get-tuple-element.85.q_ref, bf16[4096,128]{1,0:T(8,128)(2,1)} %get-tuple-element.169.k_ref, ...), custom_call_target="tpu_custom_call" | custom-call | flops 8053063680 | tf_op jit(solution)/shard_map/attention_backward/pallas_call | solution.py:476
  428.9 21.6 %collective-permute-done.41 = bf16[2,2,192,384]{3,2,1,0:T(8,128)(2,1)} collective-permute-done((bf16[2,2,192,384]{3,2,1,0:T(8,128)(2,1)}, bf16[2,2,192,384]{3,2,1,0:T(8,128)(2,1)}, u32[]{:S(2)}, u32[]{:S(2)}) %collective-permute-start.41) | collective-permute-done | bytes 589856 | tf_op jit(solution)/shard_map/ppermute | solution.py:57
  457.5 5.0 convolution_convert_fusion.6
  469.9 8.3 %collective-permute-done.44 = bf16[2,1024,128]{2,1,0:T(8,128)(2,1)S(1)} collective-permute-done((bf16[2,1024,128]{2,1,0:T(8,128)(2,1)S(1)}, bf16[2,1024,128]{2,1,0:T(8,128)(2,1)S(1)}, u32[]{:S(2)}, u32[]{:S(2)}) %collective-permute-start.44) | collective-permute-done | bytes 524320 | tf_op jit(solution)/shard_map/ppermute | solution.py:57
  479.0 5.1 collective-permute-start.45
  489.5 14.5 %collective-permute-done.45 = bf16[1024,128]{1,0:T(8,128)(2,1)} collective-permute-done((bf16[1024,128]{1,0:T(8,128)(2,1)}, bf16[1024,128]{1,0:T(8,128)(2,1)}, u32[]{:S(2)}, u32[]{:S(2)}) %collective-permute-start.45) | collective-permute-done | bytes 262176 | tf_op jit(solution)/shard_map/ppermute | solution.py:57
  525.4 8.7 %reduce-scatter.7.cloned.1.call-done = bf16[192,384]{1,0:T(8,128)(2,1)} async-done(((bf16[768,384]{1,0:T(8,128)(2,1)}), bf16[192,384]{1,0:T(8,128)(2,1)}) %reduce-scatter.7.cloned.1.call-update) | async-done | bytes 147472 | tf_op jit(solution)/shard_map/reduce_scatter | solution.py:682
  544.7 14.6 %multiply_add_fusion = (f32[192,2,2240]{2,1,0:T(2,128)}, f32[192,2,2240]{2,1,0:T(2,128)S(1)}) fusion(f32[192,2,2240]{2,1,0:T(2,128)S(1)} %copy-done.1, f32[192,2,2240]{2,1,0:T(2,128)S(1)} %copy-done.19, f32[192,2,2240]{2,1,0:T(2,128)S(1)} %copy-done.20, bf16[192,1,2240]{2,1,0:T(2,128)(2,1)S(1)} %copy.81, bf16[192,1,2240]{2,1,0:T(2,128)(2,1)S(1)} %copy.80), kind=kLoop, calls=%fused_computation.15 | loop fusion | flops 15482880 | bytes 18923520 | tf_op jit(solution)/shard_map/add | solution.py:239
  (503 shorter events, 247.1 us)
Async XLA Ops:
  7.2 197.7 %all-gather.3.cloned.1.call-start = ((), (), s32[]{:S(2)}) async-start(), calls=%async_computation.4 | async-start | bytes 4423680 | tf_op jit(solution)/shard_map/all_gather | solution.py:588
  17.6 20.2 %collective-permute-start.5 = (bf16[208,896]{1,0:T(8,128)(2,1)S(1)}, bf16[208,896]{1,0:T(8,128)(2,1)}, u32[]{:S(2)}, u32[]{:S(2)}) collective-permute-start(bf16[208,896]{1,0:T(8,128)(2,1)S(1)} %pad_maximum_fusion.8), channel_id=1, source_target_pairs={{0,16},{16,0},{1,17},{17,1},{2,18},{18,2},{3,19},{19,3},{4,20},{20... | collective-permute-start | bytes 1118216 | tf_op jit(solution)/shard_map/ppermute | solution.py:57
  49.1 205.9 %all-gather.5.cloned.1.call-start = ((), (), s32[]{:S(2)}) async-start(), calls=%async_computation.5 | async-start | bytes 8847360 | tf_op jit(solution)/shard_map/all_gather | solution.py:600
  72.8 19.5 %collective-permute-start.9 = (bf16[192,2304]{1,0:T(8,128)(2,1)S(1)}, bf16[192,2304]{1,0:T(8,128)(2,1)}, u32[]{:S(2)}, u32[]{:S(2)}) collective-permute-start(bf16[192,2304]{1,0:T(8,128)(2,1)S(1)} %pad_maximum_fusion.4), channel_id=1, source_target_pairs={{0,4},{4,0},{1,5},{5,1},{2,6},{6,2},{3,7},{7,3},{8,12},{12,8},{9,1... | collective-permute-start | bytes 2654216 | tf_op jit(solution)/shard_map/ppermute | solution.py:57
  95.4 355.1 %reduce-scatter.5.cloned.1.call-start = ((), (), s32[]{:S(2)}) async-start(), calls=%async_computation.6 | async-start | bytes 8847360 | tf_op jit(solution)/shard_map/reduce_scatter | solution.py:682
  95.5 25.4 %collective-permute-start.8 = (bf16[1024,128]{1,0:T(8,128)(2,1)S(1)}, bf16[1024,128]{1,0:T(8,128)(2,1)S(1)}, u32[]{:S(2)}, u32[]{:S(2)}) collective-permute-start(bf16[1024,128]{1,0:T(8,128)(2,1)S(1)} %copy-done.69), channel_id=1, source_target_pairs={{0,8},{8,0},{1,9},{9,1},{2,10},{10,2},{3,11},{11,3},{4,12},{12,4},... | collective-permute-start | bytes 786440 | tf_op jit(solution)/shard_map/ppermute | solution.py:57
  138.1 20.4 %collective-permute-start.12 = (bf16[2,208,384]{2,1,0:T(8,128)(2,1)S(1)}, bf16[2,208,384]{2,1,0:T(8,128)(2,1)}, u32[]{:S(2)}, u32[]{:S(2)}) collective-permute-start(bf16[2,208,384]{2,1,0:T(8,128)(2,1)S(1)} %maximum_select_fusion.6.refs_0_), channel_id=1, source_target_pairs={{0,4},{4,0},{1,5},{5,1},{2,6},{6,2},{3,7},{7,3},{8,12},{12,8},{9,1... | collective-permute-start | bytes 958472 | tf_op jit(solution)/shard_map/ppermute | solution.py:57
  140.2 32.1 %collective-permute-start.16 = (bf16[256,1536]{1,0:T(8,128)(2,1)S(1)}, bf16[256,1536]{1,0:T(8,128)(2,1)}, u32[]{:S(2)}, u32[]{:S(2)}) collective-permute-start(bf16[256,1536]{1,0:T(8,128)(2,1)S(1)} %get-tuple-element.100.refs_0_), channel_id=1, source_target_pairs={{0,4},{4,0},{1,5},{5,1},{2,6},{6,2},{3,7},{7,3},{8,12},{12,8},{9,1... | collective-permute-start | bytes 2359304 | tf_op jit(solution)/shard_map/ppermute | solution.py:57
  141.7 47.1 %collective-permute-start.17 = (bf16[256,1536]{1,0:T(8,128)(2,1)S(1)}, bf16[256,1536]{1,0:T(8,128)(2,1)}, u32[]{:S(2)}, u32[]{:S(2)}) collective-permute-start(bf16[256,1536]{1,0:T(8,128)(2,1)S(1)} %get-tuple-element.101.refs_1_), channel_id=1, source_target_pairs={{0,4},{4,0},{1,5},{5,1},{2,6},{6,2},{3,7},{7,3},{8,12},{12,8},{9,1... | collective-permute-start | bytes 2359304 | tf_op jit(solution)/shard_map/ppermute | solution.py:57
  164.6 34.4 %collective-permute-start.14 = (bf16[512,1536]{1,0:T(8,128)(2,1)}, bf16[512,1536]{1,0:T(8,128)(2,1)}, u32[]{:S(2)}, u32[]{:S(2)}) collective-permute-start(bf16[512,1536]{1,0:T(8,128)(2,1)} %convolution_convert_fusion.5), channel_id=1, source_target_pairs={{0,1},{1,0},{2,3},{3,2},{4,5},{5,4},{6,7},{7,6},{8,9},{9,8},{10,11... | collective-permute-start | bytes 4718600 | tf_op jit(solution)/shard_map/ppermute | solution.py:57
  203.2 19.6 %collective-permute-start.15 = (bf16[256,1536]{1,0:T(8,128)(2,1)S(1)}, bf16[256,1536]{1,0:T(8,128)(2,1)S(1)}, u32[]{:S(2)}, u32[]{:S(2)}) collective-permute-start(bf16[256,1536]{1,0:T(8,128)(2,1)S(1)} %fusion.31), channel_id=1, source_target_pairs={{0,2},{2,0},{1,3},{3,1},{4,6},{6,4},{5,7},{7,5},{8,10},{10,8},{9,1... | collective-permute-start | bytes 2359304 | tf_op jit(solution)/shard_map/ppermute | solution.py:57
  224.7 18.9 %collective-permute-start.22 = (bf16[256,1536]{1,0:T(8,128)(2,1)S(1)}, bf16[256,1536]{1,0:T(8,128)(2,1)S(1)}, u32[]{:S(2)}, u32[]{:S(2)}) collective-permute-start(bf16[256,1536]{1,0:T(8,128)(2,1)S(1)} %multiply_convert_fusion.refs_0_), channel_id=1, source_target_pairs={{0,2},{2,0},{1,3},{3,1},{4,6},{6,4},{5,7},{7,5},{8,10},{10,8},{9,1... | collective-permute-start | bytes 2359304 | tf_op jit(solution)/shard_map/ppermute | solution.py:57
  226.3 19.7 %collective-permute-start.21 = (bf16[256,1536]{1,0:T(8,128)(2,1)S(1)}, bf16[256,1536]{1,0:T(8,128)(2,1)S(1)}, u32[]{:S(2)}, u32[]{:S(2)}) collective-permute-start(bf16[256,1536]{1,0:T(8,128)(2,1)S(1)} %multiply_convert_fusion.refs_0_), channel_id=1, source_target_pairs={{0,4},{4,0},{1,5},{5,1},{2,6},{6,2},{3,7},{7,3},{8,12},{12,8},{9,1... | collective-permute-start | bytes 2359304 | tf_op jit(solution)/shard_map/ppermute | solution.py:57
  227.7 20.6 %collective-permute-start.25 = (bf16[256,1536]{1,0:T(8,128)(2,1)S(1)}, bf16[256,1536]{1,0:T(8,128)(2,1)S(1)}, u32[]{:S(2)}, u32[]{:S(2)}) collective-permute-start(bf16[256,1536]{1,0:T(8,128)(2,1)S(1)} %multiply_convert_fusion.refs_0_), channel_id=1, source_target_pairs={{0,1},{1,0},{2,3},{3,2},{4,5},{5,4},{6,7},{7,6},{8,9},{9,8},{10,11... | collective-permute-start | bytes 2359304 | tf_op jit(solution)/shard_map/ppermute | solution.py:57
  244.5 24.6 %collective-permute-start.23 = (bf16[256,768]{1,0:T(8,128)(2,1)}, bf16[256,768]{1,0:T(8,128)(2,1)}, u32[]{:S(2)}, u32[]{:S(2)}) collective-permute-start(bf16[256,768]{1,0:T(8,128)(2,1)} %slice.300), channel_id=1, source_target_pairs={{0,4},{4,0},{1,5},{5,1},{2,6},{6,2},{3,7},{7,3},{8,12},{12,8},{9,1... | collective-permute-start | bytes 1179656 | tf_op jit(solution)/shard_map/ppermute | solution.py:57
  246.8 22.3 %collective-permute-start.24 = (bf16[256,768]{1,0:T(8,128)(2,1)}, bf16[256,768]{1,0:T(8,128)(2,1)}, u32[]{:S(2)}, u32[]{:S(2)}) collective-permute-start(bf16[256,768]{1,0:T(8,128)(2,1)} %slice.301), channel_id=1, source_target_pairs={{0,2},{2,0},{1,3},{3,1},{4,6},{6,4},{5,7},{7,5},{8,10},{10,8},{9,1... | collective-permute-start | bytes 1179656 | tf_op jit(solution)/shard_map/ppermute | solution.py:57
  312.0 213.4 %reduce-scatter.9.cloned.1.call-start = ((), (), s32[]{:S(2)}) async-start(), calls=%async_computation.8 | async-start | bytes 4423680 | tf_op jit(solution)/shard_map/reduce_scatter | solution.py:682
  336.1 19.9 %collective-permute-start.31 = (bf16[512,768]{1,0:T(8,128)(2,1)S(1)}, bf16[512,768]{1,0:T(8,128)(2,1)S(1)}, u32[]{:S(2)}, u32[]{:S(2)}) collective-permute-start(bf16[512,768]{1,0:T(8,128)(2,1)S(1)} %slice.304), channel_id=1, source_target_pairs={{0,4},{4,0},{1,5},{5,1},{2,6},{6,2},{3,7},{7,3},{8,12},{12,8},{9,1... | collective-permute-start | bytes 2359304 | tf_op jit(solution)/shard_map/ppermute | solution.py:57
  339.3 19.6 %collective-permute-start.32 = (bf16[512,768]{1,0:T(8,128)(2,1)S(1)}, bf16[512,768]{1,0:T(8,128)(2,1)S(1)}, u32[]{:S(2)}, u32[]{:S(2)}) collective-permute-start(bf16[512,768]{1,0:T(8,128)(2,1)S(1)} %pad_maximum_fusion.5), channel_id=1, source_target_pairs={{0,2},{2,0},{1,3},{3,1},{4,6},{6,4},{5,7},{7,5},{8,10},{10,8},{9,1... | collective-permute-start | bytes 2359304 | tf_op jit(solution)/shard_map/ppermute | solution.py:57
  372.9 20.1 %collective-permute-start.36 = (bf16[256,1536]{1,0:T(8,128)(2,1)S(1)}, bf16[256,1536]{1,0:T(8,128)(2,1)}, u32[]{:S(2)}, u32[]{:S(2)}) collective-permute-start(bf16[256,1536]{1,0:T(8,128)(2,1)S(1)} %add_convert_fusion.2.refs_0_), channel_id=1, source_target_pairs={{0,2},{2,0},{1,3},{3,1},{4,6},{6,4},{5,7},{7,5},{8,10},{10,8},{9,1... | collective-permute-start | bytes 2359304 | tf_op jit(solution)/shard_map/ppermute | solution.py:57
  393.6 140.5 %reduce-scatter.7.cloned.1.call-start = ((), (), s32[]{:S(2)}) async-start(), calls=%async_computation.7 | async-start | bytes 737280 | tf_op jit(solution)/shard_map/reduce_scatter | solution.py:682
  400.8 49.8 %collective-permute-start.40 = (bf16[512,1536]{1,0:T(8,128)(2,1)}, bf16[512,1536]{1,0:T(8,128)(2,1)}, u32[]{:S(2)}, u32[]{:S(2)}) collective-permute-start(bf16[512,1536]{1,0:T(8,128)(2,1)} %add_convert_fusion), channel_id=1, source_target_pairs={{0,4},{4,0},{1,5},{5,1},{2,6},{6,2},{3,7},{7,3},{8,12},{12,8},{9,1... | collective-permute-start | bytes 4718600 | tf_op jit(solution)/shard_map/ppermute | solution.py:57
  407.2 43.3 %collective-permute-start.41 = (bf16[2,2,192,384]{3,2,1,0:T(8,128)(2,1)}, bf16[2,2,192,384]{3,2,1,0:T(8,128)(2,1)}, u32[]{:S(2)}, u32[]{:S(2)}) collective-permute-start(bf16[2,2,192,384]{3,2,1,0:T(8,128)(2,1)} %get-tuple-element.180), channel_id=1, source_target_pairs={{0,4},{4,0},{1,5},{5,1},{2,6},{6,2},{3,7},{7,3},{8,12},{12,8},{9,1... | collective-permute-start | bytes 1769480 | tf_op jit(solution)/shard_map/ppermute | solution.py:57
  469.2 20.2 %collective-permute-start.42 = (bf16[256,1536]{1,0:T(8,128)(2,1)}, bf16[256,1536]{1,0:T(8,128)(2,1)}, u32[]{:S(2)}, u32[]{:S(2)}) collective-permute-start(bf16[256,1536]{1,0:T(8,128)(2,1)} %slice.409), channel_id=1, source_target_pairs={{0,2},{2,0},{1,3},{3,1},{4,6},{6,4},{5,7},{7,5},{8,10},{10,8},{9,1... | collective-permute-start | bytes 2359304 | tf_op jit(solution)/shard_map/ppermute | solution.py:57
  479.0 25.0 %collective-permute-start.45 = (bf16[1024,128]{1,0:T(8,128)(2,1)}, bf16[1024,128]{1,0:T(8,128)(2,1)}, u32[]{:S(2)}, u32[]{:S(2)}) collective-permute-start(bf16[1024,128]{1,0:T(8,128)(2,1)} %fusion.54), channel_id=1, source_target_pairs={{0,8},{8,0},{1,9},{9,1},{2,10},{10,2},{3,11},{11,3},{4,12},{12,4},... | collective-permute-start | bytes 786440 | tf_op jit(solution)/shard_map/ppermute | solution.py:57
  485.4 21.4 %collective-permute-start.46 = (bf16[192,2304]{1,0:T(8,128)(2,1)}, bf16[192,2304]{1,0:T(8,128)(2,1)}, u32[]{:S(2)}, u32[]{:S(2)}) collective-permute-start(bf16[192,2304]{1,0:T(8,128)(2,1)} %get-tuple-element.174), channel_id=1, source_target_pairs={{0,4},{4,0},{1,5},{5,1},{2,6},{6,2},{3,7},{7,3},{8,12},{12,8},{9,1... | collective-permute-start | bytes 2654216 | tf_op jit(solution)/shard_map/ppermute | solution.py:57
  489.2 91.5 %reduce-scatter.11.cloned.1.call-start = ((), (), s32[]{:S(2)}) async-start(), calls=%async_computation.9 | async-start | bytes 1064960 | tf_op jit(solution)/shard_map/reduce_scatter | solution.py:682
  514.9 21.7 %collective-permute-start.53 = (bf16[2,2,208,512]{3,2,1,0:T(8,128)(2,1)}, bf16[2,2,208,512]{3,2,1,0:T(8,128)(2,1)}, u32[]{:S(2)}, u32[]{:S(2)}) collective-permute-start(bf16[2,2,208,512]{3,2,1,0:T(8,128)(2,1)} %get-tuple-element.178), channel_id=1, source_target_pairs={{0,4},{4,0},{1,5},{5,1},{2,6},{6,2},{3,7},{7,3},{8,12},{12,8},{9,1... | collective-permute-start | bytes 2555912 | tf_op jit(solution)/shard_map/ppermute | solution.py:57
  519.1 72.6 %collective-permute-start.50 = (bf16[256,1536]{1,0:T(8,128)(2,1)}, bf16[256,1536]{1,0:T(8,128)(2,1)}, u32[]{:S(2)}, u32[]{:S(2)}) collective-permute-start(bf16[256,1536]{1,0:T(8,128)(2,1)} %fusion.25.refs_0_), channel_id=1, source_target_pairs={{0,1},{1,0},{2,3},{3,2},{4,5},{5,4},{6,7},{7,6},{8,9},{9,8},{10,11... | collective-permute-start | bytes 2359304 | tf_op jit(solution)/shard_map/ppermute | solution.py:57
  524.3 41.9 %collective-permute-start.48 = (bf16[512,1536]{1,0:T(8,128)(2,1)}, bf16[512,1536]{1,0:T(8,128)(2,1)}, u32[]{:S(2)}, u32[]{:S(2)}) collective-permute-start(bf16[512,1536]{1,0:T(8,128)(2,1)} %get-tuple-element.212), channel_id=1, source_target_pairs={{0,2},{2,0},{1,3},{3,1},{4,6},{6,4},{5,7},{7,5},{8,10},{10,8},{9,1... | collective-permute-start | bytes 4718600 | tf_op jit(solution)/shard_map/ppermute | solution.py:57
  566.3 22.1 %collective-permute-start.49 = (bf16[256,1536]{1,0:T(8,128)(2,1)}, bf16[256,1536]{1,0:T(8,128)(2,1)}, u32[]{:S(2)}, u32[]{:S(2)}) collective-permute-start(bf16[256,1536]{1,0:T(8,128)(2,1)} %fusion.25.refs_0_), channel_id=1, source_target_pairs={{0,2},{2,0},{1,3},{3,1},{4,6},{6,4},{5,7},{7,5},{8,10},{10,8},{9,1... | collective-permute-start | bytes 2359304 | tf_op jit(solution)/shard_map/ppermute | solution.py:57
  574.5 21.6 %collective-permute-start.52 = (bf16[512,1536]{1,0:T(8,128)(2,1)}, bf16[512,1536]{1,0:T(8,128)(2,1)S(1)}, u32[]{:S(2)}, u32[]{:S(2)}) collective-permute-start(bf16[512,1536]{1,0:T(8,128)(2,1)} %fusion.18.refs_0_), channel_id=1, source_target_pairs={{0,1},{1,0},{2,3},{3,2},{4,5},{5,4},{6,7},{7,6},{8,9},{9,8},{10,11... | collective-permute-start | bytes 4718600 | tf_op jit(solution)/shard_map/ppermute | solution.py:57
  (122 other events, 893.5 us)
Sparse Core Ops, SparseCore 0:
  49.2 74.9 all-gather.2
  126.4 128.5 all-gather.4
  312.1 122.3 reduce-scatter.4
  437.3 72.3 reduce-scatter.8
  511.9 22.1 reduce-scatter.6
  539.3 22.1 reduce-scatter.10

commit v5 on v4

--- a/solution.py
+++ b/solution.py
@@ -645,7 +645,7 @@
         [normed_two, by_y, swap(normed_two, "c"), swap(by_y, "c")], range(4), count=8
     )
     firsts = feed_forward(ff_input, grad_hidden, w_gateup, half, 0, count)
-    by_x, by_both = after((by_x, by_both), firsts[0])
+    by_both = after(by_both, firsts[0])
     by_both = jnp.concatenate(by_both, axis=1)
     ff_input = stack_rows(
         [by_x, by_both, swap(by_x, "c"), swap(by_both, "c")], range(4, 8), into=ff_input, count=8
@@ -713,15 +713,19 @@
     )
     kv_sent = low(jnp.where(c == 0, grad_values, grad_keys))
     kv_sent, from_far, x_output = after((kv_sent, from_far, x_output), grad_queries, rows_gateup)
-    rows_output = over_rows(low(add_up(x_output)).reshape(-1, heads * HD))
-    mlp_sums = mlp_near + wide_float(from_far)
-    from_y = swap(low(mlp_sums[quarter:]), "y")
     kv_grad = jnp.where(c == 0, grad_keys, grad_values) + wide_float(swap(kv_sent, "c"))
     kv_grad = kv_grad.reshape(2, 2, tokens, HD)
     kv_kept, kv_sent = (
         lax.dynamic_index_in_dim(kv_grad, at, axis=1, keepdims=False) for at in (x, 1 - x)
     )
-    kv_grad = kv_kept + wide_float(swap(low(kv_sent), "x"))
+    kv_sent = low(kv_sent)
+    from_far, x_output, mlp_near, normed_late = after(
+        (from_far, x_output, mlp_near, normed_one), kv_sent
+    )
+    rows_output = over_rows(low(add_up(x_output)).reshape(-1, heads * HD))
+    mlp_sums = mlp_near + wide_float(from_far)
+    from_y = swap(low(mlp_sums[quarter:]), "y")
+    kv_grad = kv_kept + wide_float(swap(kv_sent, "x"))
     parts_gateup = send_hidden(after(rows_gateup, kv_grad))
     from_y = after(from_y, kv_grad)
     layer_own = low(residual + mlp_sums[:quarter] + wide_float(from_y))
@@ -743,7 +747,8 @@
     part_other = swap(low(part_total), "y")
     layer_by_y = swap(after(layer_own, part_other), "y")
     grad_normed_one = part_total + wide_float(part_other)
-    core_input = wide_float(pick(layer_input.reshape(2, 2 * quarter, D), c))
+    core_input = pick(after(layer_input, part_total).reshape(2, 2 * quarter, D), c)
+    core_input = wide_float(core_input)
     core_inverse = lax.rsqrt(jnp.mean(core_input * core_input, axis=-1, keepdims=True) + norm_eps)
     core_grad = wide_float(pick(residual_low.reshape(2, 2 * quarter, D), c)) + rms_back(
         grad_normed_one, core_input * core_inverse, core_inverse
@@ -752,7 +757,7 @@
     input_grad = stack_rows([core_grad, swap(core_grad, "c")], [c, 1 - c])
     layer_output = spread_core(layer_own, after(layer_by_y, core_grad))
 
-    grad_query_weight = low(matmul_tn(normed_one, grad_queries)).reshape(wide, rows, heads * HD)
+    grad_query_weight = low(matmul_tn(normed_late, grad_queries)).reshape(wide, rows, heads * HD)
     grad_kv_weight = low(matmul_tn(normed_one, grad_kv)).reshape(wide, rows, HD)
     bias_query = jnp.sum(wide_float(grad_queries), axis=0).reshape(heads, wide, bias_part)
     bias_query = jnp.transpose(bias_query, (1, 0, 2)).reshape(wide, heads * bias_part)
@@ -764,25 +769,28 @@
     extra = jnp.pad(low(bias_all)[:, None], ((0, 0), (0, 15), (0, 3 * HD)))
     grad_qkv = jnp.concatenate([grad_query_weight, grad_kv_weight], axis=2)
     x_qkv = send_x(jnp.concatenate([grad_qkv, extra], axis=1))
-    sums_qkv = low(add_up(after(x_qkv, part_total, rows_output, rows_down)))
+    parts_gateup = after(parts_gateup, part_total)
+    summed_gate = join_hidden(*(part[:, :half] for part in parts_gateup))
+    summed_up = join_hidden(*(part[:, half:] for part in parts_gateup))
+    summed_gateup = jnp.stack([summed_gate[:, :hidden], summed_up[:, :hidden]], axis=1)
+    summed_gateup = with_layout_constraint(summed_gateup, Layout((0, 1, 2)))
+    gateup_update = adam_update(
+        summed_gateup, gateup_weight, gateup_weight_first, gateup_weight_second, True, token_count
+    )
+    sums_qkv = low(add_up(after(x_qkv, gateup_update[1], rows_output, rows_down)))
     summed = wide_float(over_rows(sums_qkv.reshape(-1, 4 * HD)))
     summed_query = summed[:rows, : heads * HD]
     summed_kv = summed[:rows, heads * HD :]
     summed_query_bias = summed[rows, : heads * bias_part].reshape(heads, bias_part)
     kv_bias = summed[rows, heads * bias_part : heads * bias_part + 4 * kv_part]
-    parts_gateup = after(parts_gateup, sums_qkv)
     parts_down = send_hidden(after(rows_down, sums_qkv))
-    summed_gate = join_hidden(*(part[:, :half] for part in parts_gateup))
-    summed_up = join_hidden(*(part[:, half:] for part in parts_gateup))
-    summed_output = wide_float(after(rows_output, core_grad))
+    summed_output = wide_float(after(rows_output, sums_qkv))
 
     grad_gain_one = jnp.sum(
         summed_query * my_qkv[:, : heads * HD], axis=1
     ) + jnp.sum(summed_kv * my_qkv[:, heads * HD :], axis=1)
     summed_query = summed_query * row_gains[0]
     summed_kv = summed_kv * row_gains[0]
-    summed_gateup = jnp.stack([summed_gate[:, :hidden], summed_up[:, :hidden]], axis=1)
-    summed_gateup = with_layout_constraint(summed_gateup, Layout((0, 1, 2)))
     grad_gain_two = (
         jnp.sum(summed_gateup * wide_float(low(gateup_weight)), axis=(1, 2)) / row_gains[1, :, 0]
     )
@@ -827,9 +835,6 @@
     )
     output_update = adam_update(
         summed_output, output_weight, output_weight_first, output_weight_second, True, token_count
-    )
-    gateup_update = adam_update(
-        summed_gateup, gateup_weight, gateup_weight_first, gateup_weight_second, True, token_count
     )
     summed_down = join_hidden(*after(parts_down, core_grad))[:, :hidden].T
     down_update = adam_update(

time: 618 us -> 605 us (0.979)
  waiting for transfers between devices: 200 us -> 188 us
    ppermute x58, waiting for transfers between devices: 191 us -> 184 us  [swap(): return lax.ppermute(block, axis, [(i, i ^ distance) for i in range(size)])]
    unnamed x183 -> x179, local copies, waits for them, and re-layouts: 16.3 us -> 15.6 us
  transfers between devices with their start and end apart: 64 -> 64, of which waited for: 32 -> 30; matrix products, arithmetic and copies ran while one was open for 33% -> 35% of each run, Pallas kernels for 12% -> 12%
where the time goes in v5:
time: 605 us; the launch traced here: 595 us
  waiting for transfers between devices  188 us (31%)
  matrix products  101 us (17%)
  other arithmetic  93.5 us (15%)
  Pallas kernels  91.8 us (15%)
  starting transfers between devices  54.8 us (9%)
  local copies, waits for them, and re-layouts  49.8 us (8%)
  between operations  16.1 us (3%)
    ppermute x58, waiting for transfers between devices, swap(): return lax.ppermute(block, axis, [(i, i ^ distance) for i in range(size)])  184 us
    ppermute x58, starting transfers between devices, swap(): return lax.ppermute(block, axis, [(i, i ^ distance) for i in range(size)])  54.3 us
    dot_general x10, matrix products, matmul_nt(): lax.dot_general(left, right, (((1,), (1,)), ((), ())), preferred_element_...  44.3 us
    dot_general x5, matrix products, matmul_tn(): lax.dot_general(left, right, (((0,), (0,)), ((), ())), preferred_element_...  41 us
    pallas_call x2, Pallas kernels, feed_forward(): pl.pallas_call(kernel, grid=(count // block,), in_specs=[by_tokens(D), by...  28.1 us
    convert_element_type x18, other arithmetic, low(): return a.astype(jnp.bfloat16)  25.3 us
    pallas_call x6, Pallas kernels, stack_rows(): pl.pallas_call(kernel, in_specs=[pl.BlockSpec(memory_space=pltpu.SMEM)] +...  23.6 us
    add x5, other arithmetic, adam_update(): update = update + decay_rate * master  18.1 us
  transfers between devices with their start and end apart: 64, of which 30 were waited for; matrix products, arithmetic and copies ran while one was open for 35% of the time, Pallas kernels for 12%

profile of v5, /device:TPU:0, one launch (start us, length us, event | category | flops | bytes accessed | tf_op | source)
XLA Modules:
  0.0 595.1 jit_solution(16981361550750996905)
XLA Ops:
  24.8 13.0 %collective-permute-done.5 = bf16[208,896]{1,0:T(8,128)(2,1)} collective-permute-done((bf16[208,896]{1,0:T(8,128)(2,1)S(1)}, bf16[208,896]{1,0:T(8,128)(2,1)}, u32[]{:S(2)}, u32[]{:S(2)}) %collective-permute-start.5) | collective-permute-done | bytes 372768 | tf_op jit(solution)/shard_map/ppermute | solution.py:57
  43.2 5.0 collective-permute-done.6
  57.7 8.0 %collective-permute-done.4.refs_1_ = bf16[2,208,512]{2,1,0:T(8,128)(2,1)S(1)} collective-permute-done((bf16[2,208,512]{2,1,0:T(8,128)(2,1)S(1)}, bf16[2,208,512]{2,1,0:T(8,128)(2,1)S(1)}, u32[]{:S(2)}, u32[]{:S(2)}) %collective-permute-start.4) | collective-permute-done | bytes 426016 | tf_op jit(solution)/shard_map/ppermute | solution.py:57
  66.4 6.2 %collective-permute-done.7.refs_3_ = bf16[2,208,512]{2,1,0:T(8,128)(2,1)} collective-permute-done((bf16[2,208,512]{2,1,0:T(8,128)(2,1)S(1)}, bf16[2,208,512]{2,1,0:T(8,128)(2,1)}, u32[]{:S(2)}, u32[]{:S(2)}) %collective-permute-start.7) | collective-permute-done | bytes 426016 | tf_op jit(solution)/shard_map/ppermute | solution.py:57
  81.6 7.1 %project.1 = (bf16[1024,1536]{1,0:T(8,128)(2,1)}, bf16[1024,384]{1,0:T(8,128)(2,1)}, bf16[1024,128]{1,0:T(8,128)(2,1)}) custom-call(bf16[1024,1536]{1,0:T(8,128)(2,1)} %x_ref.1, bf16[1536,512]{1,0:T(8,128)(2,1)} %get-tuple-element.88.w_ref, f32[1,512]{1,0:T(1,128)} %bitcast.283, f32[1024,128]{1,0:T(8,128)} %get-tuple-element.224.c_ref, ...), custom_call_target="tpu_custom_call" | custom-call | tf_op jit(solution)/shard_map/project/pallas_call | solution.py:270
  97.3 23.5 %collective-permute-done.8 = bf16[1024,128]{1,0:T(8,128)(2,1)S(1)} collective-permute-done((bf16[1024,128]{1,0:T(8,128)(2,1)S(1)}, bf16[1024,128]{1,0:T(8,128)(2,1)S(1)}, u32[]{:S(2)}, u32[]{:S(2)}) %collective-permute-start.8) | collective-permute-done | bytes 262176 | tf_op jit(solution)/shard_map/ppermute | solution.py:57
  125.9 6.9 %collective-permute-done.10 = bf16[2,1024,128]{2,1,0:T(8,128)(2,1)S(1)} collective-permute-done((bf16[2,1024,128]{2,1,0:T(8,128)(2,1)S(1)}, bf16[2,1024,128]{2,1,0:T(8,128)(2,1)S(1)}, u32[]{:S(2)}, u32[]{:S(2)}) %collective-permute-start.10) | collective-permute-done | bytes 524320 | tf_op jit(solution)/shard_map/ppermute | solution.py:57
  144.9 12.1 %attention_forward.1 = (f32[1024,384]{1,0:T(8,128)}, f32[3,1024,1]{2,1,0:T(8,128)}) custom-call(s32[4]{0:T(128)} %reshape.479.starts_ref, s32[1]{0:T(128)} %bitcast.7.place_ref, bf16[1024,384]{1,0:T(8,128)(2,1)} %get-tuple-element.90.q_ref, bf16[4096,128]{1,0:T(8,128)(2,1)} %get-tuple-element.179.k_ref, bf16[4096,128]{1,0:T(8,128)(2,1)} %get-tuple-element.178.v_ref, ...), custom_call_target="tpu_custom_call" | custom-call | tf_op jit(solution)/shard_map/attention_forward/pallas_call | solution.py:390
  164.6 7.7 %collective-permute-done.16.refs_4_ = bf16[256,1536]{1,0:T(8,128)(2,1)} collective-permute-done((bf16[256,1536]{1,0:T(8,128)(2,1)S(1)}, bf16[256,1536]{1,0:T(8,128)(2,1)}, u32[]{:S(2)}, u32[]{:S(2)}) %collective-permute-start.16) | collective-permute-done | bytes 786464 | tf_op jit(solution)/shard_map/ppermute | solution.py:57
  172.3 16.5 %collective-permute-done.17.refs_5_ = bf16[256,1536]{1,0:T(8,128)(2,1)} collective-permute-done((bf16[256,1536]{1,0:T(8,128)(2,1)S(1)}, bf16[256,1536]{1,0:T(8,128)(2,1)}, u32[]{:S(2)}, u32[]{:S(2)}) %collective-permute-start.17) | collective-permute-done | bytes 786464 | tf_op jit(solution)/shard_map/ppermute | solution.py:57
  193.3 5.7 stack_rows.6
  204.9 13.0 %convolution_convert_fusion.2.g_ref = bf16[2048,1152]{1,0:T(8,128)(2,1)} fusion(bf16[2048,1536]{1,0:T(8,128)(2,1)} %stack_rows.6, bf16[1536,1152]{1,0:T(8,128)(2,1)} %all-gather.3.cloned.1.call-done), kind=kOutput, calls=%fused_computation.2 | convolution fusion | flops 7250116608 | bytes 14548992 | tf_op jit(solution)/shard_map/dot_general | solution.py:42
  217.9 5.0 collective-permute-done.15
  227.7 15.9 %collective-permute-done.22.refs_1_ = bf16[256,1536]{1,0:T(8,128)(2,1)S(1)} collective-permute-done((bf16[256,1536]{1,0:T(8,128)(2,1)S(1)}, bf16[256,1536]{1,0:T(8,128)(2,1)S(1)}, u32[]{:S(2)}, u32[]{:S(2)}) %collective-permute-start.22) | collective-permute-done | bytes 786464 | tf_op jit(solution)/shard_map/ppermute | solution.py:57
  255.1 14.1 %feed_forward.2 = (bf16[2048,1152]{1,0:T(8,128)(2,1)}, bf16[2048,2304]{1,0:T(8,128)(2,1)}) custom-call(bf16[2048,1536]{1,0:T(8,128)(2,1)} %stack_rows.7.b_ref.refs_4_, bf16[2048,1152]{1,0:T(8,128)(2,1)} %convolution_convert_fusion.2.g_ref, bf16[1536,2304]{1,0:T(8,128)(2,1)} %all-gather.5.cloned.1.call-done.wgu_ref), custom_call_target="tpu_custom_call" | custom-call | tf_op jit(solution)/shard_map/feed_forward/pallas_call | solution.py:305
  277.5 13.9 %feed_forward.3 = (bf16[2048,1152]{1,0:T(8,128)(2,1)}, bf16[2048,2304]{1,0:T(8,128)(2,1)}) custom-call(bf16[2048,1536]{1,0:T(8,128)(2,1)} %stack_rows.8.b_ref, bf16[2048,1152]{1,0:T(8,128)(2,1)} %convolution_convert_fusion.2.g_ref, bf16[1536,2304]{1,0:T(8,128)(2,1)} %all-gather.5.cloned.1.call-done.wgu_ref, ...), custom_call_target="tpu_custom_call", output_to_operand_aliasing={{0}: (3, {}), {1}: (4, {})} | custom-call | tf_op jit(solution)/shard_map/feed_forward/pallas_call | solution.py:305
  291.4 20.7 %convolution_convert_fusion = bf16[1536,2304]{1,0:T(8,128)(2,1)} fusion(bf16[2048,1536]{1,0:T(8,128)(2,1)} %stack_rows.8.b_ref, bf16[2048,2304]{1,0:T(8,128)(2,1)} %get-tuple-element.118), kind=kOutput, calls=%fused_computation | convolution fusion | flops 14499053568 | bytes 22806528 | tf_op jit(solution)/shard_map/dot_general | solution.py:50
  312.2 11.4 %fusion.4 = bf16[1024,1536]{1,0:T(8,128)(2,1)S(1)} fusion(bf16[1536,2304]{1,0:T(8,128)(2,1)} %all-gather.5.cloned.1.call-done.wgu_ref, bf16[2048,2304]{1,0:T(8,128)(2,1)} %get-tuple-element.118), kind=kOutput, calls=%fused_computation.9 | convolution fusion | flops 7249330176 | bytes 14942208 | tf_op jit(solution)/shard_map/dot_general | solution.py:46
  324.1 11.1 %fusion.7 = bf16[1024,1536]{1,0:T(8,128)(2,1)S(1)} fusion(bf16[1536,2304]{1,0:T(8,128)(2,1)} %all-gather.5.cloned.1.call-done.wgu_ref, bf16[2048,2304]{1,0:T(8,128)(2,1)} %get-tuple-element.118), kind=kOutput, calls=%fused_computation.10 | convolution fusion | flops 7249330176 | bytes 14942208 | tf_op jit(solution)/shard_map/dot_general | solution.py:46
  340.9 4.5 convolution_convert_fusion.4
  345.4 4.5 convolution_convert_fusion.3
  349.9 6.3 %collective-permute-done.31 = bf16[512,768]{1,0:T(8,128)(2,1)S(1)} collective-permute-done((bf16[512,768]{1,0:T(8,128)(2,1)S(1)}, bf16[512,768]{1,0:T(8,128)(2,1)S(1)}, u32[]{:S(2)}, u32[]{:S(2)}) %collective-permute-start.31) | collective-permute-done | bytes 786464 | tf_op jit(solution)/shard_map/ppermute | solution.py:57
  362.2 7.6 %collective-permute-done.33 = bf16[256,768]{1,0:T(8,128)(2,1)S(1)} collective-permute-done((bf16[256,768]{1,0:T(8,128)(2,1)S(1)}, bf16[256,768]{1,0:T(8,128)(2,1)S(1)}, u32[]{:S(2)}, u32[]{:S(2)}) %collective-permute-start.33) | collective-permute-done | bytes 393248 | tf_op jit(solution)/shard_map/ppermute | solution.py:57
  377.6 10.5 %convolution_convert_fusion.1 = bf16[1536,1152]{1,0:T(8,128)(2,1)} fusion(bf16[2048,1536]{1,0:T(8,128)(2,1)S(1)} %bitcast.236, bf16[2048,1152]{1,0:T(8,128)(2,1)S(1)} %bitcast.238), kind=kOutput, calls=%fused_computation.1 | convolution fusion | flops 7249526784 | bytes 14548992 | tf_op jit(solution)/shard_map/dot_general | solution.py:50
  410.5 15.6 %attention_backward.1 = (bf16[1024,384]{1,0:T(8,128)(2,1)}, f32[4096,128]{1,0:T(8,128)}, f32[4096,128]{1,0:T(8,128)}) custom-call(s32[4]{0:T(128)} %reshape.479.starts_ref, s32[1]{0:T(128)} %bitcast.7.place_ref, bf16[1024,384]{1,0:T(8,128)(2,1)} %get-tuple-element.90.q_ref, bf16[4096,128]{1,0:T(8,128)(2,1)} %get-tuple-element.179.k_ref, ...), custom_call_target="tpu_custom_call" | custom-call | flops 8053063680 | tf_op jit(solution)/shard_map/attention_backward/pallas_call | solution.py:476
  429.1 21.6 %collective-permute-done.41 = bf16[2,2,192,384]{3,2,1,0:T(8,128)(2,1)} collective-permute-done((bf16[2,2,192,384]{3,2,1,0:T(8,128)(2,1)}, bf16[2,2,192,384]{3,2,1,0:T(8,128)(2,1)}, u32[]{:S(2)}, u32[]{:S(2)}) %collective-permute-start.41) | collective-permute-done | bytes 589856 | tf_op jit(solution)/shard_map/ppermute | solution.py:57
  464.2 5.9 collective-permute-done.44
  471.0 5.2 collective-permute-start.45
  481.6 13.8 %collective-permute-done.45 = bf16[1024,128]{1,0:T(8,128)(2,1)} collective-permute-done((bf16[1024,128]{1,0:T(8,128)(2,1)}, bf16[1024,128]{1,0:T(8,128)(2,1)}, u32[]{:S(2)}, u32[]{:S(2)}) %collective-permute-start.45) | collective-permute-done | bytes 262176 | tf_op jit(solution)/shard_map/ppermute | solution.py:57
  521.1 7.4 %multiply_reduce_fusion = (f32[192]{0:T(256)S(1)}, f32[192,2,2240]{2,1,0:T(2,128)S(1)}) fusion(bf16[192,1,2240]{2,1,0:T(2,128)(2,1)S(1)} %copy.81, bf16[192,1,2240]{2,1,0:T(2,128)(2,1)S(1)} %copy.80, f32[192,2,2240]{2,1,0:T(2,128)S(1)} %copy-done.1), kind=kLoop, calls=%fused_computation.15 | loop fusion | flops 6881088 | bytes 8602368 | tf_op jit(solution)/shard_map/reduce_sum | solution.py:795
  530.3 11.2 %multiply_add_fusion = f32[192,2,2240]{2,1,0:T(2,128)} fusion(f32[192,2,2240]{2,1,0:T(2,128)S(1)} %copy-done.1, f32[192,2,2240]{2,1,0:T(2,128)S(1)} %get-tuple-element.167, f32[192,2,2240]{2,1,0:T(2,128)S(1)} %copy-done.20, f32[192,2,2240]{2,1,0:T(2,128)S(1)} %copy-done.21), kind=kLoop, calls=%fused_computation.16 | loop fusion | flops 12042240 | bytes 17203200 | tf_op jit(solution)/shard_map/add | solution.py:239
  563.4 4.0 reduce-scatter.11.cloned.1.call-done
  (500 shorter events, 244.1 us)
Async XLA Ops:
  7.2 197.7 %all-gather.3.cloned.1.call-start = ((), (), s32[]{:S(2)}) async-start(), calls=%async_computation.4 | async-start | bytes 4423680 | tf_op jit(solution)/shard_map/all_gather | solution.py:588
  17.6 20.2 %collective-permute-start.5 = (bf16[208,896]{1,0:T(8,128)(2,1)S(1)}, bf16[208,896]{1,0:T(8,128)(2,1)}, u32[]{:S(2)}, u32[]{:S(2)}) collective-permute-start(bf16[208,896]{1,0:T(8,128)(2,1)S(1)} %pad_maximum_fusion.8), channel_id=1, source_target_pairs={{0,16},{16,0},{1,17},{17,1},{2,18},{18,2},{3,19},{19,3},{4,20},{20... | collective-permute-start | bytes 1118216 | tf_op jit(solution)/shard_map/ppermute | solution.py:57
  49.1 206.0 %all-gather.5.cloned.1.call-start = ((), (), s32[]{:S(2)}) async-start(), calls=%async_computation.5 | async-start | bytes 8847360 | tf_op jit(solution)/shard_map/all_gather | solution.py:600
  72.8 19.5 %collective-permute-start.9 = (bf16[192,2304]{1,0:T(8,128)(2,1)S(1)}, bf16[192,2304]{1,0:T(8,128)(2,1)}, u32[]{:S(2)}, u32[]{:S(2)}) collective-permute-start(bf16[192,2304]{1,0:T(8,128)(2,1)S(1)} %pad_maximum_fusion.4), channel_id=1, source_target_pairs={{0,4},{4,0},{1,5},{5,1},{2,6},{6,2},{3,7},{7,3},{8,12},{12,8},{9,1... | collective-permute-start | bytes 2654216 | tf_op jit(solution)/shard_map/ppermute | solution.py:57
  95.4 355.3 %reduce-scatter.5.cloned.1.call-start = ((), (), s32[]{:S(2)}) async-start(), calls=%async_computation.6 | async-start | bytes 8847360 | tf_op jit(solution)/shard_map/reduce_scatter | solution.py:682
  95.5 25.4 %collective-permute-start.8 = (bf16[1024,128]{1,0:T(8,128)(2,1)S(1)}, bf16[1024,128]{1,0:T(8,128)(2,1)S(1)}, u32[]{:S(2)}, u32[]{:S(2)}) collective-permute-start(bf16[1024,128]{1,0:T(8,128)(2,1)S(1)} %copy-done.67), channel_id=1, source_target_pairs={{0,8},{8,0},{1,9},{9,1},{2,10},{10,2},{3,11},{11,3},{4,12},{12,4},... | collective-permute-start | bytes 786440 | tf_op jit(solution)/shard_map/ppermute | solution.py:57
  138.1 20.4 %collective-permute-start.12 = (bf16[2,208,384]{2,1,0:T(8,128)(2,1)S(1)}, bf16[2,208,384]{2,1,0:T(8,128)(2,1)}, u32[]{:S(2)}, u32[]{:S(2)}) collective-permute-start(bf16[2,208,384]{2,1,0:T(8,128)(2,1)S(1)} %maximum_select_fusion.6.refs_0_), channel_id=1, source_target_pairs={{0,4},{4,0},{1,5},{5,1},{2,6},{6,2},{3,7},{7,3},{8,12},{12,8},{9,1... | collective-permute-start | bytes 958472 | tf_op jit(solution)/shard_map/ppermute | solution.py:57
  140.2 32.1 %collective-permute-start.16 = (bf16[256,1536]{1,0:T(8,128)(2,1)S(1)}, bf16[256,1536]{1,0:T(8,128)(2,1)}, u32[]{:S(2)}, u32[]{:S(2)}) collective-permute-start(bf16[256,1536]{1,0:T(8,128)(2,1)S(1)} %get-tuple-element.105.refs_0_), channel_id=1, source_target_pairs={{0,4},{4,0},{1,5},{5,1},{2,6},{6,2},{3,7},{7,3},{8,12},{12,8},{9,1... | collective-permute-start | bytes 2359304 | tf_op jit(solution)/shard_map/ppermute | solution.py:57
  141.7 47.1 %collective-permute-start.17 = (bf16[256,1536]{1,0:T(8,128)(2,1)S(1)}, bf16[256,1536]{1,0:T(8,128)(2,1)}, u32[]{:S(2)}, u32[]{:S(2)}) collective-permute-start(bf16[256,1536]{1,0:T(8,128)(2,1)S(1)} %get-tuple-element.106.refs_1_), channel_id=1, source_target_pairs={{0,4},{4,0},{1,5},{5,1},{2,6},{6,2},{3,7},{7,3},{8,12},{12,8},{9,1... | collective-permute-start | bytes 2359304 | tf_op jit(solution)/shard_map/ppermute | solution.py:57
  164.6 34.4 %collective-permute-start.14 = (bf16[512,1536]{1,0:T(8,128)(2,1)}, bf16[512,1536]{1,0:T(8,128)(2,1)}, u32[]{:S(2)}, u32[]{:S(2)}) collective-permute-start(bf16[512,1536]{1,0:T(8,128)(2,1)} %convolution_convert_fusion.5), channel_id=1, source_target_pairs={{0,1},{1,0},{2,3},{3,2},{4,5},{5,4},{6,7},{7,6},{8,9},{9,8},{10,11... | collective-permute-start | bytes 4718600 | tf_op jit(solution)/shard_map/ppermute | solution.py:57
  203.2 19.6 %collective-permute-start.15 = (bf16[256,1536]{1,0:T(8,128)(2,1)S(1)}, bf16[256,1536]{1,0:T(8,128)(2,1)S(1)}, u32[]{:S(2)}, u32[]{:S(2)}) collective-permute-start(bf16[256,1536]{1,0:T(8,128)(2,1)S(1)} %fusion.31), channel_id=1, source_target_pairs={{0,2},{2,0},{1,3},{3,1},{4,6},{6,4},{5,7},{7,5},{8,10},{10,8},{9,1... | collective-permute-start | bytes 2359304 | tf_op jit(solution)/shard_map/ppermute | solution.py:57
  226.3 19.6 %collective-permute-start.21 = (bf16[256,1536]{1,0:T(8,128)(2,1)S(1)}, bf16[256,1536]{1,0:T(8,128)(2,1)}, u32[]{:S(2)}, u32[]{:S(2)}) collective-permute-start(bf16[256,1536]{1,0:T(8,128)(2,1)S(1)} %multiply_convert_fusion.refs_0_), channel_id=1, source_target_pairs={{0,4},{4,0},{1,5},{5,1},{2,6},{6,2},{3,7},{7,3},{8,12},{12,8},{9,1... | collective-permute-start | bytes 2359304 | tf_op jit(solution)/shard_map/ppermute | solution.py:57
  227.7 21.5 %collective-permute-start.25 = (bf16[256,1536]{1,0:T(8,128)(2,1)S(1)}, bf16[256,1536]{1,0:T(8,128)(2,1)S(1)}, u32[]{:S(2)}, u32[]{:S(2)}) collective-permute-start(bf16[256,1536]{1,0:T(8,128)(2,1)S(1)} %multiply_convert_fusion.refs_0_), channel_id=1, source_target_pairs={{0,1},{1,0},{2,3},{3,2},{4,5},{5,4},{6,7},{7,6},{8,9},{9,8},{10,11... | collective-permute-start | bytes 2359304 | tf_op jit(solution)/shard_map/ppermute | solution.py:57
  244.4 24.8 %collective-permute-start.23 = (bf16[256,768]{1,0:T(8,128)(2,1)}, bf16[256,768]{1,0:T(8,128)(2,1)}, u32[]{:S(2)}, u32[]{:S(2)}) collective-permute-start(bf16[256,768]{1,0:T(8,128)(2,1)} %slice.300), channel_id=1, source_target_pairs={{0,4},{4,0},{1,5},{5,1},{2,6},{6,2},{3,7},{7,3},{8,12},{12,8},{9,1... | collective-permute-start | bytes 1179656 | tf_op jit(solution)/shard_map/ppermute | solution.py:57
  247.7 21.5 %collective-permute-start.24 = (bf16[256,768]{1,0:T(8,128)(2,1)}, bf16[256,768]{1,0:T(8,128)(2,1)}, u32[]{:S(2)}, u32[]{:S(2)}) collective-permute-start(bf16[256,768]{1,0:T(8,128)(2,1)} %slice.301), channel_id=1, source_target_pairs={{0,2},{2,0},{1,3},{3,1},{4,6},{6,4},{5,7},{7,5},{8,10},{10,8},{9,1... | collective-permute-start | bytes 1179656 | tf_op jit(solution)/shard_map/ppermute | solution.py:57
  249.2 22.7 %collective-permute-start.27 = (bf16[256,1536]{1,0:T(8,128)(2,1)}, bf16[256,1536]{1,0:T(8,128)(2,1)}, u32[]{:S(2)}, u32[]{:S(2)}) collective-permute-start(bf16[256,1536]{1,0:T(8,128)(2,1)} %collective-permute-done.21.refs_0_), channel_id=1, source_target_pairs={{0,1},{1,0},{2,3},{3,2},{4,5},{5,4},{6,7},{7,6},{8,9},{9,8},{10,11... | collective-permute-start | bytes 2359304 | tf_op jit(solution)/shard_map/ppermute | solution.py:57
  312.1 229.4 %reduce-scatter.9.cloned.1.call-start = ((), (), s32[]{:S(2)}) async-start(), calls=%async_computation.8 | async-start | bytes 4423680 | tf_op jit(solution)/shard_map/reduce_scatter | solution.py:682
  336.2 19.9 %collective-permute-start.31 = (bf16[512,768]{1,0:T(8,128)(2,1)S(1)}, bf16[512,768]{1,0:T(8,128)(2,1)S(1)}, u32[]{:S(2)}, u32[]{:S(2)}) collective-permute-start(bf16[512,768]{1,0:T(8,128)(2,1)S(1)} %slice.307), channel_id=1, source_target_pairs={{0,4},{4,0},{1,5},{5,1},{2,6},{6,2},{3,7},{7,3},{8,12},{12,8},{9,1... | collective-permute-start | bytes 2359304 | tf_op jit(solution)/shard_map/ppermute | solution.py:57
  339.4 19.6 %collective-permute-start.32 = (bf16[512,768]{1,0:T(8,128)(2,1)S(1)}, bf16[512,768]{1,0:T(8,128)(2,1)S(1)}, u32[]{:S(2)}, u32[]{:S(2)}) collective-permute-start(bf16[512,768]{1,0:T(8,128)(2,1)S(1)} %pad_maximum_fusion.5), channel_id=1, source_target_pairs={{0,2},{2,0},{1,3},{3,1},{4,6},{6,4},{5,7},{7,5},{8,10},{10,8},{9,1... | collective-permute-start | bytes 2359304 | tf_op jit(solution)/shard_map/ppermute | solution.py:57
  373.0 20.1 %collective-permute-start.35 = (bf16[256,1536]{1,0:T(8,128)(2,1)S(1)}, bf16[256,1536]{1,0:T(8,128)(2,1)}, u32[]{:S(2)}, u32[]{:S(2)}) collective-permute-start(bf16[256,1536]{1,0:T(8,128)(2,1)S(1)} %add_convert_fusion.2.refs_0_), channel_id=1, source_target_pairs={{0,2},{2,0},{1,3},{3,1},{4,6},{6,4},{5,7},{7,5},{8,10},{10,8},{9,1... | collective-permute-start | bytes 2359304 | tf_op jit(solution)/shard_map/ppermute | solution.py:57
  393.6 147.9 %reduce-scatter.7.cloned.1.call-start = ((), (), s32[]{:S(2)}) async-start(), calls=%async_computation.7 | async-start | bytes 737280 | tf_op jit(solution)/shard_map/reduce_scatter | solution.py:682
  400.9 49.8 %collective-permute-start.40 = (bf16[512,1536]{1,0:T(8,128)(2,1)}, bf16[512,1536]{1,0:T(8,128)(2,1)}, u32[]{:S(2)}, u32[]{:S(2)}) collective-permute-start(bf16[512,1536]{1,0:T(8,128)(2,1)} %add_convert_fusion), channel_id=1, source_target_pairs={{0,4},{4,0},{1,5},{5,1},{2,6},{6,2},{3,7},{7,3},{8,12},{12,8},{9,1... | collective-permute-start | bytes 4718600 | tf_op jit(solution)/shard_map/ppermute | solution.py:57
  407.2 43.5 %collective-permute-start.41 = (bf16[2,2,192,384]{3,2,1,0:T(8,128)(2,1)}, bf16[2,2,192,384]{3,2,1,0:T(8,128)(2,1)}, u32[]{:S(2)}, u32[]{:S(2)}) collective-permute-start(bf16[2,2,192,384]{3,2,1,0:T(8,128)(2,1)} %get-tuple-element.190), channel_id=1, source_target_pairs={{0,4},{4,0},{1,5},{5,1},{2,6},{6,2},{3,7},{7,3},{8,12},{12,8},{9,1... | collective-permute-start | bytes 1769480 | tf_op jit(solution)/shard_map/ppermute | solution.py:57
  460.8 20.7 %collective-permute-start.43 = (bf16[256,1536]{1,0:T(8,128)(2,1)}, bf16[256,1536]{1,0:T(8,128)(2,1)}, u32[]{:S(2)}, u32[]{:S(2)}) collective-permute-start(bf16[256,1536]{1,0:T(8,128)(2,1)} %slice.407), channel_id=1, source_target_pairs={{0,2},{2,0},{1,3},{3,1},{4,6},{6,4},{5,7},{7,5},{8,10},{10,8},{9,1... | collective-permute-start | bytes 2359304 | tf_op jit(solution)/shard_map/ppermute | solution.py:57
  471.0 24.4 %collective-permute-start.45 = (bf16[1024,128]{1,0:T(8,128)(2,1)}, bf16[1024,128]{1,0:T(8,128)(2,1)}, u32[]{:S(2)}, u32[]{:S(2)}) collective-permute-start(bf16[1024,128]{1,0:T(8,128)(2,1)} %fusion.54), channel_id=1, source_target_pairs={{0,8},{8,0},{1,9},{9,1},{2,10},{10,2},{3,11},{11,3},{4,12},{12,4},... | collective-permute-start | bytes 786440 | tf_op jit(solution)/shard_map/ppermute | solution.py:57
  477.5 21.3 %collective-permute-start.46 = (bf16[192,2304]{1,0:T(8,128)(2,1)}, bf16[192,2304]{1,0:T(8,128)(2,1)}, u32[]{:S(2)}, u32[]{:S(2)}) collective-permute-start(bf16[192,2304]{1,0:T(8,128)(2,1)} %get-tuple-element.184), channel_id=1, source_target_pairs={{0,4},{4,0},{1,5},{5,1},{2,6},{6,2},{3,7},{7,3},{8,12},{12,8},{9,1... | collective-permute-start | bytes 2654216 | tf_op jit(solution)/shard_map/ppermute | solution.py:57
  481.3 86.1 %reduce-scatter.11.cloned.1.call-start = ((), (), s32[]{:S(2)}) async-start(), calls=%async_computation.9 | async-start | bytes 1064960 | tf_op jit(solution)/shard_map/reduce_scatter | solution.py:682
  504.0 74.6 %collective-permute-start.50 = (bf16[256,1536]{1,0:T(8,128)(2,1)}, bf16[256,1536]{1,0:T(8,128)(2,1)}, u32[]{:S(2)}, u32[]{:S(2)}) collective-permute-start(bf16[256,1536]{1,0:T(8,128)(2,1)} %fusion.25.refs_0_), channel_id=1, source_target_pairs={{0,1},{1,0},{2,3},{3,2},{4,5},{5,4},{6,7},{7,6},{8,9},{9,8},{10,11... | collective-permute-start | bytes 2359304 | tf_op jit(solution)/shard_map/ppermute | solution.py:57
  509.5 32.0 %collective-permute-start.53 = (bf16[2,2,208,512]{3,2,1,0:T(8,128)(2,1)}, bf16[2,2,208,512]{3,2,1,0:T(8,128)(2,1)}, u32[]{:S(2)}, u32[]{:S(2)}) collective-permute-start(bf16[2,2,208,512]{3,2,1,0:T(8,128)(2,1)} %get-tuple-element.188), channel_id=1, source_target_pairs={{0,4},{4,0},{1,5},{5,1},{2,6},{6,2},{3,7},{7,3},{8,12},{12,8},{9,1... | collective-permute-start | bytes 2555912 | tf_op jit(solution)/shard_map/ppermute | solution.py:57
  515.2 36.3 %collective-permute-start.48 = (bf16[512,1536]{1,0:T(8,128)(2,1)}, bf16[512,1536]{1,0:T(8,128)(2,1)}, u32[]{:S(2)}, u32[]{:S(2)}) collective-permute-start(bf16[512,1536]{1,0:T(8,128)(2,1)} %get-tuple-element.222), channel_id=1, source_target_pairs={{0,2},{2,0},{1,3},{3,1},{4,6},{6,4},{5,7},{7,5},{8,10},{10,8},{9,1... | collective-permute-start | bytes 4718600 | tf_op jit(solution)/shard_map/ppermute | solution.py:57
  551.6 23.7 %collective-permute-start.49 = (bf16[256,1536]{1,0:T(8,128)(2,1)}, bf16[256,1536]{1,0:T(8,128)(2,1)}, u32[]{:S(2)}, u32[]{:S(2)}) collective-permute-start(bf16[256,1536]{1,0:T(8,128)(2,1)} %fusion.25.refs_0_), channel_id=1, source_target_pairs={{0,2},{2,0},{1,3},{3,1},{4,6},{6,4},{5,7},{7,5},{8,10},{10,8},{9,1... | collective-permute-start | bytes 2359304 | tf_op jit(solution)/shard_map/ppermute | solution.py:57
  558.7 24.4 %collective-permute-start.52 = (bf16[512,1536]{1,0:T(8,128)(2,1)}, bf16[512,1536]{1,0:T(8,128)(2,1)S(1)}, u32[]{:S(2)}, u32[]{:S(2)}) collective-permute-start(bf16[512,1536]{1,0:T(8,128)(2,1)} %fusion.18.refs_0_), channel_id=1, source_target_pairs={{0,1},{1,0},{2,3},{3,2},{4,5},{5,4},{6,7},{7,6},{8,9},{9,8},{10,11... | collective-permute-start | bytes 4718600 | tf_op jit(solution)/shard_map/ppermute | solution.py:57
  (120 other events, 967.7 us)
Sparse Core Ops, SparseCore 0:
  49.2 74.9 all-gather.2
  126.4 128.5 all-gather.4
  312.3 123.1 reduce-scatter.4
  437.6 72.4 reduce-scatter.8
  512.2 22.1 reduce-scatter.6
  544.2 23.1 reduce-scatter.10

commit v6 on v5

--- a/solution.py
+++ b/solution.py
@@ -28,6 +28,7 @@
 NARROW = ("y", "c")
 BLOCK_Q = 512
 BLOCK_K = 512
+FORWARD_K = 1024
 
 
 def low(a):
@@ -321,11 +322,11 @@
     )(tokens_in, grads_in, w_gateup, *olds)
 
 
-def over_blocks(first_begin, last_begin, base, run, carry):
-    first = first_begin // BLOCK_K
-    end = (base + BLOCK_Q - 1) // BLOCK_K + 1
-    clear = jnp.minimum((last_begin + BLOCK_K - 1) // BLOCK_K, end)
-    clear_end = jnp.maximum((base + 1) // BLOCK_K, clear)
+def over_blocks(first_begin, last_begin, base, run, width, carry):
+    first = first_begin // width
+    end = (base + BLOCK_Q - 1) // width + 1
+    clear = jnp.minimum((last_begin + width - 1) // width, end)
+    clear_end = jnp.maximum((base + 1) // width, clear)
     before = clear - first
 
     def edge(t, carry):
@@ -355,12 +356,12 @@
 
         def run(j, carry, masked):
             top, total, acc = carry
-            at = pl.multiple_of(j * BLOCK_K, BLOCK_K)
-            k = k_ref[pl.ds(at, BLOCK_K), :]
-            v = v_ref[pl.ds(at, BLOCK_K), :]
+            at = pl.multiple_of(j * FORWARD_K, FORWARD_K)
+            k = k_ref[pl.ds(at, FORWARD_K), :]
+            v = v_ref[pl.ds(at, FORWARD_K), :]
             s = matmul_nt(q, k)
             if masked:
-                col = at + lax.broadcasted_iota(jnp.int32, (1, BLOCK_K), 1)
+                col = at + lax.broadcasted_iota(jnp.int32, (1, FORWARD_K), 1)
                 s = jnp.where((col <= row) & (col >= begin), s, masked_score)
             new_top = jnp.maximum(top, jnp.max(s, axis=1, keepdims=True))
             p = jnp.exp(s - new_top)
@@ -374,6 +375,7 @@
             starts_ref[2 * step + 1],
             base,
             run,
+            FORWARD_K,
             (
                 jnp.full((rows, 1), masked_score, jnp.float32),
                 jnp.zeros((rows, 1), jnp.float32),
@@ -463,6 +465,7 @@
             starts_ref[2 * step + 1],
             base,
             run,
+            BLOCK_K,
             jnp.zeros((rows, HD), jnp.float32),
         )
         for h in range(heads):

time: 605 us -> 608 us (level)
  matrix products: 101 us -> 112 us
    dot_general x2, matrix products: 15.7 us -> 26.2 us  [matmul(): return jnp.dot(left, right, preferred_element_type=jnp.float32)]
  transfers between devices with their start and end apart: 64 -> 64, of which waited for: 30 -> 28; matrix products, arithmetic and copies ran while one was open for 35% -> 36% of each run, Pallas kernels for 12% -> 12%
where the time goes in v6:
time: 608 us; the launch traced here: 599 us
  waiting for transfers between devices  184 us (30%)
  matrix products  112 us (18%)
  other arithmetic  93.6 us (15%)
  Pallas kernels  92.4 us (15%)
  starting transfers between devices  51.2 us (8%)
  local copies, waits for them, and re-layouts  50 us (8%)
  between operations  16.1 us (3%)
    ppermute x58, waiting for transfers between devices, swap(): return lax.ppermute(block, axis, [(i, i ^ distance) for i in range(size)])  181 us
    ppermute x58, starting transfers between devices, swap(): return lax.ppermute(block, axis, [(i, i ^ distance) for i in range(size)])  50.5 us
    dot_general x10, matrix products, matmul_nt(): lax.dot_general(left, right, (((1,), (1,)), ((), ())), preferred_element_...  44.4 us
    dot_general x5, matrix products, matmul_tn(): lax.dot_general(left, right, (((0,), (0,)), ((), ())), preferred_element_...  41 us
    pallas_call x2, Pallas kernels, feed_forward(): pl.pallas_call(kernel, grid=(count // block,), in_specs=[by_tokens(D), by...  27.9 us
    dot_general x2, matrix products, matmul(): return jnp.dot(left, right, preferred_element_type=jnp.float32)  26.2 us
    convert_element_type x18, other arithmetic, low(): return a.astype(jnp.bfloat16)  25.3 us
    pallas_call x6, Pallas kernels, stack_rows(): pl.pallas_call(kernel, in_specs=[pl.BlockSpec(memory_space=pltpu.SMEM)] +...  23.6 us
  transfers between devices with their start and end apart: 64, of which 28 were waited for; matrix products, arithmetic and copies ran while one was open for 36% of the time, Pallas kernels for 12%

profile of v6, /device:TPU:0, one launch (start us, length us, event | category | flops | bytes accessed | tf_op | source)
XLA Modules:
  0.0 598.8 jit_solution(5157416755699677643)
XLA Ops:
  24.8 13.0 %collective-permute-done.5 = bf16[208,896]{1,0:T(8,128)(2,1)} collective-permute-done((bf16[208,896]{1,0:T(8,128)(2,1)S(1)}, bf16[208,896]{1,0:T(8,128)(2,1)}, u32[]{:S(2)}, u32[]{:S(2)}) %collective-permute-start.5) | collective-permute-done | bytes 372768 | tf_op jit(solution)/shard_map/ppermute | solution.py:58
  43.2 5.0 collective-permute-done.6
  57.7 8.0 %collective-permute-done.4.refs_1_ = bf16[2,208,512]{2,1,0:T(8,128)(2,1)S(1)} collective-permute-done((bf16[2,208,512]{2,1,0:T(8,128)(2,1)S(1)}, bf16[2,208,512]{2,1,0:T(8,128)(2,1)S(1)}, u32[]{:S(2)}, u32[]{:S(2)}) %collective-permute-start.4) | collective-permute-done | bytes 426016 | tf_op jit(solution)/shard_map/ppermute | solution.py:58
  66.4 6.2 %collective-permute-done.7.refs_3_ = bf16[2,208,512]{2,1,0:T(8,128)(2,1)} collective-permute-done((bf16[2,208,512]{2,1,0:T(8,128)(2,1)S(1)}, bf16[2,208,512]{2,1,0:T(8,128)(2,1)}, u32[]{:S(2)}, u32[]{:S(2)}) %collective-permute-start.7) | collective-permute-done | bytes 426016 | tf_op jit(solution)/shard_map/ppermute | solution.py:58
  81.6 7.1 %project.1 = (bf16[1024,1536]{1,0:T(8,128)(2,1)}, bf16[1024,384]{1,0:T(8,128)(2,1)}, bf16[1024,128]{1,0:T(8,128)(2,1)}) custom-call(bf16[1024,1536]{1,0:T(8,128)(2,1)} %x_ref.1, bf16[1536,512]{1,0:T(8,128)(2,1)} %get-tuple-element.88.w_ref, f32[1,512]{1,0:T(1,128)} %bitcast.283, f32[1024,128]{1,0:T(8,128)} %get-tuple-element.224.c_ref, ...), custom_call_target="tpu_custom_call" | custom-call | tf_op jit(solution)/shard_map/project/pallas_call | solution.py:271
  97.6 23.3 %collective-permute-done.8 = bf16[1024,128]{1,0:T(8,128)(2,1)S(1)} collective-permute-done((bf16[1024,128]{1,0:T(8,128)(2,1)S(1)}, bf16[1024,128]{1,0:T(8,128)(2,1)S(1)}, u32[]{:S(2)}, u32[]{:S(2)}) %collective-permute-start.8) | collective-permute-done | bytes 262176 | tf_op jit(solution)/shard_map/ppermute | solution.py:58
  126.0 6.8 %collective-permute-done.10 = bf16[2,1024,128]{2,1,0:T(8,128)(2,1)S(1)} collective-permute-done((bf16[2,1024,128]{2,1,0:T(8,128)(2,1)S(1)}, bf16[2,1024,128]{2,1,0:T(8,128)(2,1)S(1)}, u32[]{:S(2)}, u32[]{:S(2)}) %collective-permute-start.10) | collective-permute-done | bytes 524320 | tf_op jit(solution)/shard_map/ppermute | solution.py:58
  144.9 12.8 %attention_forward.1 = (f32[1024,384]{1,0:T(8,128)}, f32[3,1024,1]{2,1,0:T(8,128)}) custom-call(s32[4]{0:T(128)} %reshape.479.starts_ref, s32[1]{0:T(128)} %bitcast.7.place_ref, bf16[1024,384]{1,0:T(8,128)(2,1)} %get-tuple-element.90.q_ref, bf16[4096,128]{1,0:T(8,128)(2,1)} %get-tuple-element.179.k_ref, bf16[4096,128]{1,0:T(8,128)(2,1)} %get-tuple-element.178.v_ref, ...), custom_call_target="tpu_custom_call" | custom-call | tf_op jit(solution)/shard_map/attention_forward/pallas_call | solution.py:392
  165.3 6.9 %collective-permute-done.16.refs_4_ = bf16[256,1536]{1,0:T(8,128)(2,1)} collective-permute-done((bf16[256,1536]{1,0:T(8,128)(2,1)S(1)}, bf16[256,1536]{1,0:T(8,128)(2,1)}, u32[]{:S(2)}, u32[]{:S(2)}) %collective-permute-start.16) | collective-permute-done | bytes 786464 | tf_op jit(solution)/shard_map/ppermute | solution.py:58
  172.3 16.5 %collective-permute-done.17.refs_5_ = bf16[256,1536]{1,0:T(8,128)(2,1)} collective-permute-done((bf16[256,1536]{1,0:T(8,128)(2,1)S(1)}, bf16[256,1536]{1,0:T(8,128)(2,1)}, u32[]{:S(2)}, u32[]{:S(2)}) %collective-permute-start.17) | collective-permute-done | bytes 786464 | tf_op jit(solution)/shard_map/ppermute | solution.py:58
  193.3 5.7 stack_rows.6
  204.8 23.5 %convolution_convert_fusion.2.g_ref = bf16[2048,1152]{1,0:T(8,128)(2,1)} fusion(bf16[2048,1536]{1,0:T(8,128)(2,1)} %stack_rows.6, bf16[1536,1152]{1,0:T(8,128)(2,1)} %all-gather.3.cloned.1.call-done), kind=kOutput, calls=%fused_computation.2 | convolution fusion | flops 7250116608 | bytes 14548992 | tf_op jit(solution)/shard_map/dot_general | solution.py:43
  232.1 17.3 %collective-permute-done.22.refs_1_ = bf16[256,1536]{1,0:T(8,128)(2,1)S(1)} collective-permute-done((bf16[256,1536]{1,0:T(8,128)(2,1)S(1)}, bf16[256,1536]{1,0:T(8,128)(2,1)S(1)}, u32[]{:S(2)}, u32[]{:S(2)}) %collective-permute-start.22) | collective-permute-done | bytes 786464 | tf_op jit(solution)/shard_map/ppermute | solution.py:58
  260.1 13.9 %feed_forward.2 = (bf16[2048,1152]{1,0:T(8,128)(2,1)}, bf16[2048,2304]{1,0:T(8,128)(2,1)}) custom-call(bf16[2048,1536]{1,0:T(8,128)(2,1)} %stack_rows.7.b_ref.refs_4_, bf16[2048,1152]{1,0:T(8,128)(2,1)} %convolution_convert_fusion.2.g_ref, bf16[1536,2304]{1,0:T(8,128)(2,1)} %all-gather.5.cloned.1.call-done.wgu_ref), custom_call_target="tpu_custom_call" | custom-call | tf_op jit(solution)/shard_map/feed_forward/pallas_call | solution.py:306
  282.3 13.9 %feed_forward.3 = (bf16[2048,1152]{1,0:T(8,128)(2,1)}, bf16[2048,2304]{1,0:T(8,128)(2,1)}) custom-call(bf16[2048,1536]{1,0:T(8,128)(2,1)} %stack_rows.8.b_ref, bf16[2048,1152]{1,0:T(8,128)(2,1)} %convolution_convert_fusion.2.g_ref, bf16[1536,2304]{1,0:T(8,128)(2,1)} %all-gather.5.cloned.1.call-done.wgu_ref, ...), custom_call_target="tpu_custom_call", output_to_operand_aliasing={{0}: (3, {}), {1}: (4, {})} | custom-call | tf_op jit(solution)/shard_map/feed_forward/pallas_call | solution.py:306
  296.3 20.7 %convolution_convert_fusion = bf16[1536,2304]{1,0:T(8,128)(2,1)} fusion(bf16[2048,1536]{1,0:T(8,128)(2,1)} %stack_rows.8.b_ref, bf16[2048,2304]{1,0:T(8,128)(2,1)} %get-tuple-element.118), kind=kOutput, calls=%fused_computation | convolution fusion | flops 14499053568 | bytes 22806528 | tf_op jit(solution)/shard_map/dot_general | solution.py:51
  317.0 11.4 %fusion.4 = bf16[1024,1536]{1,0:T(8,128)(2,1)S(1)} fusion(bf16[1536,2304]{1,0:T(8,128)(2,1)} %all-gather.5.cloned.1.call-done.wgu_ref, bf16[2048,2304]{1,0:T(8,128)(2,1)} %get-tuple-element.118), kind=kOutput, calls=%fused_computation.9 | convolution fusion | flops 7249330176 | bytes 14942208 | tf_op jit(solution)/shard_map/dot_general | solution.py:47
  329.0 11.1 %fusion.7 = bf16[1024,1536]{1,0:T(8,128)(2,1)S(1)} fusion(bf16[1536,2304]{1,0:T(8,128)(2,1)} %all-gather.5.cloned.1.call-done.wgu_ref, bf16[2048,2304]{1,0:T(8,128)(2,1)} %get-tuple-element.118), kind=kOutput, calls=%fused_computation.10 | convolution fusion | flops 7249330176 | bytes 14942208 | tf_op jit(solution)/shard_map/dot_general | solution.py:47
  345.7 4.5 convolution_convert_fusion.4
  350.2 4.5 convolution_convert_fusion.3
  354.7 6.2 %collective-permute-done.31 = bf16[512,768]{1,0:T(8,128)(2,1)S(1)} collective-permute-done((bf16[512,768]{1,0:T(8,128)(2,1)S(1)}, bf16[512,768]{1,0:T(8,128)(2,1)S(1)}, u32[]{:S(2)}, u32[]{:S(2)}) %collective-permute-start.31) | collective-permute-done | bytes 786464 | tf_op jit(solution)/shard_map/ppermute | solution.py:58
  366.4 8.3 %collective-permute-done.33 = bf16[256,768]{1,0:T(8,128)(2,1)S(1)} collective-permute-done((bf16[256,768]{1,0:T(8,128)(2,1)S(1)}, bf16[256,768]{1,0:T(8,128)(2,1)S(1)}, u32[]{:S(2)}, u32[]{:S(2)}) %collective-permute-start.33) | collective-permute-done | bytes 393248 | tf_op jit(solution)/shard_map/ppermute | solution.py:58
  382.4 10.5 %convolution_convert_fusion.1 = bf16[1536,1152]{1,0:T(8,128)(2,1)} fusion(bf16[2048,1536]{1,0:T(8,128)(2,1)S(1)} %bitcast.236, bf16[2048,1152]{1,0:T(8,128)(2,1)S(1)} %bitcast.238), kind=kOutput, calls=%fused_computation.1 | convolution fusion | flops 7249526784 | bytes 14548992 | tf_op jit(solution)/shard_map/dot_general | solution.py:51
  392.9 4.0 convert_add_fusion.2
  415.2 15.6 %attention_backward.1 = (bf16[1024,384]{1,0:T(8,128)(2,1)}, f32[4096,128]{1,0:T(8,128)}, f32[4096,128]{1,0:T(8,128)}) custom-call(s32[4]{0:T(128)} %reshape.479.starts_ref, s32[1]{0:T(128)} %bitcast.7.place_ref, bf16[1024,384]{1,0:T(8,128)(2,1)} %get-tuple-element.90.q_ref, bf16[4096,128]{1,0:T(8,128)(2,1)} %get-tuple-element.179.k_ref, ...), custom_call_target="tpu_custom_call" | custom-call | flops 8053063680 | tf_op jit(solution)/shard_map/attention_backward/pallas_call | solution.py:479
  433.8 21.5 %collective-permute-done.41 = bf16[2,2,192,384]{3,2,1,0:T(8,128)(2,1)} collective-permute-done((bf16[2,2,192,384]{3,2,1,0:T(8,128)(2,1)}, bf16[2,2,192,384]{3,2,1,0:T(8,128)(2,1)}, u32[]{:S(2)}, u32[]{:S(2)}) %collective-permute-start.41) | collective-permute-done | bytes 589856 | tf_op jit(solution)/shard_map/ppermute | solution.py:58
  468.1 6.7 %collective-permute-done.44 = bf16[2,1024,128]{2,1,0:T(8,128)(2,1)S(1)} collective-permute-done((bf16[2,1024,128]{2,1,0:T(8,128)(2,1)S(1)}, bf16[2,1024,128]{2,1,0:T(8,128)(2,1)S(1)}, u32[]{:S(2)}, u32[]{:S(2)}) %collective-permute-start.44) | collective-permute-done | bytes 524320 | tf_op jit(solution)/shard_map/ppermute | solution.py:58
  475.6 5.1 collective-permute-start.45
  486.2 14.5 %collective-permute-done.45 = bf16[1024,128]{1,0:T(8,128)(2,1)} collective-permute-done((bf16[1024,128]{1,0:T(8,128)(2,1)}, bf16[1024,128]{1,0:T(8,128)(2,1)}, u32[]{:S(2)}, u32[]{:S(2)}) %collective-permute-start.45) | collective-permute-done | bytes 262176 | tf_op jit(solution)/shard_map/ppermute | solution.py:58
  526.3 7.4 %multiply_reduce_fusion = (f32[192]{0:T(256)S(1)}, f32[192,2,2240]{2,1,0:T(2,128)S(1)}) fusion(bf16[192,1,2240]{2,1,0:T(2,128)(2,1)S(1)} %copy.81, bf16[192,1,2240]{2,1,0:T(2,128)(2,1)S(1)} %copy.80, f32[192,2,2240]{2,1,0:T(2,128)S(1)} %copy-done.1), kind=kLoop, calls=%fused_computation.15 | loop fusion | flops 6881088 | bytes 8602368 | tf_op jit(solution)/shard_map/reduce_sum | solution.py:798
  535.5 11.2 %multiply_add_fusion = f32[192,2,2240]{2,1,0:T(2,128)} fusion(f32[192,2,2240]{2,1,0:T(2,128)S(1)} %copy-done.1, f32[192,2,2240]{2,1,0:T(2,128)S(1)} %get-tuple-element.167, f32[192,2,2240]{2,1,0:T(2,128)S(1)} %copy-done.20, f32[192,2,2240]{2,1,0:T(2,128)S(1)} %copy-done.21), kind=kLoop, calls=%fused_computation.16 | loop fusion | flops 12042240 | bytes 17203200 | tf_op jit(solution)/shard_map/add | solution.py:240
  560.1 3.9 fusion.18.refs_0_
  (500 shorter events, 235.5 us)
Async XLA Ops:
  7.2 197.6 %all-gather.3.cloned.1.call-start = ((), (), s32[]{:S(2)}) async-start(), calls=%async_computation.4 | async-start | bytes 4423680 | tf_op jit(solution)/shard_map/all_gather | solution.py:591
  17.6 20.2 %collective-permute-start.5 = (bf16[208,896]{1,0:T(8,128)(2,1)S(1)}, bf16[208,896]{1,0:T(8,128)(2,1)}, u32[]{:S(2)}, u32[]{:S(2)}) collective-permute-start(bf16[208,896]{1,0:T(8,128)(2,1)S(1)} %pad_maximum_fusion.8), channel_id=1, source_target_pairs={{0,16},{16,0},{1,17},{17,1},{2,18},{18,2},{3,19},{19,3},{4,20},{20... | collective-permute-start | bytes 1118216 | tf_op jit(solution)/shard_map/ppermute | solution.py:58
  49.1 211.0 %all-gather.5.cloned.1.call-start = ((), (), s32[]{:S(2)}) async-start(), calls=%async_computation.5 | async-start | bytes 8847360 | tf_op jit(solution)/shard_map/all_gather | solution.py:603
  95.4 360.0 %reduce-scatter.5.cloned.1.call-start = ((), (), s32[]{:S(2)}) async-start(), calls=%async_computation.6 | async-start | bytes 8847360 | tf_op jit(solution)/shard_map/reduce_scatter | solution.py:685
  95.7 25.2 %collective-permute-start.8 = (bf16[1024,128]{1,0:T(8,128)(2,1)S(1)}, bf16[1024,128]{1,0:T(8,128)(2,1)S(1)}, u32[]{:S(2)}, u32[]{:S(2)}) collective-permute-start(bf16[1024,128]{1,0:T(8,128)(2,1)S(1)} %copy-done.67), channel_id=1, source_target_pairs={{0,8},{8,0},{1,9},{9,1},{2,10},{10,2},{3,11},{11,3},{4,12},{12,4},... | collective-permute-start | bytes 786440 | tf_op jit(solution)/shard_map/ppermute | solution.py:58
  138.1 21.1 %collective-permute-start.12 = (bf16[2,208,384]{2,1,0:T(8,128)(2,1)S(1)}, bf16[2,208,384]{2,1,0:T(8,128)(2,1)}, u32[]{:S(2)}, u32[]{:S(2)}) collective-permute-start(bf16[2,208,384]{2,1,0:T(8,128)(2,1)S(1)} %maximum_select_fusion.6.refs_0_), channel_id=1, source_target_pairs={{0,4},{4,0},{1,5},{5,1},{2,6},{6,2},{3,7},{7,3},{8,12},{12,8},{9,1... | collective-permute-start | bytes 958472 | tf_op jit(solution)/shard_map/ppermute | solution.py:58
  139.6 19.6 %collective-permute-start.13 = (bf16[2,208,384]{2,1,0:T(8,128)(2,1)S(1)}, bf16[2,208,384]{2,1,0:T(8,128)(2,1)}, u32[]{:S(2)}, u32[]{:S(2)}) collective-permute-start(bf16[2,208,384]{2,1,0:T(8,128)(2,1)S(1)} %maximum_select_fusion.7.refs_2_), channel_id=1, source_target_pairs={{0,4},{4,0},{1,5},{5,1},{2,6},{6,2},{3,7},{7,3},{8,12},{12,8},{9,1... | collective-permute-start | bytes 958472 | tf_op jit(solution)/shard_map/ppermute | solution.py:58
  140.1 32.1 %collective-permute-start.16 = (bf16[256,1536]{1,0:T(8,128)(2,1)S(1)}, bf16[256,1536]{1,0:T(8,128)(2,1)}, u32[]{:S(2)}, u32[]{:S(2)}) collective-permute-start(bf16[256,1536]{1,0:T(8,128)(2,1)S(1)} %get-tuple-element.105.refs_0_), channel_id=1, source_target_pairs={{0,4},{4,0},{1,5},{5,1},{2,6},{6,2},{3,7},{7,3},{8,12},{12,8},{9,1... | collective-permute-start | bytes 2359304 | tf_op jit(solution)/shard_map/ppermute | solution.py:58
  141.6 47.1 %collective-permute-start.17 = (bf16[256,1536]{1,0:T(8,128)(2,1)S(1)}, bf16[256,1536]{1,0:T(8,128)(2,1)}, u32[]{:S(2)}, u32[]{:S(2)}) collective-permute-start(bf16[256,1536]{1,0:T(8,128)(2,1)S(1)} %get-tuple-element.106.refs_1_), channel_id=1, source_target_pairs={{0,4},{4,0},{1,5},{5,1},{2,6},{6,2},{3,7},{7,3},{8,12},{12,8},{9,1... | collective-permute-start | bytes 2359304 | tf_op jit(solution)/shard_map/ppermute | solution.py:58
  165.3 33.6 %collective-permute-start.14 = (bf16[512,1536]{1,0:T(8,128)(2,1)}, bf16[512,1536]{1,0:T(8,128)(2,1)}, u32[]{:S(2)}, u32[]{:S(2)}) collective-permute-start(bf16[512,1536]{1,0:T(8,128)(2,1)} %convolution_convert_fusion.5), channel_id=1, source_target_pairs={{0,1},{1,0},{2,3},{3,2},{4,5},{5,4},{6,7},{7,6},{8,9},{9,8},{10,11... | collective-permute-start | bytes 4718600 | tf_op jit(solution)/shard_map/ppermute | solution.py:58
  203.2 25.1 %collective-permute-start.15 = (bf16[256,1536]{1,0:T(8,128)(2,1)S(1)}, bf16[256,1536]{1,0:T(8,128)(2,1)S(1)}, u32[]{:S(2)}, u32[]{:S(2)}) collective-permute-start(bf16[256,1536]{1,0:T(8,128)(2,1)S(1)} %fusion.31), channel_id=1, source_target_pairs={{0,2},{2,0},{1,3},{3,1},{4,6},{6,4},{5,7},{7,5},{8,10},{10,8},{9,1... | collective-permute-start | bytes 2359304 | tf_op jit(solution)/shard_map/ppermute | solution.py:58
  230.7 21.1 %collective-permute-start.21 = (bf16[256,1536]{1,0:T(8,128)(2,1)S(1)}, bf16[256,1536]{1,0:T(8,128)(2,1)}, u32[]{:S(2)}, u32[]{:S(2)}) collective-permute-start(bf16[256,1536]{1,0:T(8,128)(2,1)S(1)} %multiply_convert_fusion.refs_0_), channel_id=1, source_target_pairs={{0,4},{4,0},{1,5},{5,1},{2,6},{6,2},{3,7},{7,3},{8,12},{12,8},{9,1... | collective-permute-start | bytes 2359304 | tf_op jit(solution)/shard_map/ppermute | solution.py:58
  232.1 22.1 %collective-permute-start.25 = (bf16[256,1536]{1,0:T(8,128)(2,1)S(1)}, bf16[256,1536]{1,0:T(8,128)(2,1)S(1)}, u32[]{:S(2)}, u32[]{:S(2)}) collective-permute-start(bf16[256,1536]{1,0:T(8,128)(2,1)S(1)} %multiply_convert_fusion.refs_0_), channel_id=1, source_target_pairs={{0,1},{1,0},{2,3},{3,2},{4,5},{5,4},{6,7},{7,6},{8,9},{9,8},{10,11... | collective-permute-start | bytes 2359304 | tf_op jit(solution)/shard_map/ppermute | solution.py:58
  250.3 23.7 %collective-permute-start.23 = (bf16[256,768]{1,0:T(8,128)(2,1)}, bf16[256,768]{1,0:T(8,128)(2,1)}, u32[]{:S(2)}, u32[]{:S(2)}) collective-permute-start(bf16[256,768]{1,0:T(8,128)(2,1)} %slice.300), channel_id=1, source_target_pairs={{0,4},{4,0},{1,5},{5,1},{2,6},{6,2},{3,7},{7,3},{8,12},{12,8},{9,1... | collective-permute-start | bytes 1179656 | tf_op jit(solution)/shard_map/ppermute | solution.py:58
  253.5 20.5 %collective-permute-start.24 = (bf16[256,768]{1,0:T(8,128)(2,1)}, bf16[256,768]{1,0:T(8,128)(2,1)}, u32[]{:S(2)}, u32[]{:S(2)}) collective-permute-start(bf16[256,768]{1,0:T(8,128)(2,1)} %slice.301), channel_id=1, source_target_pairs={{0,2},{2,0},{1,3},{3,1},{4,6},{6,4},{5,7},{7,5},{8,10},{10,8},{9,1... | collective-permute-start | bytes 1179656 | tf_op jit(solution)/shard_map/ppermute | solution.py:58
  254.2 22.5 %collective-permute-start.27 = (bf16[256,1536]{1,0:T(8,128)(2,1)}, bf16[256,1536]{1,0:T(8,128)(2,1)}, u32[]{:S(2)}, u32[]{:S(2)}) collective-permute-start(bf16[256,1536]{1,0:T(8,128)(2,1)} %collective-permute-done.21.refs_0_), channel_id=1, source_target_pairs={{0,1},{1,0},{2,3},{3,2},{4,5},{5,4},{6,7},{7,6},{8,9},{9,8},{10,11... | collective-permute-start | bytes 2359304 | tf_op jit(solution)/shard_map/ppermute | solution.py:58
  317.0 229.8 %reduce-scatter.9.cloned.1.call-start = ((), (), s32[]{:S(2)}) async-start(), calls=%async_computation.8 | async-start | bytes 4423680 | tf_op jit(solution)/shard_map/reduce_scatter | solution.py:685
  341.1 19.9 %collective-permute-start.31 = (bf16[512,768]{1,0:T(8,128)(2,1)S(1)}, bf16[512,768]{1,0:T(8,128)(2,1)S(1)}, u32[]{:S(2)}, u32[]{:S(2)}) collective-permute-start(bf16[512,768]{1,0:T(8,128)(2,1)S(1)} %slice.307), channel_id=1, source_target_pairs={{0,4},{4,0},{1,5},{5,1},{2,6},{6,2},{3,7},{7,3},{8,12},{12,8},{9,1... | collective-permute-start | bytes 2359304 | tf_op jit(solution)/shard_map/ppermute | solution.py:58
  344.3 19.6 %collective-permute-start.32 = (bf16[512,768]{1,0:T(8,128)(2,1)S(1)}, bf16[512,768]{1,0:T(8,128)(2,1)S(1)}, u32[]{:S(2)}, u32[]{:S(2)}) collective-permute-start(bf16[512,768]{1,0:T(8,128)(2,1)S(1)} %pad_maximum_fusion.5), channel_id=1, source_target_pairs={{0,2},{2,0},{1,3},{3,1},{4,6},{6,4},{5,7},{7,5},{8,10},{10,8},{9,1... | collective-permute-start | bytes 2359304 | tf_op jit(solution)/shard_map/ppermute | solution.py:58
  377.8 20.1 %collective-permute-start.35 = (bf16[256,1536]{1,0:T(8,128)(2,1)S(1)}, bf16[256,1536]{1,0:T(8,128)(2,1)}, u32[]{:S(2)}, u32[]{:S(2)}) collective-permute-start(bf16[256,1536]{1,0:T(8,128)(2,1)S(1)} %add_convert_fusion.2.refs_0_), channel_id=1, source_target_pairs={{0,2},{2,0},{1,3},{3,1},{4,6},{6,4},{5,7},{7,5},{8,10},{10,8},{9,1... | collective-permute-start | bytes 2359304 | tf_op jit(solution)/shard_map/ppermute | solution.py:58
  398.4 148.3 %reduce-scatter.7.cloned.1.call-start = ((), (), s32[]{:S(2)}) async-start(), calls=%async_computation.7 | async-start | bytes 737280 | tf_op jit(solution)/shard_map/reduce_scatter | solution.py:685
  405.6 49.8 %collective-permute-start.40 = (bf16[512,1536]{1,0:T(8,128)(2,1)}, bf16[512,1536]{1,0:T(8,128)(2,1)}, u32[]{:S(2)}, u32[]{:S(2)}) collective-permute-start(bf16[512,1536]{1,0:T(8,128)(2,1)} %add_convert_fusion), channel_id=1, source_target_pairs={{0,4},{4,0},{1,5},{5,1},{2,6},{6,2},{3,7},{7,3},{8,12},{12,8},{9,1... | collective-permute-start | bytes 4718600 | tf_op jit(solution)/shard_map/ppermute | solution.py:58
  411.1 44.3 %collective-permute-start.41 = (bf16[2,2,192,384]{3,2,1,0:T(8,128)(2,1)}, bf16[2,2,192,384]{3,2,1,0:T(8,128)(2,1)}, u32[]{:S(2)}, u32[]{:S(2)}) collective-permute-start(bf16[2,2,192,384]{3,2,1,0:T(8,128)(2,1)} %get-tuple-element.190), channel_id=1, source_target_pairs={{0,4},{4,0},{1,5},{5,1},{2,6},{6,2},{3,7},{7,3},{8,12},{12,8},{9,1... | collective-permute-start | bytes 1769480 | tf_op jit(solution)/shard_map/ppermute | solution.py:58
  464.7 21.5 %collective-permute-start.43 = (bf16[256,1536]{1,0:T(8,128)(2,1)}, bf16[256,1536]{1,0:T(8,128)(2,1)}, u32[]{:S(2)}, u32[]{:S(2)}) collective-permute-start(bf16[256,1536]{1,0:T(8,128)(2,1)} %slice.407), channel_id=1, source_target_pairs={{0,2},{2,0},{1,3},{3,1},{4,6},{6,4},{5,7},{7,5},{8,10},{10,8},{9,1... | collective-permute-start | bytes 2359304 | tf_op jit(solution)/shard_map/ppermute | solution.py:58
  475.6 25.0 %collective-permute-start.45 = (bf16[1024,128]{1,0:T(8,128)(2,1)}, bf16[1024,128]{1,0:T(8,128)(2,1)}, u32[]{:S(2)}, u32[]{:S(2)}) collective-permute-start(bf16[1024,128]{1,0:T(8,128)(2,1)} %fusion.54), channel_id=1, source_target_pairs={{0,8},{8,0},{1,9},{9,1},{2,10},{10,2},{3,11},{11,3},{4,12},{12,4},... | collective-permute-start | bytes 786440 | tf_op jit(solution)/shard_map/ppermute | solution.py:58
  482.1 21.3 %collective-permute-start.46 = (bf16[192,2304]{1,0:T(8,128)(2,1)}, bf16[192,2304]{1,0:T(8,128)(2,1)}, u32[]{:S(2)}, u32[]{:S(2)}) collective-permute-start(bf16[192,2304]{1,0:T(8,128)(2,1)} %get-tuple-element.184), channel_id=1, source_target_pairs={{0,4},{4,0},{1,5},{5,1},{2,6},{6,2},{3,7},{7,3},{8,12},{12,8},{9,1... | collective-permute-start | bytes 2654216 | tf_op jit(solution)/shard_map/ppermute | solution.py:58
  485.9 85.2 %reduce-scatter.11.cloned.1.call-start = ((), (), s32[]{:S(2)}) async-start(), calls=%async_computation.9 | async-start | bytes 1064960 | tf_op jit(solution)/shard_map/reduce_scatter | solution.py:685
  509.2 73.1 %collective-permute-start.50 = (bf16[256,1536]{1,0:T(8,128)(2,1)}, bf16[256,1536]{1,0:T(8,128)(2,1)}, u32[]{:S(2)}, u32[]{:S(2)}) collective-permute-start(bf16[256,1536]{1,0:T(8,128)(2,1)} %fusion.25.refs_0_), channel_id=1, source_target_pairs={{0,1},{1,0},{2,3},{3,2},{4,5},{5,4},{6,7},{7,6},{8,9},{9,8},{10,11... | collective-permute-start | bytes 2359304 | tf_op jit(solution)/shard_map/ppermute | solution.py:58
  514.7 32.0 %collective-permute-start.53 = (bf16[2,2,208,512]{3,2,1,0:T(8,128)(2,1)}, bf16[2,2,208,512]{3,2,1,0:T(8,128)(2,1)}, u32[]{:S(2)}, u32[]{:S(2)}) collective-permute-start(bf16[2,2,208,512]{3,2,1,0:T(8,128)(2,1)} %get-tuple-element.188), channel_id=1, source_target_pairs={{0,4},{4,0},{1,5},{5,1},{2,6},{6,2},{3,7},{7,3},{8,12},{12,8},{9,1... | collective-permute-start | bytes 2555912 | tf_op jit(solution)/shard_map/ppermute | solution.py:58
  520.7 36.3 %collective-permute-start.48 = (bf16[512,1536]{1,0:T(8,128)(2,1)}, bf16[512,1536]{1,0:T(8,128)(2,1)}, u32[]{:S(2)}, u32[]{:S(2)}) collective-permute-start(bf16[512,1536]{1,0:T(8,128)(2,1)} %get-tuple-element.222), channel_id=1, source_target_pairs={{0,2},{2,0},{1,3},{3,1},{4,6},{6,4},{5,7},{7,5},{8,10},{10,8},{9,1... | collective-permute-start | bytes 4718600 | tf_op jit(solution)/shard_map/ppermute | solution.py:58
  557.0 21.9 %collective-permute-start.49 = (bf16[256,1536]{1,0:T(8,128)(2,1)}, bf16[256,1536]{1,0:T(8,128)(2,1)}, u32[]{:S(2)}, u32[]{:S(2)}) collective-permute-start(bf16[256,1536]{1,0:T(8,128)(2,1)} %fusion.25.refs_0_), channel_id=1, source_target_pairs={{0,2},{2,0},{1,3},{3,1},{4,6},{6,4},{5,7},{7,5},{8,10},{10,8},{9,1... | collective-permute-start | bytes 2359304 | tf_op jit(solution)/shard_map/ppermute | solution.py:58
  564.0 22.7 %collective-permute-start.52 = (bf16[512,1536]{1,0:T(8,128)(2,1)}, bf16[512,1536]{1,0:T(8,128)(2,1)S(1)}, u32[]{:S(2)}, u32[]{:S(2)}) collective-permute-start(bf16[512,1536]{1,0:T(8,128)(2,1)} %fusion.18.refs_0_), channel_id=1, source_target_pairs={{0,1},{1,0},{2,3},{3,2},{4,5},{5,4},{6,7},{7,6},{8,9},{9,8},{10,11... | collective-permute-start | bytes 4718600 | tf_op jit(solution)/shard_map/ppermute | solution.py:58
  (120 other events, 953.1 us)
Sparse Core Ops, SparseCore 0:
  49.2 74.9 all-gather.2
  126.4 128.5 all-gather.4
  317.1 123.9 reduce-scatter.4
  443.3 72.3 reduce-scatter.8
  517.8 22.1 reduce-scatter.6
  549.4 21.6 reduce-scatter.10
